TPU v7x, 128 devices: a whole 4x4x4 slice. The times are simulated.
128 devices in a mesh: ctx: 16 (over y, x), head: 8 (over z, core).
Axes of the slice: x: 4, y: 4, z: 4, core: 2. Of those that a mesh axis runs over, the one named last changes fastest.
Arguments:
- branch_rows: bfloat16 [16384, 2048], P(('ctx', 'head')), may hold values from -6 to 6
- expert_ids: int32 [16384, 8], P(('ctx', 'head')), may hold values from 0 to 127, all different within a row; in each aligned block of 128 rows (0 to 127, 128 to 255, ...) at most 12 rows name the same one
- targets: int32 [16384], P(('ctx', 'head')), may hold values from 0 to 8191, as said below
- router: bfloat16 [2048, 128], replicated, may hold values from -0.046875 to 0.046875
- w_gate: bfloat16 [128, 2048, 768], P(('ctx', 'head')), may hold values from -0.125 to 0.125
- w_up: bfloat16 [128, 2048, 768], P(('ctx', 'head')), may hold values from -0.125 to 0.125
- w_down: bfloat16 [128, 768, 2048], P(('ctx', 'head')), may hold values from -0.3125 to 0.3125
- stream: bfloat16 [8192, 2048], P('ctx', 'head'), may hold values from -6 to 6
- attn_gain: float32 [2048], replicated, may hold values from 0.1 to 1.9
- q_gain: float32 [4096], P('head'), may hold values from 0.5 to 7
- k_gain: float32 [512], replicated, may hold values from 0.8 to 6
- w_query: bfloat16 [2048, 4096], P(None, 'head')
- w_key: bfloat16 [2048, 512], replicated
- w_value: bfloat16 [2048, 512], replicated, may hold values from -0.125 to 0.125
- w_out: bfloat16 [4096, 2048], P('head'), may hold values from -0.375 to 0.375
Outputs:
- layer_out: bfloat16 [8192, 2048], P('ctx', 'head')
Inputs may be any that keep to these rules, and one draw needn't show every extreme that they name: `expert_ids`: in each device's 128 rows no expert is named more than 12 times. `targets`: each device's 128 rows name exactly 8 positions in each block of 512 joined positions; positions may repeat.
All inputs are finite; a program needn't handle non-finite values.
Results may differ from a plain program's by a relative error of at most 0.018.
Values may be sent and summed in bfloat16 or wider, within the bound.
No kernel may reach another device: no remote copies, remote signals or barrier semaphores. Data moves between devices by JAX's collectives and lax.ppermute only.
A program may use at most 192 MiB of HBM per device.

v0:
```python
import math

import jax
import jax.numpy as jnp
from jax import lax
from jax.sharding import PartitionSpec as P

QH = 32
KVH = 4
HD = 128


EPSILON = 1e-06
THETA = 1000000.0


def grouped_exchange(shard, axis, split_dim, concat_dim, work, item_dim, out_dim):
    items = jax.tree.leaves(shard)[0].shape[item_dim]
    count = 2 if items % 2 == 0 else 1
    gathered = []
    for k in range(count):
        group = jax.tree.map(
            lambda a: lax.slice_in_dim(
                a, k * (items // count), (k + 1) * (items // count), axis=item_dim
            ),
            shard,
        )
        gathered.append(
            work(
                lax.all_to_all(
                    group, axis, split_axis=split_dim, concat_axis=concat_dim, tiled=True
                )
            )
        )
    return jax.tree.map(lambda *parts: jnp.concatenate(parts, axis=out_dim), *gathered)


def sent_to_all(shard, axis):
    count = lax.axis_size(axis)
    return lax.all_to_all(
        jnp.broadcast_to(shard[None], (count, *shard.shape)), axis, 0, 0, tiled=True
    )


def in_order(tiles, dim):
    tiles = jnp.moveaxis(tiles, 0, dim)
    lengths = tiles.shape
    return tiles.reshape(*lengths[:dim], lengths[dim] * lengths[dim + 1], *lengths[dim + 2 :])


def collect(shard, axis, dim):
    tiles = sent_to_all(shard, axis)
    return in_order(tiles, dim)


def rotary(vectors, positions):
    half_dim = vectors.shape[-1] // 2
    frequency = jnp.power(
        jnp.float32(THETA), -jnp.arange(half_dim, dtype=jnp.float32) * 2.0 / vectors.shape[-1]
    )
    angles = positions.astype(jnp.float32)[:, None] * frequency[None, :]
    cosines = jnp.cos(angles)[:, None, :]
    sines = jnp.sin(angles)[:, None, :]
    front_part = vectors[..., :half_dim]
    back_part = vectors[..., half_dim:]
    return jnp.concatenate(
        [front_part * cosines - back_part * sines, back_part * cosines + front_part * sines], -1
    )


def head_norm(vectors, scales):
    return vectors * lax.rsqrt(jnp.mean(vectors * vectors, -1, keepdims=True) + EPSILON) * scales


def expert_rows(inputs, gate_proj, up_proj, down_proj):
    dims_in = inputs.shape
    flat_rows = inputs.reshape(-1, dims_in[-1])
    gate_part = jnp.dot(flat_rows, gate_proj, preferred_element_type=jnp.float32)
    upward = jnp.dot(flat_rows, up_proj, preferred_element_type=jnp.float32)
    hidden = (jax.nn.silu(gate_part) * upward).astype(jnp.bfloat16)
    produced = jnp.dot(hidden, down_proj, preferred_element_type=jnp.float32).astype(jnp.bfloat16)
    return produced.reshape(dims_in[:-1] + (down_proj.shape[1],))


def rank_within(labels, count):
    onehot = (labels[:, None] == jnp.arange(count, dtype=jnp.int32)[None, :]).astype(jnp.int32)
    earlier = jnp.cumsum(onehot, 0) - onehot
    return jnp.sum(earlier * onehot, 1)


def attend(state_now, pieces, stacked, query_pos):
    highest, totals, weighted = state_now
    key_piece, value_piece = pieces
    scores = jnp.einsum(
        "hqd,kd->hqk", stacked, key_piece, preferred_element_type=jnp.float32
    ) / math.sqrt(key_piece.shape[1])
    key_pos = jnp.arange(key_piece.shape[0], dtype=jnp.int32)
    allowed = (query_pos[:, None] >= key_pos[None, :])[None, :, :]
    fresh = jnp.maximum(highest, jnp.max(jnp.where(allowed, scores, -1e30), -1))
    weights = jnp.where(allowed, jnp.exp(scores - fresh[:, :, None]), 0.0)
    totals = jnp.sum(weights, -1)
    weighted = jnp.einsum(
        "hqk,kd->hqd", weights.astype(jnp.bfloat16), value_piece, preferred_element_type=jnp.float32
    )
    return (fresh, totals, weighted)


def fresh_state(heads, rows, width):
    return (
        jnp.full((heads, rows), -1e30, jnp.float32),
        jnp.zeros((heads, rows), jnp.float32),
        jnp.zeros((heads, rows, width), jnp.float32),
    )


def finish(state_now):
    highest, totals, weighted = state_now
    return (weighted / totals[:, :, None]).astype(jnp.bfloat16)


def body(
    branch_rows,
    expert_ids,
    targets,
    router,
    w_gate,
    w_up,
    w_down,
    stream,
    attn_gain,
    q_gain,
    k_gain,
    w_query,
    w_key,
    w_value,
    w_out,
):
    ctx_count = lax.axis_size("ctx")
    head_count = lax.axis_size("head")
    experts = router.shape[1]
    rows_here = branch_rows.shape[0]
    top_count = expert_ids.shape[1]
    model_width = branch_rows.shape[1]
    capacity = 3 * rows_here * top_count // (2 * experts)
    logits = jnp.dot(branch_rows, router, preferred_element_type=jnp.float32)
    chosen = expert_ids[:, :, None] == jnp.arange(experts, dtype=jnp.int32)[None, None, :]
    picked = jnp.sum(jnp.where(chosen, logits[:, None, :], 0.0), -1)
    gate_probs = jax.nn.softmax(picked, -1)
    flat_ids = expert_ids.reshape(-1)
    places = flat_ids * capacity + rank_within(flat_ids, experts)
    repeated = jnp.repeat(branch_rows, top_count, axis=0)
    outgoing = jnp.zeros((experts * capacity, model_width), jnp.bfloat16).at[places].set(repeated)
    gate_local = w_gate[0]
    up_local = w_up[0]
    down_local = w_down[0]

    def serve_rows(arrived):
        produced = expert_rows(arrived, gate_local, up_local, down_local)
        return lax.all_to_all(produced, ("ctx", "head"), split_axis=0, concat_axis=0, tiled=True)

    returned = grouped_exchange(
        outgoing.reshape(experts, capacity, model_width), ("ctx", "head"), 0, 0, serve_rows, 1, 1
    )
    collected = returned.reshape(experts * capacity, model_width)[places].reshape(
        rows_here, top_count, model_width
    )
    merged = jnp.sum(gate_probs[:, :, None] * collected.astype(jnp.float32), 1).astype(jnp.bfloat16)
    local_tokens = stream.shape[0]
    slice_width = stream.shape[1]
    per_owner = rows_here // ctx_count
    owner_ids = targets // local_tokens
    order_in = rank_within(owner_ids, ctx_count)
    owner_grid = jnp.broadcast_to(owner_ids[:, None], (rows_here, head_count))
    head_grid = jnp.broadcast_to(
        jnp.arange(head_count, dtype=jnp.int32)[None, :], (rows_here, head_count)
    )
    order_grid = jnp.broadcast_to(order_in[:, None], (rows_here, head_count))
    local_grid = jnp.broadcast_to((targets % local_tokens)[:, None], (rows_here, head_count))
    parcels = jnp.zeros((ctx_count, head_count, per_owner, slice_width), jnp.bfloat16)
    parcels = parcels.at[owner_grid, head_grid, order_grid].set(
        merged.reshape(rows_here, head_count, slice_width)
    )
    spot_table = (
        jnp.zeros((ctx_count, head_count, per_owner), jnp.int32)
        .at[owner_grid, head_grid, order_grid]
        .set(local_grid)
    )
    landed, spot_ids = (
        lax.all_to_all(
            parcels.reshape(ctx_count * head_count, per_owner, slice_width),
            ("ctx", "head"),
            split_axis=0,
            concat_axis=0,
            tiled=True,
        ),
        lax.all_to_all(
            spot_table.reshape(ctx_count * head_count, per_owner),
            ("ctx", "head"),
            split_axis=0,
            concat_axis=0,
            tiled=True,
        ),
    )
    joined = (
        stream.astype(jnp.float32)
        .at[spot_ids.reshape(-1)]
        .add(landed.reshape(-1, slice_width).astype(jnp.float32))
        .astype(jnp.bfloat16)
    )
    full_rows = collect(joined, "head", 1)
    full_float = full_rows.astype(jnp.float32)
    normed = (
        full_float
        * lax.rsqrt(jnp.mean(full_float * full_float, -1, keepdims=True) + EPSILON)
        * attn_gain
    ).astype(jnp.bfloat16)
    per_device = w_query.shape[1] // HD
    first_head = lax.axis_index("head") * per_device
    kv_head = first_head // (QH // KVH)
    ctx_here = lax.axis_index("ctx")
    start_pos = ctx_here * local_tokens
    positions = start_pos + jnp.arange(local_tokens, dtype=jnp.int32)
    queries = jnp.dot(normed, w_query, preferred_element_type=jnp.float32).reshape(
        local_tokens, per_device, HD
    )
    queries = rotary(head_norm(queries, q_gain.reshape(per_device, HD)), positions).astype(
        jnp.bfloat16
    )
    stacked_queries = queries.transpose(1, 0, 2)
    key_columns = lax.dynamic_slice_in_dim(w_key, kv_head * HD, HD, 1)
    value_columns = lax.dynamic_slice_in_dim(w_value, kv_head * HD, HD, 1)
    key_scales = lax.dynamic_slice_in_dim(k_gain, kv_head * HD, HD, 0)
    key_rows = jnp.dot(normed, key_columns, preferred_element_type=jnp.float32).reshape(
        local_tokens, 1, HD
    )
    key_rows = (
        rotary(head_norm(key_rows, key_scales.reshape(1, HD)), positions)
        .astype(jnp.bfloat16)
        .reshape(local_tokens, HD)
    )
    values = jnp.dot(normed, value_columns, preferred_element_type=jnp.float32).astype(jnp.bfloat16)
    start_states = fresh_state(per_device, local_tokens, HD)
    folded = attend(
        start_states,
        (
            lax.all_gather(key_rows, "ctx", axis=0, tiled=True),
            lax.all_gather(values, "ctx", axis=0, tiled=True),
        ),
        stacked_queries,
        positions,
    )
    attended_heads = finish(folded)
    attended = attended_heads.transpose(1, 0, 2).reshape(local_tokens, per_device * HD)
    partial_out = jnp.dot(attended, w_out, preferred_element_type=jnp.float32)
    summed = lax.psum_scatter(
        partial_out.astype(jnp.bfloat16), "head", scatter_dimension=1, tiled=True
    ).astype(jnp.float32)
    return (joined.astype(jnp.float32) + summed).astype(jnp.bfloat16)


def solution(mesh):
    in_specs = (
        P(("ctx", "head"), None),
        P(("ctx", "head"), None),
        P(("ctx", "head")),
        P(),
        P(("ctx", "head"), None, None),
        P(("ctx", "head"), None, None),
        P(("ctx", "head"), None, None),
        P("ctx", "head"),
        P(),
        P("head"),
        P(),
        P(None, "head"),
        P(),
        P(),
        P("head", None),
    )
    out_specs = P("ctx", "head")
    return jax.shard_map(body, mesh=mesh, in_specs=in_specs, out_specs=out_specs, check_vma=False)
```

profile of v0, /device:TPU:1, one launch (start us, length us, event | category | flops | bytes accessed | tf_op | source)
XLA Modules:
  0.0 565.9 jit_solution(18149453498909541032)
XLA Ops:
  11.4 10.7 %scatter_custom_fusion = bf16[1536,2048]{1,0:T(8,128)(2,1)} fusion(s32[1024]{0:T(1024)S(1)} %bitcast.116, bf16[]{:T(256)} %constant.93.clone.1, bf16[128,2048]{1,0:T(8,128)(2,1)} %param.15), kind=kCustom, calls=%fused_computation.18 | custom fusion | bytes 6815746 | tf_op jit(solution)/shard_map/scatter | solution.py:152
  22.1 10.6 %reshape.495 = bf16[128,12,2048]{2,1,0:T(8,128)(2,1)} reshape(bf16[1536,2048]{1,0:T(8,128)(2,1)} %scatter_custom_fusion) | data formatting | bytes 12582912 | tf_op jit(solution)/shard_map/reshape | solution.py:162
  32.7 7.0 %fusion.80 = (bf16[128,6,2048]{2,1,0:T(8,128)(2,1)}, bf16[128,6,2048]{2,1,0:T(8,128)(2,1)S(1)}) fusion(bf16[128,12,2048]{2,1,0:T(8,128)(2,1)} %reshape.495), kind=kLoop, calls=%fused_computation.133 | loop fusion | bytes 12582912 | tf_op jit(solution)/shard_map/slice | solution.py:23
  39.7 64.4 %all_to_all.39 = bf16[128,6,2048]{2,1,0:T(8,128)(2,1)} all-to-all(bf16[128,6,2048]{2,1,0:T(8,128)(2,1)S(1)} %get-tuple-element.10), channel_id=1, replica_groups=mesh['ctx'=16,'head'=8] {'ctx','head'}, dimensions={0} | all-to-all | bytes 6291456 | tf_op jit(solution)/shard_map/all_to_all | solution.py:30
  110.0 6.3 %reshape.498 = bf16[768,2048]{1,0:T(8,128)(2,1)} reshape(bf16[128,6,2048]{2,1,0:T(8,128)(2,1)} %all_to_all.39) | data formatting | bytes 6291456 | tf_op jit(solution)/shard_map/reshape | solution.py:77
  116.4 6.9 %fusion.12 = f32[768,768]{1,0:T(8,128)} fusion(bf16[768,2048]{1,0:T(8,128)(2,1)} %reshape.498, bf16[1,2048,768]{2,1,0:T(8,128)(2,1)} %param.20), kind=kOutput, calls=%fused_computation.26 | convolution fusion | flops 2415919104 | bytes 8650752 | tf_op jit(solution)/shard_map/dot_general | solution.py:79
  123.2 11.0 %convolution_convert_fusion = bf16[768,2048]{1,0:T(8,128)(2,1)} fusion(bf16[1,768,2048]{2,1,0:T(8,128)(2,1)S(1)} %copy-done, f32[768,768]{1,0:T(8,128)} %fusion.12, bf16[768,2048]{1,0:T(8,128)(2,1)} %reshape.498, bf16[1,2048,768]{2,1,0:T(8,128)(2,1)} %param.19), kind=kOutput, calls=%fused_computation.22 | convolution fusion | flops 4836950016 | bytes 14942208 | tf_op jit(solution)/shard_map/dot_general | solution.py:81
  140.5 22.2 %all-to-all-done.1 = bf16[128,6,2048]{2,1,0:T(8,128)(2,1)} async-done(((bf16[128,6,2048]{2,1,0:T(8,128)(2,1)}), bf16[128,6,2048]{2,1,0:T(8,128)(2,1)}, u32[]{:S(2)}, u32[]{:S(2)}) %all-to-all-start.1) | async-done | bytes 3145760 | tf_op jit(solution)/shard_map/all_to_all | solution.py:30
  175.1 6.9 %fusion.14 = f32[768,768]{1,0:T(8,128)} fusion(bf16[768,2048]{1,0:T(8,128)(2,1)} %reshape.496, bf16[1,2048,768]{2,1,0:T(8,128)(2,1)} %param.20), kind=kOutput, calls=%fused_computation.28 | convolution fusion | flops 2415919104 | bytes 8650752 | tf_op jit(solution)/shard_map/dot_general | solution.py:79
  182.0 11.0 %convolution_convert_fusion.1 = bf16[768,2048]{1,0:T(8,128)(2,1)} fusion(bf16[1,768,2048]{2,1,0:T(8,128)(2,1)S(1)} %copy-done, f32[768,768]{1,0:T(8,128)} %fusion.14, bf16[768,2048]{1,0:T(8,128)(2,1)} %reshape.496, bf16[1,2048,768]{2,1,0:T(8,128)(2,1)} %param.19), kind=kOutput, calls=%fused_computation.23 | convolution fusion | flops 4836950016 | bytes 14942208 | tf_op jit(solution)/shard_map/dot_general | solution.py:81
  199.3 22.1 %all-to-all-done.4 = bf16[128,6,2048]{2,1,0:T(8,128)(2,1)} async-done(((bf16[128,6,2048]{2,1,0:T(8,128)(2,1)}), bf16[128,6,2048]{2,1,0:T(8,128)(2,1)}, u32[]{:S(2)}, u32[]{:S(2)}) %all-to-all-start.4) | async-done | bytes 3145760 | tf_op jit(solution)/shard_map/all_to_all | solution.py:159
  234.5 45.2 %all-to-all-done.2 = bf16[128,6,2048]{2,1,0:T(8,128)(2,1)} async-done(((bf16[128,6,2048]{2,1,0:T(8,128)(2,1)}), bf16[128,6,2048]{2,1,0:T(8,128)(2,1)}, u32[]{:S(2)}, u32[]{:S(2)}) %all-to-all-start.2) | async-done | bytes 3145760 | tf_op jit(solution)/shard_map/all_to_all | solution.py:159
  284.5 10.4 %pad_maximum_fusion = bf16[128,12,2048]{2,1,0:T(8,128)(2,1)} fusion(bf16[128,6,2048]{2,1,0:T(8,128)(2,1)} %all-to-all-done.4, bf16[128,6,2048]{2,1,0:T(8,128)(2,1)} %all-to-all-done.2), kind=kLoop, calls=%fused_computation.12 | loop fusion | flops 12582912 | bytes 12582912 | tf_op jit(solution)/shard_map/concatenate | solution.py:35
  295.0 10.7 %reshape.500 = bf16[1536,2048]{1,0:T(8,128)(2,1)} reshape(bf16[128,12,2048]{2,1,0:T(8,128)(2,1)} %pad_maximum_fusion) | data formatting | bytes 12582912 | tf_op jit(solution)/shard_map/reshape | solution.py:164
  305.7 12.4 %gather_fusion = bf16[1024,2048]{1,0:T(8,128)(2,1)} fusion(bf16[1536,2048]{1,0:T(8,128)(2,1)} %reshape.500, s32[1024]{0:T(1024)S(1)} %broadcast_clamp_fusion), kind=kCustom, calls=%fused_computation | custom fusion | bytes 8392704 | tf_op jit(solution)/shard_map/gather | solution.py:164
  318.1 6.6 %fusion.5 = bf16[128,2048]{1,0:T(8,128)(2,1)S(1)} fusion(bf16[1024,2048]{1,0:T(8,128)(2,1)} %gather_fusion, f32[128,8]{1,0:T(8,128)S(1)} %fusion.68), kind=kLoop, calls=%fused_computation.14 | loop fusion | flops 6029312 | bytes 4722688 | tf_op jit(solution)/shard_map/reduce_sum | solution.py:167
  330.8 9.8 %all-to-all-start.5 = ((bf16[128,8,256]{2,1,0:T(8,128)(2,1)}), bf16[128,8,256]{2,1,0:T(8,128)(2,1)S(1)}, u32[]{:S(2)}, u32[]{:S(2)}) async-start(bf16[128,8,256]{2,1,0:T(8,128)(2,1)} %bitcast.13), calls=%async_computation.5 | async-start | bytes 1048576 | tf_op jit(solution)/shard_map/all_to_all | solution.py:189
  342.1 12.1 %all-to-all-done.5 = bf16[128,8,256]{2,1,0:T(8,128)(2,1)S(1)} async-done(((bf16[128,8,256]{2,1,0:T(8,128)(2,1)}), bf16[128,8,256]{2,1,0:T(8,128)(2,1)S(1)}, u32[]{:S(2)}, u32[]{:S(2)}) %all-to-all-start.5) | async-done | bytes 524320 | tf_op jit(solution)/shard_map/all_to_all | solution.py:189
  368.2 25.7 %all-to-all-done.6 = bf16[8,512,256]{2,1,0:T(8,128)(2,1)} async-done(((bf16[8,512,256]{2,1,0:T(8,128)(2,1)}), bf16[8,512,256]{2,1,0:T(8,128)(2,1)}, u32[]{:S(2)}, u32[]{:S(2)}) %all-to-all-start.6) | async-done | bytes 2097184 | tf_op jit(solution)/shard_map/all_to_all | solution.py:40
  418.2 25.9 %all-gather.3.cloned.1.call-done = bf16[8192,128]{0,1:T(8,128)(2,1)} async-done(((bf16[512,128]{0,1:T(8,128)(2,1)}), bf16[8192,128]{0,1:T(8,128)(2,1)}) %all-gather.3.cloned.1.call-update) | async-done | bytes 2097168 | tf_op jit(solution)/shard_map/all_gather | solution.py:246
  444.2 27.2 %select_reduce_fusion = (f32[4,512]{1,0:T(4,128)S(1)}, f32[4,512,8192]{2,1,0:T(8,128)}) fusion(pred[512,8192]{1,0:T(8,128)(4,1)} %iota_compare_fusion, bf16[8192,128]{0,1:T(8,128)(2,1)} %all-gather.3.cloned.1.call-done, bf16[512,4,64]{0,2,1:T(8,128)(2,1)S(1)} %get-tuple-element.12, bf16[512,4,64]{0,2,1:T(8,128)(2,1)S(1)} %get-tuple-element.11), kind=kOutput, calls=%fused_computation.6 | convolution fusion | flops 4346345472 | bytes 73932800 | tf_op jit(solution)/shard_map/hqd,kd->hqk/dot_general | solution.py:94
  471.4 23.3 %fusion = f32[4,512]{1,0:T(4,128)S(1)} fusion(f32[4,512,8192]{2,1,0:T(8,128)} %get-tuple-element.24, f32[4,512]{1,0:T(4,128)S(1)} %broadcast_maximum_fusion, pred[512,8192]{1,0:T(8,128)(4,1)} %iota_compare_fusion), kind=kLoop, calls=%fused_computation.7 | loop fusion | flops 67106816 | bytes 71319552 | tf_op jit(solution)/shard_map/reduce_sum | solution.py:101
  494.7 26.5 %divide_convert_fusion = bf16[512,4,128]{0,2,1:T(8,128)(2,1)} fusion(bf16[8192,128]{1,0:T(8,128)(2,1)} %all-gather.5.cloned.1.call-done, f32[4,512,8192]{2,1,0:T(8,128)} %get-tuple-element.24, f32[4,512]{1,0:T(4,128)S(1)} %broadcast_maximum_fusion, pred[512,8192]{1,0:T(8,128)(4,1)} %iota_compare_fusion, f32[512,4]{0,1:T(4,128)S(1)} %bitcast.118), kind=kOutput, calls=%fused_computation.46 | convolution fusion | flops 4362600448 | bytes 73940992 | tf_op jit(solution)/shard_map/hqk,kd->hqd/dot_general | solution.py:102
  525.8 31.2 %reduce-scatter.2.cloned.1.call-done = bf16[512,256]{1,0:T(8,128)(2,1)} async-done(((bf16[512,2048]{1,0:T(8,128)(2,1)}), bf16[512,256]{1,0:T(8,128)(2,1)}) %reduce-scatter.2.cloned.1.call-update) | async-done | bytes 262160 | tf_op jit(solution)/shard_map/reduce_scatter | solution.py:255
  (127 shorter events, 105.8 us)
Async XLA Ops:
  6.5 116.7 %copy-start = (bf16[1,768,2048]{2,1,0:T(8,128)(2,1)S(1)}, bf16[1,768,2048]{2,1,0:T(8,128)(2,1)}, u32[]{:S(2)}) copy-start(bf16[1,768,2048]{2,1,0:T(8,128)(2,1)} %param.21) | copy-start | bytes 9437188
  104.1 58.6 %all-to-all-start.1 = ((bf16[128,6,2048]{2,1,0:T(8,128)(2,1)}), bf16[128,6,2048]{2,1,0:T(8,128)(2,1)}, u32[]{:S(2)}, u32[]{:S(2)}) async-start(bf16[128,6,2048]{2,1,0:T(8,128)(2,1)} %get-tuple-element.9), calls=%async_computation.1 | async-start | bytes 8388608 | tf_op jit(solution)/shard_map/all_to_all | solution.py:30
  162.6 58.8 %all-to-all-start.4 = ((bf16[128,6,2048]{2,1,0:T(8,128)(2,1)}), bf16[128,6,2048]{2,1,0:T(8,128)(2,1)}, u32[]{:S(2)}, u32[]{:S(2)}) async-start(bf16[128,6,2048]{2,1,0:T(8,128)(2,1)} %reshape.499), calls=%async_computation.4 | async-start | bytes 8388608 | tf_op jit(solution)/shard_map/all_to_all | solution.py:159
  199.2 27.7 %copy-start.15 = (s32[128]{0:T(128)S(1)}, s32[128]{0:T(128)}, u32[]{:S(2)}) copy-start(s32[128]{0:T(128)} %param.17) | copy-start | bytes 1540
  199.2 28.5 %copy-start.12 = (s32[3]{0:T(128)S(1)}, s32[3]{0:T(128)}, u32[]{:S(2)}) copy-start(s32[3]{0:T(128)} %constant.119) | copy-start | bytes 40
  199.2 28.6 %copy-start.13 = (s32[3]{0:T(128)S(1)}, s32[3]{0:T(128)}, u32[]{:S(2)}) copy-start(s32[3]{0:T(128)} %constant.122) | copy-start | bytes 40
  199.2 28.6 %copy-start.14 = (s32[3]{0:T(128)S(1)}, s32[3]{0:T(128)}, u32[]{:S(2)}) copy-start(s32[3]{0:T(128)} %constant.116) | copy-start | bytes 40
  199.2 34.1 %copy-start.7 = (bf16[128,2048]{1,0:T(8,128)(2,1)S(1)}, bf16[128,2048]{1,0:T(8,128)(2,1)}, u32[]{:S(2)}) copy-start(bf16[128,2048]{1,0:T(8,128)(2,1)} %param.15) | copy-start | bytes 1572868
  199.3 34.1 %copy-start.8 = (bf16[2048,128]{1,0:T(8,128)(2,1)S(1)}, bf16[2048,128]{1,0:T(8,128)(2,1)}, u32[]{:S(2)}) copy-start(bf16[2048,128]{1,0:T(8,128)(2,1)} %param.18) | copy-start | bytes 1572868
  221.4 58.3 %all-to-all-start.2 = ((bf16[128,6,2048]{2,1,0:T(8,128)(2,1)}), bf16[128,6,2048]{2,1,0:T(8,128)(2,1)}, u32[]{:S(2)}, u32[]{:S(2)}) async-start(bf16[128,6,2048]{2,1,0:T(8,128)(2,1)} %reshape.497), calls=%async_computation.2 | async-start | bytes 8388608 | tf_op jit(solution)/shard_map/all_to_all | solution.py:159
  279.7 51.1 %all-to-all-start = ((s32[128,1,8]{2,1,0:T(1,128)}), s32[128,1,8]{2,1,0:T(1,128)S(1)}, u32[]{:S(2)}, u32[]{:S(2)}) async-start(s32[128,1,8]{2,1,0:T(1,128)} %bitcast.1), calls=%async_computation | async-start | bytes 131072 | tf_op jit(solution)/shard_map/all_to_all | solution.py:196
  318.1 22.6 %copy-start.9 = (bf16[512,256]{1,0:T(8,128)(2,1)S(1)}, bf16[512,256]{1,0:T(8,128)(2,1)}, u32[]{:S(2)}) copy-start(bf16[512,256]{1,0:T(8,128)(2,1)} %param.22) | copy-start | bytes 786436
  330.8 23.4 %all-to-all-start.5 = ((bf16[128,8,256]{2,1,0:T(8,128)(2,1)}), bf16[128,8,256]{2,1,0:T(8,128)(2,1)S(1)}, u32[]{:S(2)}, u32[]{:S(2)}) async-start(bf16[128,8,256]{2,1,0:T(8,128)(2,1)} %bitcast.13), calls=%async_computation.5 | async-start | bytes 1048576 | tf_op jit(solution)/shard_map/all_to_all | solution.py:189
  360.6 1.5 copy-start.4
  362.0 31.9 %all-to-all-start.6 = ((bf16[8,512,256]{2,1,0:T(8,128)(2,1)}), bf16[8,512,256]{2,1,0:T(8,128)(2,1)}, u32[]{:S(2)}, u32[]{:S(2)}) async-start(bf16[8,512,256]{2,1,0:T(8,128)(2,1)} %broadcast_in_dim.69), calls=%async_computation.6 | async-start | bytes 4194304 | tf_op jit(solution)/shard_map/all_to_all | solution.py:40
  367.5 76.7 %all-gather.3.cloned.1.call-start = ((), (), s32[]{:S(2)}) async-start(), calls=%async_computation.8 | async-start | bytes 2228224 | tf_op jit(solution)/shard_map/all_gather | solution.py:246
  368.2 29.1 %copy-start.10 = (f32[2048]{0:T(1024)S(1)}, f32[2048]{0:T(1024)}, u32[]{:S(2)}) copy-start(f32[2048]{0:T(1024)} %param.23) | copy-start | bytes 24580
  397.9 1.4 copy-start.2
  402.1 92.6 %all-gather.5.cloned.1.call-start = ((), (), s32[]{:S(2)}) async-start(), calls=%async_computation.9 | async-start | bytes 2228224 | tf_op jit(solution)/shard_map/all_gather | solution.py:247
  412.2 1.6 copy-start.6
  413.8 1.6 copy-start.3
  413.8 4.1 copy-start.11
  417.8 139.1 %reduce-scatter.2.cloned.1.call-start = ((), (), s32[]{:S(2)}) async-start(), calls=%async_computation.10 | async-start | bytes 2359296 | tf_op jit(solution)/shard_map/reduce_scatter | solution.py:255
  521.2 37.6 %copy-start.1 = (bf16[1,768,2048]{2,1,0:T(8,128)(2,1)S(1)}, bf16[1,768,2048]{2,1,0:T(8,128)(2,1)}, u32[]{:S(2)}) copy-start(bf16[1,768,2048]{2,1,0:T(8,128)(2,1)} %param.21) | copy-start | bytes 9437188
  (1 other events, 0.8 us)
Sparse Core Ops, SparseCore 0:
  402.3 41.8 all-gather.2
  446.3 44.3 all-gather.4
  525.9 31.0 reduce-scatter.1
where the time goes:
time: 577 us; the launch traced here: 566 us
  waiting for transfers between devices  184 us (32%)
  local copies, waits for them, and re-layouts  103 us (18%)
  matrix products  99.5 us (17%)
  blocking collectives  64.4 us (11%)
  other arithmetic  62.2 us (11%)
  starting transfers between devices  37.8 us (7%)
  between operations  14.1 us (2%)
    all_to_all x2, waiting for transfers between devices, serve_rows(): lax.all_to_all(produced, ('ctx', 'head'), split_axis=0, concat_axis=0, ti...  67.4 us
    all_to_all x1, blocking collectives, grouped_exchange(): lax.all_to_all(group, axis, split_axis=split_dim, concat_axis=concat_dim,...  64.4 us
    reduce_scatter x1, waiting for transfers between devices, body(): lax.psum_scatter(partial_out.astype(jnp.bfloat16), 'head', scatter_dimens...  31.2 us
    dot_general x1, matrix products, attend(): jnp.einsum('hqd,kd->hqk', stacked, key_piece, preferred_element_type=jnp....  27.2 us
    dot_general x1, matrix products, attend(): jnp.einsum('hqk,kd->hqd', weights.astype(jnp.bfloat16), value_piece, pref...  26.5 us
    all_gather x1, waiting for transfers between devices, body(): lax.all_gather(key_rows, 'ctx', axis=0, tiled=True)  25.9 us
    all_to_all x1, waiting for transfers between devices, sent_to_all(): lax.all_to_all(jnp.broadcast_to(shard[None], (count, *shard.shape)), axis...  25.7 us
    reduce_sum x1, other arithmetic, attend(): totals = jnp.sum(weights, -1)  23.3 us
  transfers between devices with their start and end apart: 9, of which 7 were waited for; matrix products, arithmetic and copies ran while one was open for 32% of the time, Pallas kernels for 0%

commit v1 on v0

v1 whole, which is shorter than its diff:
```python
import math

import jax
import jax.numpy as jnp
from jax import lax
from jax.experimental import pallas as pl
from jax.experimental.pallas import tpu as pltpu
from jax.sharding import PartitionSpec as P

QH = 32
KVH = 4
HD = 128
EPSILON = 1e-06
THETA = 1000000.0
F32 = jnp.float32
BF16 = jnp.bfloat16
VMEM = pltpu.VMEM
NEG = -1e30


def iota(shape, dim):
    return lax.broadcasted_iota(jnp.int32, shape, dim)


def dot(a, b):
    return jnp.dot(a, b, preferred_element_type=F32)


def dot_t(a, b):
    return lax.dot_general(a, b, (((1,), (1,)), ((), ())), preferred_element_type=F32)


def dispatch_kernel(rows_ref, ids_ref, trow_ref, tcol_ref, router_ref, y_ref, rank_ref, gate_ref, spot_ref, rows_s, rank_s):
    step = pl.program_id(0)
    experts = 128
    blk = y_ref.shape[0] // 8

    @pl.when(step == 0)
    def _():
        n = rows_ref.shape[0]
        first = iota((n, n), 0)
        second = iota((n, n), 1)
        owner_row = trow_ref[...] // 512
        owner_col = tcol_ref[...] // 512
        same = jnp.where((owner_col == owner_row) & (first < second), 1.0, 0.0)
        place = owner_row.astype(F32) * 8.0 + jnp.sum(same, 0, keepdims=True)
        perm = jnp.where(first.astype(F32) == place, 1.0, 0.0)
        spot = (trow_ref[...] % 512).astype(F32)
        spot_ref[...] = jnp.broadcast_to(jnp.sum(perm * spot, 1, keepdims=True), (n, 128))
        perm_b = perm.astype(BF16)
        rows = dot(perm_b, rows_ref[...]).astype(BF16)
        rows_s[...] = rows
        ids = dot_t(ids_ref[...].astype(F32).astype(BF16), perm_b)
        expert = iota((experts, n), 0).astype(F32)
        member = jnp.zeros((experts, n), F32)
        for k in range(ids.shape[0]):
            member = member + jnp.where(expert == ids[k : k + 1, :], 1.0, 0.0)
        before = jnp.where(first < second, 1.0, 0.0).astype(BF16)
        rank = jnp.where(member > 0.5, dot(member.astype(BF16), before), -1.0)
        rank_s[...] = rank.astype(BF16)
        rank_ref[...] = rank.T
        member_q = member.T > 0.5
        logits = dot(rows, router_ref[...])
        highest = jnp.max(jnp.where(member_q, logits, NEG), 1, keepdims=True)
        raised = jnp.where(member_q, jnp.exp(jnp.minimum(logits - highest, 0.0)), 0.0)
        gate_ref[...] = raised / jnp.sum(raised, 1, keepdims=True)

    spread = jnp.where(iota((blk * 8, experts), 0) // 8 + step * blk == iota((blk * 8, experts), 1), 1.0, 0.0).astype(BF16)
    rank_e = dot(spread, rank_s[...])
    slot = (iota(rank_e.shape, 0) % 8).astype(F32)
    main = jnp.where(rank_e == slot, 1.0, 0.0).astype(BF16)
    low = jnp.where((rank_e == slot + 8.0) & (slot < 4.0), 1.0, 0.0).astype(BF16)
    high = jnp.where((rank_e == slot + 4.0) & (slot >= 4.0), 1.0, 0.0).astype(BF16)
    half = rows_s.shape[1] // 2
    y_ref[:, : 2 * half] = dot(main, rows_s[...]).astype(BF16)
    y_ref[:, 2 * half :] = (dot(low, rows_s[:, :half]) + dot(high, rows_s[:, half:])).astype(BF16)


def dispatch(rows, ids, targets, router):
    n, width = rows.shape
    steps = 4
    whole = lambda shape: pl.BlockSpec(shape, lambda i: tuple(0 for _ in shape))
    return pl.pallas_call(
        dispatch_kernel,
        grid=(steps,),
        in_specs=[whole((n, width)), whole((8, n)), whole((1, n)), whole((n, 1)), whole(router.shape)],
        out_specs=[
            pl.BlockSpec((1024 // steps, width * 3 // 2), lambda i: (i, 0)),
            whole((n, 128)),
            whole((n, 128)),
            whole((n, 128)),
        ],
        out_shape=[
            jax.ShapeDtypeStruct((1024, width * 3 // 2), BF16),
            jax.ShapeDtypeStruct((n, 128), F32),
            jax.ShapeDtypeStruct((n, 128), F32),
            jax.ShapeDtypeStruct((n, 128), F32),
        ],
        scratch_shapes=[VMEM((n, width), BF16), VMEM((128, n), BF16)],
        compiler_params=pltpu.CompilerParams(vmem_limit_bytes=40 * 1024 * 1024),
        name="dispatch_rows",
    )(rows, ids.T, targets.reshape(1, n), targets.reshape(n, 1), router)


def expert_kernel(y_ref, wg_ref, wu_ref, wd_ref, o_ref):
    rows = y_ref.shape[0]
    half_rows = rows // 2
    width = wg_ref.shape[0]
    half = width // 2
    r = iota((half_rows, rows), 0)
    col = iota((half_rows, rows), 1)
    source = r // 4 * 8 + r % 4
    low = jnp.where(col == source, 1.0, 0.0).astype(BF16)
    high = jnp.where(col == source + 4, 1.0, 0.0).astype(BF16)
    extra = y_ref[:, width:]
    inputs = jnp.concatenate(
        [
            y_ref[:, :width],
            jnp.concatenate([dot(low, extra).astype(BF16), dot(high, extra).astype(BF16)], 1),
        ],
        0,
    )
    gate_part = dot(inputs, wg_ref[...])
    upward = dot(inputs, wu_ref[...])
    hidden = (gate_part / (1.0 + jnp.exp(-gate_part)) * upward).astype(BF16)
    produced = dot(hidden, wd_ref[...]).astype(BF16)
    o_ref[:, :width] = produced[:rows]
    rt = iota((rows, half_rows), 0)
    ct = iota((rows, half_rows), 1)
    target = ct // 4 * 8 + ct % 4
    low_t = jnp.where(rt == target, 1.0, 0.0).astype(BF16)
    high_t = jnp.where(rt == target + 4, 1.0, 0.0).astype(BF16)
    o_ref[:, width:] = (dot(low_t, produced[rows:, :half]) + dot(high_t, produced[rows:, half:])).astype(BF16)


def run_expert(y, w_gate, w_up, w_down):
    steps = 4
    whole = lambda shape: pl.BlockSpec(shape, lambda i: tuple(0 for _ in shape), pipeline_mode=pl.Buffered(1))
    tile = pl.BlockSpec((y.shape[0] // steps, y.shape[1]), lambda i: (i, 0))
    return pl.pallas_call(
        expert_kernel,
        grid=(steps,),
        in_specs=[tile, whole(w_gate.shape), whole(w_up.shape), whole(w_down.shape)],
        out_specs=tile,
        out_shape=jax.ShapeDtypeStruct(y.shape, BF16),
        compiler_params=pltpu.CompilerParams(vmem_limit_bytes=52 * 1024 * 1024),
        name="expert_ffn",
    )(y, w_gate, w_up, w_down)


def combine_kernel(r_ref, extra_ref, rank_ref, gate_ref, spot_ref, o_ref, weight_s):
    step = pl.program_id(0)
    n, experts = rank_ref.shape
    rows = r_ref.shape[0]

    @pl.when(step == 0)
    def _():
        spread = jnp.where(iota((experts, rows), 0) == iota((experts, rows), 1) // 8, 1.0, 0.0).astype(BF16)
        gate = gate_ref[...]
        gate_hi = gate.astype(BF16)
        gate_lo = (gate - gate_hi.astype(F32)).astype(BF16)
        rank_e = dot(rank_ref[...].astype(BF16), spread)
        slot = (iota(rank_e.shape, 1) % 8).astype(F32)
        main = rank_e == slot
        low = (rank_e == slot + 8.0) & (slot < 4.0)
        high = (rank_e == slot + 4.0) & (slot >= 4.0)
        for part, gates in enumerate((gate_hi, gate_lo)):
            spread_gate = dot(gates, spread)
            lines = slice(part * n, (part + 1) * n)
            chosen = jnp.where(main, spread_gate, 0.0).astype(BF16)
            weight_s[0, lines, :rows] = chosen
            weight_s[1, lines, :rows] = chosen
            weight_s[0, lines, rows:] = jnp.where(low, spread_gate, 0.0).astype(BF16)
            weight_s[1, lines, rows:] = jnp.where(high, spread_gate, 0.0).astype(BF16)

    both = weight_s[step // (pl.num_programs(0) // 2)]
    merged = dot(both[:, :rows], r_ref[...]) + dot(both[:, rows:], extra_ref[...])
    merged = merged[:n] + merged[n:]
    parts = o_ref.shape[1]
    w = merged.shape[1] // parts
    spot = spot_ref[...]
    lane = iota(spot.shape, 1)
    big = jnp.floor(spot * (1.0 / 16.0))
    tail = jnp.where(lane == 0, big, jnp.where(lane == 1, spot - 16.0 * big, 0.0))
    tail = tail.reshape(n // 8, 8, 128).astype(BF16)
    for h in range(parts):
        o_ref[:, h, :, :w] = merged[:, h * w : (h + 1) * w].reshape(n // 8, 8, w).astype(BF16)
        o_ref[:, h, :, w:] = tail


def combine(r, rank, gate, spot):
    steps = 4
    n = rank.shape[0]
    width = r.shape[1] * 2 // 3
    rows = r.shape[0]
    whole = lambda shape: pl.BlockSpec(shape, lambda i: tuple(0 for _ in shape))
    return pl.pallas_call(
        combine_kernel,
        grid=(steps,),
        in_specs=[
            pl.BlockSpec((rows, width // steps), lambda i: (0, i)),
            pl.BlockSpec((rows, width // steps), lambda i: (0, steps + i % (steps // 2))),
            whole((n, 128)),
            whole((n, 128)),
            whole((n, 128)),
        ],
        out_specs=pl.BlockSpec((n // 8, 8 // steps, 8, width // 8 + 128), lambda i: (0, i, 0, 0)),
        out_shape=jax.ShapeDtypeStruct((n // 8, 8, 8, width // 8 + 128), BF16),
        scratch_shapes=[VMEM((2, 2 * n, 2 * rows), BF16)],
        compiler_params=pltpu.CompilerParams(vmem_limit_bytes=40 * 1024 * 1024),
        name="combine_rows",
    )(r, r, rank, gate, spot)


def join_kernel(landed_ref, stream_ref, o_ref):
    tokens, w = stream_ref.shape
    tail = landed_ref[:, w:].astype(F32)
    spot = tail[:, 0:1] * 16.0 + tail[:, 1:2]
    count = landed_ref.shape[0]
    hit = jnp.where(spot == iota((count, tokens), 1).astype(F32), 1.0, 0.0).astype(BF16)
    added = lax.dot_general(hit, landed_ref[:, :w], (((0,), (0,)), ((), ())), preferred_element_type=F32)
    o_ref[...] = (stream_ref[...].astype(F32) + added).astype(BF16)


def join(landed, stream):
    return pl.pallas_call(
        join_kernel,
        out_shape=jax.ShapeDtypeStruct(stream.shape, BF16),
        compiler_params=pltpu.CompilerParams(vmem_limit_bytes=40 * 1024 * 1024),
        name="join_rows",
    )(landed, stream)


def qkv_kernel(place_ref, *refs):
    x_refs = refs[:8]
    gain_ref, wq_ref, wk_ref, wv_ref, qg_ref, kg_ref, cos_ref, sin_ref, q_ref, kv_ref, norm_s = refs[8:]
    z = place_ref[1]
    core = place_ref[2]
    tokens, w = x_refs[0].shape
    width = 8 * w
    square = jnp.zeros((tokens, 1), F32)
    for x_ref in x_refs:
        x = x_ref[...].astype(F32)
        square = square + jnp.sum(x * x, 1, keepdims=True)
    scale = lax.rsqrt(square * (1.0 / width) + EPSILON)
    half = tokens // 2
    start = pl.multiple_of(core * half, half)
    for i, x_ref in enumerate(x_refs):
        block = 2 * lax.rem(z + 4 - i % 4, 4) + (core if i < 4 else 1 - core)
        norm = (x_ref[...].astype(F32) * scale * gain_ref[pl.ds(block, 1), :]).astype(BF16)
        norm_s[:, pl.ds(pl.multiple_of(block * w, w), w)] = norm
    queries = dot(norm_s[...], wq_ref[...])
    mine = norm_s[pl.ds(start, half), :]
    keys = dot(mine, wk_ref[...])
    values = dot(mine, wv_ref[...])
    cos = cos_ref[...]
    sin = sin_ref[...]

    def finished(vectors, gains, cos, sin):
        mean = jnp.mean(vectors * vectors, -1, keepdims=True)
        vectors = vectors * lax.rsqrt(mean + EPSILON) * gains
        return vectors * cos + pltpu.roll(vectors, HD // 2, 1) * sin

    factor = math.log2(math.e) / math.sqrt(HD)
    for h in range(q_ref.shape[0]):
        part = slice(h * HD, (h + 1) * HD)
        q_ref[h] = (finished(queries[:, part], qg_ref[:, part], cos, sin) * factor).astype(BF16)
    cos_k = cos_ref[pl.ds(start, half), :]
    sin_k = sin_ref[pl.ds(start, half), :]
    kv_ref[:, :HD] = finished(keys, kg_ref[...], cos_k, sin_k).astype(BF16)
    kv_ref[:, HD:] = values.astype(BF16)


def project(place, blocks, attn_gain, w_query, w_key, w_value, q_gain, k_gain, cos, sin):
    tokens, w = blocks[0].shape
    heads = w_query.shape[1] // HD
    whole = lambda shape: pl.BlockSpec(shape, lambda i, s: tuple(0 for _ in shape))
    column = lambda shape: pl.BlockSpec((shape[0], HD), lambda i, s: (0, s[1]))
    return pl.pallas_call(
        qkv_kernel,
        grid_spec=pltpu.PrefetchScalarGridSpec(
            num_scalar_prefetch=1,
            grid=(1,),
            in_specs=[whole((tokens, w))] * 8
            + [
                whole((8, w)),
                whole(w_query.shape),
                column(w_key.shape),
                column(w_value.shape),
                whole((1, heads * HD)),
                column((1, HD)),
                whole((tokens, HD)),
                whole((tokens, HD)),
            ],
            out_specs=[whole((heads, tokens, HD)), whole((tokens // 2, 2 * HD))],
            scratch_shapes=[VMEM((tokens, 8 * w), BF16)],
        ),
        out_shape=[
            jax.ShapeDtypeStruct((heads, tokens, HD), BF16),
            jax.ShapeDtypeStruct((tokens // 2, 2 * HD), BF16),
        ],
        compiler_params=pltpu.CompilerParams(vmem_limit_bytes=48 * 1024 * 1024),
        name="project_qkv",
    )(
        place,
        *blocks,
        attn_gain.reshape(8, w),
        w_query,
        w_key,
        w_value,
        q_gain.reshape(1, -1),
        k_gain.reshape(1, -1),
        cos,
        sin,
    )


def attend_kernel(place_ref, q_ref, kv_ref, o_ref):
    ctx = place_ref[0]
    core = place_ref[2]
    tokens = q_ref.shape[1]
    shard = kv_ref.shape[1]
    group = 4
    span = group * shard
    q = q_ref[0]

    def fold(carry, chunk, masked):
        highest, totals, weighted = carry
        piece = kv_ref[pl.ds(chunk * group, group)].reshape(span, 2 * HD)
        scores = dot_t(q, piece[:, :HD])
        if masked:
            t = iota((tokens, span), 1)
            key_pos = (chunk * group + t // shard) * (2 * shard) + core * shard + t % shard
            query_pos = ctx * tokens + iota((tokens, span), 0)
            scores = jnp.where(query_pos >= key_pos, scores, NEG)
        fresh = jnp.maximum(highest, jnp.max(scores, 1, keepdims=True))
        weights = jnp.exp2(scores - fresh)
        if masked:
            weights = jnp.where(query_pos >= key_pos, weights, 0.0)
        fade = jnp.exp2(highest - fresh)
        totals = totals * fade + jnp.sum(weights, 1, keepdims=True)
        weighted = weighted * fade + dot(weights.astype(BF16), piece[:, HD:])
        return fresh, totals, weighted

    start = (jnp.full((tokens, 1), NEG, F32), jnp.zeros((tokens, 1), F32), jnp.zeros((tokens, HD), F32))
    whole = ctx // group
    state = lax.fori_loop(0, whole, lambda j, carry: fold(carry, j, False), start)
    highest, totals, weighted = fold(state, whole, True)
    o_ref[0, :, :HD] = weighted
    lane = iota((tokens, HD), 1)
    o_ref[0, :, HD:] = jnp.where(lane < HD // 2, highest, totals)


def attend(place, queries, kv):
    heads, tokens, _ = queries.shape
    return pl.pallas_call(
        attend_kernel,
        grid_spec=pltpu.PrefetchScalarGridSpec(
            num_scalar_prefetch=1,
            grid=(heads,),
            in_specs=[
                pl.BlockSpec((1, tokens, HD), lambda i, s: (i, 0, 0)),
                pl.BlockSpec(kv.shape, lambda i, s: (0, 0, 0)),
            ],
            out_specs=pl.BlockSpec((1, tokens, 2 * HD), lambda i, s: (i, 0, 0)),
        ),
        out_shape=jax.ShapeDtypeStruct((heads, tokens, 2 * HD), F32),
        compiler_params=pltpu.CompilerParams(vmem_limit_bytes=48 * 1024 * 1024),
        name="attend",
    )(place, queries, kv)


def output_kernel(place_ref, own_ref, other_ref, w_ref, o_ref, att_s):
    @pl.when(pl.program_id(0) == 0)
    def _():
        for h in range(own_ref.shape[0]):
            m0 = own_ref[h, :, HD : HD + 1]
            m1 = other_ref[h, :, HD : HD + 1]
            top = jnp.maximum(m0, m1)
            e0 = jnp.exp2(m0 - top)
            e1 = jnp.exp2(m1 - top)
            total = own_ref[h, :, 2 * HD - 1 :] * e0 + other_ref[h, :, 2 * HD - 1 :] * e1
            value = (own_ref[h, :, :HD] * e0 + other_ref[h, :, :HD] * e1) / total
            att_s[:, h * HD : (h + 1) * HD] = value.astype(BF16)

    o_ref[0] = dot(att_s[...], w_ref[...]).astype(BF16)


def project_out(place, own, other, w_out):
    heads, tokens, _ = own.shape
    w = w_out.shape[1] // 8
    whole = pl.BlockSpec((heads, tokens, 2 * HD), lambda i, s: (0, 0, 0))
    return pl.pallas_call(
        output_kernel,
        grid_spec=pltpu.PrefetchScalarGridSpec(
            num_scalar_prefetch=1,
            grid=(8,),
            in_specs=[
                whole,
                whole,
                pl.BlockSpec((heads * HD, w), lambda i, s: (0, 2 * (i % 4) + jnp.where(i < 4, 1 - s[2], s[2]))),
            ],
            out_specs=pl.BlockSpec((1, tokens, w), lambda i, s: (i, 0, 0)),
            scratch_shapes=[VMEM((tokens, heads * HD), BF16)],
        ),
        out_shape=jax.ShapeDtypeStruct((8, tokens, w), BF16),
        compiler_params=pltpu.CompilerParams(vmem_limit_bytes=48 * 1024 * 1024),
        name="project_out",
    )(place, own, other, w_out)


def body(
    branch_rows,
    expert_ids,
    targets,
    router,
    w_gate,
    w_up,
    w_down,
    stream,
    attn_gain,
    q_gain,
    k_gain,
    w_query,
    w_key,
    w_value,
    w_out,
):
    ctx = lax.axis_index("ctx")
    head = lax.axis_index("head")
    z = head // 2
    core = head % 2
    place = jnp.stack([ctx, z, core]).astype(jnp.int32)
    experts = router.shape[1]
    tokens, w = stream.shape
    partner = [(i, i ^ 1) for i in range(8)]

    def along(shard, hops):
        return lax.ppermute(shard, "head", [(i, (i + 2 * hops) % 8) for i in range(8)])

    def everywhere(blocks):
        return lax.all_to_all(blocks, ("ctx", "head"), split_axis=0, concat_axis=0, tiled=True)

    outgoing, rank, gate, spot = dispatch(branch_rows, expert_ids, targets, router)
    shape = (experts, 8, outgoing.shape[1])
    arrived = everywhere(outgoing.reshape(shape)).reshape(outgoing.shape)
    produced = run_expert(arrived, w_gate[0], w_up[0], w_down[0])
    returned = everywhere(produced.reshape(shape)).reshape(outgoing.shape)
    parcels = combine(returned, rank, gate, spot)
    landed = everywhere(parcels.reshape(experts, 8, parcels.shape[3])).reshape(experts * 8, parcels.shape[3])
    joined = join(landed, stream)

    mine = [joined] + [along(joined, hops) for hops in (1, 2, 3)]
    blocks = mine + [lax.ppermute(block, "head", partner) for block in mine]

    half_dim = HD // 2
    frequency = jnp.power(jnp.float32(THETA), -jnp.arange(half_dim, dtype=F32) * 2.0 / HD)
    positions = ctx * tokens + jnp.arange(tokens, dtype=jnp.int32)
    angles = positions.astype(F32)[:, None] * frequency[None, :]
    cosines = jnp.cos(angles)
    sines = jnp.sin(angles)
    cos = jnp.concatenate([cosines, cosines], 1)
    sin = jnp.concatenate([-sines, sines], 1)

    queries, kv = project(place, blocks, attn_gain, w_query, w_key, w_value, q_gain, k_gain, cos, sin)
    all_kv = lax.all_to_all(
        jnp.broadcast_to(kv[None], (16, *kv.shape)), "ctx", split_axis=0, concat_axis=0, tiled=True
    )
    other_queries = lax.ppermute(queries, "head", partner)
    folded = attend(place, jnp.concatenate([queries, other_queries], 0), all_kv)
    heads = queries.shape[0]
    from_partner = lax.ppermute(folded[heads:], "head", partner)
    out = project_out(place, folded[:heads], from_partner, w_out)
    pair = out[4:].astype(F32) + lax.ppermute(out[:4], "head", partner).astype(F32)
    pair = pair.astype(BF16)
    total = lax.dynamic_index_in_dim(pair, z, 0, keepdims=False).astype(F32)
    for hops in (1, 2, 3):
        sent = lax.dynamic_index_in_dim(pair, (z + hops) % 4, 0, keepdims=False)
        total = total + along(sent, hops).astype(F32)
    return (joined.astype(F32) + total).astype(BF16)


def solution(mesh):
    in_specs = (
        P(("ctx", "head"), None),
        P(("ctx", "head"), None),
        P(("ctx", "head")),
        P(),
        P(("ctx", "head"), None, None),
        P(("ctx", "head"), None, None),
        P(("ctx", "head"), None, None),
        P("ctx", "head"),
        P(),
        P("head"),
        P(),
        P(None, "head"),
        P(),
        P(),
        P("head", None),
    )
    out_specs = P("ctx", "head")
    return jax.shard_map(body, mesh=mesh, in_specs=in_specs, out_specs=out_specs, check_vma=False)
```

time: 577 us -> 365 us (0.63)
  the two profiles are of different devices: /device:TPU:1 before, /device:TPU:24 now
where the time goes in v1:
time: 365 us
  blocking collectives  186 us (51%)
  Pallas kernels  83.7 us (23%)
  waiting for transfers between devices  61.4 us (17%)
  starting transfers between devices  14.3 us (4%)
  local copies, waits for them, and re-layouts  12.5 us (3%)
  other arithmetic  6.78 us (2%)
    all_to_all x3, blocking collectives, everywhere(): lax.all_to_all(blocks, ('ctx', 'head'), split_axis=0, concat_axis=0, tile...  186 us
    pallas_call x1, Pallas kernels, attend(): pl.pallas_call(attend_kernel, grid_spec=pltpu.PrefetchScalarGridSpec(num_...  37.5 us
    all_to_all x1, waiting for transfers between devices, body(): lax.all_to_all(jnp.broadcast_to(kv[None], (16, *kv.shape)), 'ctx', split_...  29.8 us
    ppermute x6, waiting for transfers between devices, along(): lax.ppermute(shard, 'head', [(i, (i + 2 * hops) % 8) for i in range(8)])  23 us
    pallas_call x1, Pallas kernels, run_expert(): pl.pallas_call(expert_kernel, grid=(steps,), in_specs=[tile, whole(w_gate...  22.7 us
    pallas_call x1, Pallas kernels, project_out(): pl.pallas_call(output_kernel, grid_spec=pltpu.PrefetchScalarGridSpec(num_...  8.18 us
    ppermute x6, starting transfers between devices, along(): lax.ppermute(shard, 'head', [(i, (i + 2 * hops) % 8) for i in range(8)])  7.41 us
    unnamed x30, local copies, waits for them, and re-layouts  7.4 us
  transfers between devices with their start and end apart: 14, of which 8 were waited for; matrix products, arithmetic and copies ran while one was open for 1% of the time, Pallas kernels for 0%

profile of v1, /device:TPU:24, one launch (start us, length us, event | category | flops | bytes accessed | tf_op | source)
XLA Modules:
  0.0 364.5 jit_solution(17751285700347931813)
XLA Ops:
  4.2 4.2 %dispatch_rows.1 = (bf16[1024,3072]{1,0:T(8,128)(2,1)S(1)}, f32[128,128]{1,0:T(8,128)S(1)}, f32[128,128]{1,0:T(8,128)S(1)}, f32[128,128]{1,0:T(8,128)S(1)}) custom-call(bf16[128,2048]{1,0:T(8,128)(2,1)S(1)} %copy-done.1, s32[8,128]{1,0:T(8,128)S(1)} %bitcast.31, s32[1,128]{1,0:T(1,128)S(1)} %bitcast.35, s32[128,1]{1,0:T(8,128)S(1)} %copy.16.tcol_ref, ...), custom_call_target="tpu_custom_call" | custom-call | tf_op jit(solution)/shard_map/dispatch_rows/pallas_call | solution.py:83
  8.4 84.4 %all_to_all.20 = bf16[128,8,3072]{2,1,0:T(8,128)(2,1)} all-to-all(bf16[128,8,3072]{2,1,0:T(8,128)(2,1)S(1)} %bitcast.28), channel_id=1, replica_groups=mesh['ctx'=16,'head'=8] {'ctx','head'}, dimensions={0} | all-to-all | bytes 12582912 | tf_op jit(solution)/shard_map/all_to_all | solution.py:442
  92.8 22.7 %expert_ffn.1 = bf16[1024,3072]{1,0:T(8,128)(2,1)} custom-call(bf16[1024,3072]{1,0:T(8,128)(2,1)} %bitcast.36, bf16[2048,768]{1,0:T(8,128)(2,1)} %bitcast.38, bf16[2048,768]{1,0:T(8,128)(2,1)} %bitcast.39, bf16[768,2048]{1,0:T(8,128)(2,1)} %bitcast.40), custom_call_target="tpu_custom_call" | custom-call | tf_op jit(solution)/shard_map/expert_ffn/pallas_call | solution.py:140
  115.5 80.3 %all_to_all.21 = bf16[128,8,3072]{2,1,0:T(8,128)(2,1)S(1)} all-to-all(bf16[128,8,3072]{2,1,0:T(8,128)(2,1)} %bitcast.37), channel_id=1, replica_groups=mesh['ctx'=16,'head'=8] {'ctx','head'}, dimensions={0} | all-to-all | bytes 12582912 | tf_op jit(solution)/shard_map/all_to_all | solution.py:442
  195.8 4.2 %combine_rows.1 = bf16[16,8,8,384]{3,2,1,0:T(8,128)(2,1)S(1)} custom-call(bf16[1024,3072]{1,0:T(8,128)(2,1)S(1)} %bitcast.26, bf16[1024,3072]{1,0:T(8,128)(2,1)S(1)} %bitcast.27, f32[128,128]{1,0:T(8,128)S(1)} %get-tuple-element.12.rank_ref, f32[128,128]{1,0:T(8,128)S(1)} %get-tuple-element.13.gate_ref, f32[128,128]{1,0:T(8,128)S(1)} %get-tuple-element.14.spot_ref), custom_call_target="tpu_custom_call" | custom-call | tf_op jit(solution)/shard_map/combine_rows/pallas_call | solution.py:197
  200.1 20.8 %all_to_all.22 = bf16[128,8,384]{2,1,0:T(8,128)(2,1)S(1)} all-to-all(bf16[128,8,384]{2,1,0:T(8,128)(2,1)S(1)} %bitcast.29), channel_id=1, replica_groups=mesh['ctx'=16,'head'=8] {'ctx','head'}, dimensions={0} | all-to-all | bytes 1572864 | tf_op jit(solution)/shard_map/all_to_all | solution.py:442
  221.8 1.6 collective-permute-start.1
  223.3 1.7 collective-permute-start.2
  225.1 11.0 %collective-permute-done.refs_1_ = bf16[512,256]{1,0:T(8,128)(2,1)S(1)} collective-permute-done((bf16[512,256]{1,0:T(8,128)(2,1)S(1)}, bf16[512,256]{1,0:T(8,128)(2,1)S(1)}, u32[]{:S(2)}, u32[]{:S(2)}) %collective-permute-start) | collective-permute-done | bytes 262176 | tf_op jit(solution)/shard_map/ppermute | solution.py:439
  236.9 1.8 fusion.4
  242.9 6.1 %project_qkv.1 = (bf16[4,512,128]{2,1,0:T(8,128)(2,1)S(1)}, bf16[256,256]{1,0:T(8,128)(2,1)S(1)}) custom-call(s32[3]{0:T(128)S(1)} %pad_add_fusion.place_ref, bf16[512,256]{1,0:T(8,128)(2,1)S(1)} %join_rows.1.refs_0_, bf16[512,256]{1,0:T(8,128)(2,1)S(1)} %collective-permute-done.refs_1_, bf16[512,256]{1,0:T(8,128)(2,1)S(1)} %collective-permute-done.1.refs_2_, ...), custom_call_target="tpu_custom_call" | custom-call | tf_op jit(solution)/shard_map/project_qkv/pallas_call | solution.py:279
  249.0 1.6 broadcast_in_dim.2
  250.5 5.7 %all-to-all-start.3 = ((bf16[16,256,256]{2,1,0:T(8,128)(2,1)}), bf16[16,256,256]{2,1,0:T(8,128)(2,1)S(1)}, u32[]{:S(2)}, u32[]{:S(2)}) async-start(bf16[16,256,256]{2,1,0:T(8,128)(2,1)} %broadcast_in_dim.2), calls=%async_computation.3 | async-start | bytes 4194304 | tf_op jit(solution)/shard_map/all_to_all | solution.py:466
  256.4 1.9 collective-permute-done.7
  259.4 29.8 %all-to-all-done.3.kv_ref = bf16[16,256,256]{2,1,0:T(8,128)(2,1)S(1)} async-done(((bf16[16,256,256]{2,1,0:T(8,128)(2,1)}), bf16[16,256,256]{2,1,0:T(8,128)(2,1)S(1)}, u32[]{:S(2)}, u32[]{:S(2)}) %all-to-all-start.3) | async-done | bytes 2097184 | tf_op jit(solution)/shard_map/all_to_all | solution.py:466
  289.2 37.5 %attend.1 = f32[8,512,256]{2,1,0:T(8,128)} custom-call(s32[3]{0:T(128)S(1)} %pad_add_fusion.place_ref, bf16[8,512,128]{2,1,0:T(8,128)(2,1)S(1)} %pad_maximum_fusion.q_ref, bf16[16,256,256]{2,1,0:T(8,128)(2,1)S(1)} %all-to-all-done.3.kv_ref), custom_call_target="tpu_custom_call" | custom-call | tf_op jit(solution)/shard_map/attend/pallas_call | solution.py:356
  326.7 2.6 fusion.5
  329.4 4.1 %collective-permute-done.8.other_ref = f32[4,512,256]{2,1,0:T(8,128)S(1)} collective-permute-done((f32[4,512,256]{2,1,0:T(8,128)S(1)}, f32[4,512,256]{2,1,0:T(8,128)S(1)}, u32[]{:S(2)}, u32[]{:S(2)}) %collective-permute-start.8) | collective-permute-done | bytes 2097184 | tf_op jit(solution)/shard_map/ppermute | solution.py:472
  334.9 8.2 %project_out.1 = bf16[8,512,256]{2,1,0:T(8,128)(2,1)S(1)} custom-call(s32[3]{0:T(128)S(1)} %pad_add_fusion.place_ref, f32[4,512,256]{2,1,0:T(8,128)S(1)} %get-tuple-element.18.own_ref, f32[4,512,256]{2,1,0:T(8,128)} %copy-done.13, bf16[512,2048]{1,0:T(8,128)(2,1)} %w_ref.1), custom_call_target="tpu_custom_call" | custom-call | tf_op jit(solution)/shard_map/project_out/pallas_call | solution.py:393
  343.4 2.6 collective-permute-done.9
  346.1 1.5 add_convert_fusion
  347.8 3.9 %collective-permute-start.11 = (bf16[512,256]{1,0:T(8,128)(2,1)S(1)}, bf16[512,256]{1,0:T(8,128)(2,1)S(1)}, u32[]{:S(2)}, u32[]{:S(2)}) collective-permute-start(bf16[512,256]{1,0:T(8,128)(2,1)S(1)} %get-tuple-element.21), channel_id=1, source_target_pairs={{0,4},{1,5},{2,6},{3,7},{4,0},{5,1},{6,2},{7,3},{8,12},{9,13},{10,... | collective-permute-start | bytes 786440 | tf_op jit(solution)/shard_map/ppermute | solution.py:439
  351.7 5.5 %collective-permute-done.10 = bf16[512,256]{1,0:T(8,128)(2,1)S(1)} collective-permute-done((bf16[512,256]{1,0:T(8,128)(2,1)S(1)}, bf16[512,256]{1,0:T(8,128)(2,1)S(1)}, u32[]{:S(2)}, u32[]{:S(2)}) %collective-permute-start.10) | collective-permute-done | bytes 262176 | tf_op jit(solution)/shard_map/ppermute | solution.py:439
  357.2 6.4 %collective-permute-done.11 = bf16[512,256]{1,0:T(8,128)(2,1)S(1)} collective-permute-done((bf16[512,256]{1,0:T(8,128)(2,1)S(1)}, bf16[512,256]{1,0:T(8,128)(2,1)S(1)}, u32[]{:S(2)}, u32[]{:S(2)}) %collective-permute-start.11) | collective-permute-done | bytes 262176 | tf_op jit(solution)/shard_map/ppermute | solution.py:439
  (58 shorter events, 14.1 us)
Async XLA Ops:
  0.8 1.0 copy-start.1
  1.8 1.0 copy-start.2
  195.8 25.1 %copy-start.4 = (bf16[512,256]{1,0:T(8,128)(2,1)S(1)}, bf16[512,256]{1,0:T(8,128)(2,1)}, u32[]{:S(2)}) copy-start(bf16[512,256]{1,0:T(8,128)(2,1)} %stream_ref.1) | copy-start | bytes 786436
  200.1 38.6 %copy-start.14 = (f32[2048]{0:T(1024)S(1)}, f32[2048]{0:T(1024)}, u32[]{:S(2)}) copy-start(f32[2048]{0:T(1024)} %param.23) | copy-start | bytes 24580
  220.9 20.0 %copy-start = (bf16[2048,512]{1,0:T(8,128)(2,1)S(1)}, bf16[2048,512]{1,0:T(8,128)(2,1)}, u32[]{:S(2)}) copy-start(bf16[2048,512]{1,0:T(8,128)(2,1)} %refs_9_.1) | copy-start | bytes 6291460
  220.9 20.0 %copy-start.10 = (f32[512]{0:T(512)S(1)}, f32[512]{0:T(512)}, u32[]{:S(2)}) copy-start(f32[512]{0:T(512)} %param.24) | copy-start | bytes 6148
  220.9 20.0 %copy-start.11 = (f32[512]{0:T(512)S(1)}, f32[512]{0:T(512)}, u32[]{:S(2)}) copy-start(f32[512]{0:T(512)} %param.25) | copy-start | bytes 6148
  221.7 14.4 %collective-permute-start = (bf16[512,256]{1,0:T(8,128)(2,1)S(1)}, bf16[512,256]{1,0:T(8,128)(2,1)S(1)}, u32[]{:S(2)}, u32[]{:S(2)}) collective-permute-start(bf16[512,256]{1,0:T(8,128)(2,1)S(1)} %join_rows.1.refs_0_), channel_id=1, source_target_pairs={{0,2},{1,3},{2,4},{3,5},{4,6},{5,7},{6,0},{7,1},{8,10},{9,11},{10,... | collective-permute-start | bytes 786440 | tf_op jit(solution)/shard_map/ppermute | solution.py:439
  221.8 14.3 %collective-permute-start.1 = (bf16[512,256]{1,0:T(8,128)(2,1)S(1)}, bf16[512,256]{1,0:T(8,128)(2,1)S(1)}, u32[]{:S(2)}, u32[]{:S(2)}) collective-permute-start(bf16[512,256]{1,0:T(8,128)(2,1)S(1)} %join_rows.1.refs_0_), channel_id=1, source_target_pairs={{0,4},{1,5},{2,6},{3,7},{4,0},{5,1},{6,2},{7,3},{8,12},{9,13},{10,... | collective-permute-start | bytes 786440 | tf_op jit(solution)/shard_map/ppermute | solution.py:439
  223.3 13.4 %collective-permute-start.2 = (bf16[512,256]{1,0:T(8,128)(2,1)S(1)}, bf16[512,256]{1,0:T(8,128)(2,1)S(1)}, u32[]{:S(2)}, u32[]{:S(2)}) collective-permute-start(bf16[512,256]{1,0:T(8,128)(2,1)S(1)} %join_rows.1.refs_0_), channel_id=1, source_target_pairs={{0,6},{1,7},{2,0},{3,1},{4,2},{5,3},{6,4},{7,5},{8,14},{9,15},{10,... | collective-permute-start | bytes 786440 | tf_op jit(solution)/shard_map/ppermute | solution.py:439
  225.0 15.2 %collective-permute-start.3 = (bf16[512,256]{1,0:T(8,128)(2,1)S(1)}, bf16[512,256]{1,0:T(8,128)(2,1)S(1)}, u32[]{:S(2)}, u32[]{:S(2)}) collective-permute-start(bf16[512,256]{1,0:T(8,128)(2,1)S(1)} %join_rows.1.refs_0_), channel_id=1, source_target_pairs={{0,1},{1,0},{2,3},{3,2},{4,5},{5,4},{6,7},{7,6},{8,9},{9,8},{10,11... | collective-permute-start | bytes 786440 | tf_op jit(solution)/shard_map/ppermute | solution.py:454
  236.1 4.8 %collective-permute-start.4 = (bf16[512,256]{1,0:T(8,128)(2,1)S(1)}, bf16[512,256]{1,0:T(8,128)(2,1)}, u32[]{:S(2)}, u32[]{:S(2)}) collective-permute-start(bf16[512,256]{1,0:T(8,128)(2,1)S(1)} %collective-permute-done.refs_1_), channel_id=1, source_target_pairs={{0,1},{1,0},{2,3},{3,2},{4,5},{5,4},{6,7},{7,6},{8,9},{9,8},{10,11... | collective-permute-start | bytes 786440 | tf_op jit(solution)/shard_map/ppermute | solution.py:454
  236.1 4.8 %collective-permute-start.5 = (bf16[512,256]{1,0:T(8,128)(2,1)S(1)}, bf16[512,256]{1,0:T(8,128)(2,1)}, u32[]{:S(2)}, u32[]{:S(2)}) collective-permute-start(bf16[512,256]{1,0:T(8,128)(2,1)S(1)} %collective-permute-done.1.refs_2_), channel_id=1, source_target_pairs={{0,1},{1,0},{2,3},{3,2},{4,5},{5,4},{6,7},{7,6},{8,9},{9,8},{10,11... | collective-permute-start | bytes 786440 | tf_op jit(solution)/shard_map/ppermute | solution.py:454
  236.7 4.2 %copy-start.5 = (bf16[512,256]{1,0:T(8,128)(2,1)}, bf16[512,256]{1,0:T(8,128)(2,1)S(1)}, u32[]{:S(2)}) copy-start(bf16[512,256]{1,0:T(8,128)(2,1)S(1)} %collective-permute-done.2.refs_3_) | copy-start | bytes 786436
  236.7 4.2 %collective-permute-start.6 = (bf16[512,256]{1,0:T(8,128)(2,1)S(1)}, bf16[512,256]{1,0:T(8,128)(2,1)}, u32[]{:S(2)}, u32[]{:S(2)}) collective-permute-start(bf16[512,256]{1,0:T(8,128)(2,1)S(1)} %collective-permute-done.2.refs_3_), channel_id=1, source_target_pairs={{0,1},{1,0},{2,3},{3,2},{4,5},{5,4},{6,7},{7,6},{8,9},{9,8},{10,11... | collective-permute-start | bytes 786440 | tf_op jit(solution)/shard_map/ppermute | solution.py:454
  249.0 7.3 %copy-start.3 = (bf16[4,512,128]{2,1,0:T(8,128)(2,1)}, bf16[4,512,128]{2,1,0:T(8,128)(2,1)S(1)}, u32[]{:S(2)}) copy-start(bf16[4,512,128]{2,1,0:T(8,128)(2,1)S(1)} %get-tuple-element.15) | copy-start | bytes 1572868
  250.5 38.6 %all-to-all-start.3 = ((bf16[16,256,256]{2,1,0:T(8,128)(2,1)}), bf16[16,256,256]{2,1,0:T(8,128)(2,1)S(1)}, u32[]{:S(2)}, u32[]{:S(2)}) async-start(bf16[16,256,256]{2,1,0:T(8,128)(2,1)} %broadcast_in_dim.2), calls=%async_computation.3 | async-start | bytes 4194304 | tf_op jit(solution)/shard_map/all_to_all | solution.py:466
  256.3 2.0 collective-permute-start.7
  329.3 4.2 %collective-permute-start.8 = (f32[4,512,256]{2,1,0:T(8,128)S(1)}, f32[4,512,256]{2,1,0:T(8,128)S(1)}, u32[]{:S(2)}, u32[]{:S(2)}) collective-permute-start(f32[4,512,256]{2,1,0:T(8,128)S(1)} %get-tuple-element.17), channel_id=1, source_target_pairs={{0,1},{1,0},{2,3},{3,2},{4,5},{5,4},{6,7},{7,6},{8,9},{9,8},{10,11... | collective-permute-start | bytes 6291464 | tf_op jit(solution)/shard_map/ppermute | solution.py:472
  333.6 1.3 copy-start.13
  343.2 2.9 collective-permute-start.9
  347.6 9.6 %collective-permute-start.10 = (bf16[512,256]{1,0:T(8,128)(2,1)S(1)}, bf16[512,256]{1,0:T(8,128)(2,1)S(1)}, u32[]{:S(2)}, u32[]{:S(2)}) collective-permute-start(bf16[512,256]{1,0:T(8,128)(2,1)S(1)} %get-tuple-element.19), channel_id=1, source_target_pairs={{0,2},{1,3},{2,4},{3,5},{4,6},{5,7},{6,0},{7,1},{8,10},{9,11},{10,... | collective-permute-start | bytes 786440 | tf_op jit(solution)/shard_map/ppermute | solution.py:439
  347.8 15.9 %collective-permute-start.11 = (bf16[512,256]{1,0:T(8,128)(2,1)S(1)}, bf16[512,256]{1,0:T(8,128)(2,1)S(1)}, u32[]{:S(2)}, u32[]{:S(2)}) collective-permute-start(bf16[512,256]{1,0:T(8,128)(2,1)S(1)} %get-tuple-element.21), channel_id=1, source_target_pairs={{0,4},{1,5},{2,6},{3,7},{4,0},{5,1},{6,2},{7,3},{8,12},{9,13},{10,... | collective-permute-start | bytes 786440 | tf_op jit(solution)/shard_map/ppermute | solution.py:439
  351.7 11.9 %collective-permute-start.12 = (bf16[512,256]{1,0:T(8,128)(2,1)S(1)}, bf16[512,256]{1,0:T(8,128)(2,1)S(1)}, u32[]{:S(2)}, u32[]{:S(2)}) collective-permute-start(bf16[512,256]{1,0:T(8,128)(2,1)S(1)} %get-tuple-element.20), channel_id=1, source_target_pairs={{0,6},{1,7},{2,0},{3,1},{4,2},{5,3},{6,4},{7,5},{8,14},{9,15},{10,... | collective-permute-start | bytes 786440 | tf_op jit(solution)/shard_map/ppermute | solution.py:439
  (5 other events, 4.0 us)

commit v2 on v1

v2 whole, which is shorter than its diff:
```python
import math

import jax
import jax.numpy as jnp
from jax import lax
from jax.experimental import pallas as pl
from jax.experimental.pallas import tpu as pltpu
from jax.sharding import PartitionSpec as P

QH = 32
KVH = 4
HD = 128
EPSILON = 1e-06
THETA = 1000000.0
F32 = jnp.float32
BF16 = jnp.bfloat16
VMEM = pltpu.VMEM
NEG = -1e30
MIB = 1024 * 1024


def iota(shape, dim):
    return lax.broadcasted_iota(jnp.int32, shape, dim)


def dot(a, b):
    return jnp.dot(a, b, preferred_element_type=F32)


def dot_t(a, b):
    return lax.dot_general(a, b, (((1,), (1,)), ((), ())), preferred_element_type=F32)


def dispatch_kernel(rows_ref, ids_ref, targets_ref, router_ref, y_ref, rank_ref, gate_ref, spot_ref):
    n, width = rows_ref.shape
    experts = router_ref.shape[1]
    first = iota((n, n), 0)
    second = iota((n, n), 1)
    owner = jnp.broadcast_to((targets_ref[...] // 512).astype(F32), (n, n))
    same = jnp.where((owner.T == owner) & (first < second), 1.0, 0.0)
    place = owner[0:1] * 8.0 + jnp.sum(same, 0, keepdims=True)
    perm = jnp.where(first.astype(F32) == place, 1.0, 0.0)
    spot = (targets_ref[...] % 512).astype(F32)
    spot_ref[...] = jnp.broadcast_to(jnp.sum(perm * spot, 1, keepdims=True), (n, 128))
    perm = perm.astype(BF16)
    rows = dot(perm, rows_ref[...]).astype(BF16)
    ids = dot_t(ids_ref[...].astype(F32).astype(BF16), perm)
    expert = iota((experts, n), 0).astype(F32)
    member = jnp.zeros((experts, n), F32)
    for k in range(ids.shape[0]):
        member = member + jnp.where(expert == ids[k : k + 1, :], 1.0, 0.0)
    before = jnp.where(first < second, 1.0, 0.0).astype(BF16)
    rank = jnp.where(member > 0.5, dot(member.astype(BF16), before), -1.0)
    half = width // 2
    blk = 32
    packed = rank.astype(BF16)
    for i in range(experts // blk):
        spread = jnp.where(iota((blk * 8, experts), 0) // 8 + i * blk == iota((blk * 8, experts), 1), 1.0, 0.0)
        rank_e = dot(spread.astype(BF16), packed)
        slot = (iota(rank_e.shape, 0) % 8).astype(F32)
        main = jnp.where(rank_e == slot, 1.0, 0.0).astype(BF16)
        low = jnp.where((rank_e == slot + 8.0) & (slot < 4.0), 1.0, 0.0).astype(BF16)
        high = jnp.where((rank_e == slot + 4.0) & (slot >= 4.0), 1.0, 0.0).astype(BF16)
        lines = slice(i * blk * 8, (i + 1) * blk * 8)
        y_ref[lines, :width] = dot(main, rows).astype(BF16)
        y_ref[lines, width:] = (dot(low, rows[:, :half]) + dot(high, rows[:, half:])).astype(BF16)
    rank_ref[...] = rank.T
    member_q = member.T > 0.5
    logits = dot(rows, router_ref[...])
    highest = jnp.max(jnp.where(member_q, logits, NEG), 1, keepdims=True)
    raised = jnp.where(member_q, jnp.exp(jnp.minimum(logits - highest, 0.0)), 0.0)
    gate_ref[...] = raised / jnp.sum(raised, 1, keepdims=True)


def dispatch(rows, ids, targets, router):
    n, width = rows.shape
    table = jax.ShapeDtypeStruct((n, 128), F32)
    return pl.pallas_call(
        dispatch_kernel,
        out_shape=[jax.ShapeDtypeStruct((1024, width * 3 // 2), BF16), table, table, table],
        compiler_params=pltpu.CompilerParams(vmem_limit_bytes=16 * MIB),
        name="dispatch_rows",
    )(rows, ids.T, targets.reshape(1, n), router)


def expert_kernel(y_ref, wg_ref, wu_ref, wd_ref, o_ref):
    rows = 256
    half_rows = rows // 2
    width = wg_ref.shape[0]
    half = width // 2
    r = iota((half_rows, rows), 0)
    col = iota((half_rows, rows), 1)
    source = r // 4 * 8 + r % 4
    low = jnp.where(col == source, 1.0, 0.0).astype(BF16)
    high = jnp.where(col == source + 4, 1.0, 0.0).astype(BF16)
    rt = iota((rows, half_rows), 0)
    ct = iota((rows, half_rows), 1)
    target = ct // 4 * 8 + ct % 4
    low_t = jnp.where(rt == target, 1.0, 0.0).astype(BF16)
    high_t = jnp.where(rt == target + 4, 1.0, 0.0).astype(BF16)
    for i in range(y_ref.shape[0] // rows):
        lines = slice(i * rows, (i + 1) * rows)
        extra = y_ref[lines, width:]
        inputs = jnp.concatenate(
            [
                y_ref[lines, :width],
                jnp.concatenate([dot(low, extra).astype(BF16), dot(high, extra).astype(BF16)], 1),
            ],
            0,
        )
        gate_part = dot(inputs, wg_ref[...])
        upward = dot(inputs, wu_ref[...])
        hidden = (gate_part / (1.0 + jnp.exp(-gate_part)) * upward).astype(BF16)
        produced = dot(hidden, wd_ref[...]).astype(BF16)
        o_ref[lines, :width] = produced[:rows]
        o_ref[lines, width:] = (dot(low_t, produced[rows:, :half]) + dot(high_t, produced[rows:, half:])).astype(BF16)


def run_expert(y, w_gate, w_up, w_down):
    return pl.pallas_call(
        expert_kernel,
        out_shape=jax.ShapeDtypeStruct(y.shape, BF16),
        compiler_params=pltpu.CompilerParams(vmem_limit_bytes=16 * MIB),
        name="expert_ffn",
    )(y, w_gate, w_up, w_down)


def combine_kernel(r_ref, rank_ref, gate_ref, spot_ref, o_ref):
    n, experts = rank_ref.shape
    rows = r_ref.shape[0]
    width = r_ref.shape[1] * 2 // 3
    spread = jnp.where(iota((experts, rows), 0) == iota((experts, rows), 1) // 8, 1.0, 0.0).astype(BF16)
    gate = gate_ref[...]
    gate_hi = gate.astype(BF16)
    gate_lo = (gate - gate_hi.astype(F32)).astype(BF16)
    rank_e = dot(rank_ref[...].astype(BF16), spread)
    slot = (iota(rank_e.shape, 1) % 8).astype(F32)
    gates = [dot(gate_hi, spread), dot(gate_lo, spread)]

    def chosen(mask):
        return jnp.concatenate([jnp.where(mask, g, 0.0).astype(BF16) for g in gates], 0)

    main = chosen(rank_e == slot)
    extras = [chosen((rank_e == slot + 8.0) & (slot < 4.0)), chosen((rank_e == slot + 4.0) & (slot >= 4.0))]
    spot = spot_ref[...]
    lane = iota(spot.shape, 1)
    big = jnp.floor(spot * (1.0 / 16.0))
    tail = jnp.where(lane == 0, big, jnp.where(lane == 1, spot - 16.0 * big, 0.0))
    tail = tail.reshape(n // 8, 8, 128).astype(BF16)
    parts = o_ref.shape[1]
    w = width // parts
    span = width // 4
    for c in range(4):
        lines = slice(c * span, (c + 1) * span)
        more = width + (c % 2) * span
        merged = dot(main, r_ref[:, lines]) + dot(extras[c // 2], r_ref[:, more : more + span])
        merged = merged[:n] + merged[n:]
        for i in range(span // w):
            o_ref[:, c * (span // w) + i, :, :w] = merged[:, i * w : (i + 1) * w].reshape(n // 8, 8, w).astype(BF16)
    for h in range(parts):
        o_ref[:, h, :, w:] = tail


def combine(r, rank, gate, spot):
    n = rank.shape[0]
    width = r.shape[1] * 2 // 3
    return pl.pallas_call(
        combine_kernel,
        out_shape=jax.ShapeDtypeStruct((n // 8, 8, 8, width // 8 + 128), BF16),
        compiler_params=pltpu.CompilerParams(vmem_limit_bytes=16 * MIB),
        name="combine_rows",
    )(r, rank, gate, spot)


def join_kernel(landed_ref, stream_ref, o_ref):
    tokens, w = stream_ref.shape
    tail = landed_ref[:, w:].astype(F32)
    spot = tail[:, 0:1] * 16.0 + tail[:, 1:2]
    count = landed_ref.shape[0]
    hit = jnp.where(spot == iota((count, tokens), 1).astype(F32), 1.0, 0.0).astype(BF16)
    added = lax.dot_general(hit, landed_ref[:, :w], (((0,), (0,)), ((), ())), preferred_element_type=F32)
    o_ref[...] = (stream_ref[...].astype(F32) + added).astype(BF16)


def join(landed, stream):
    return pl.pallas_call(
        join_kernel,
        out_shape=jax.ShapeDtypeStruct(stream.shape, BF16),
        compiler_params=pltpu.CompilerParams(vmem_limit_bytes=16 * MIB),
        name="join_rows",
    )(landed, stream)


def qkv_kernel(place_ref, *refs):
    x_refs = refs[:8]
    gain_ref, wq_ref, wkv_ref, qg_ref, kg_ref, cos_ref, sin_ref, low_ref, high_ref, kv_ref, norm_s = refs[8:]
    z = place_ref[1]
    core = place_ref[2]
    tokens, w = x_refs[0].shape
    width = 8 * w
    square = jnp.zeros((tokens, 1), F32)
    for x_ref in x_refs:
        x = x_ref[...].astype(F32)
        square = square + jnp.sum(x * x, 1, keepdims=True)
    scale = lax.rsqrt(square * (1.0 / width) + EPSILON)
    half = tokens // 2
    start = pl.multiple_of(core * half, half)
    for i, x_ref in enumerate(x_refs):
        block = 2 * lax.rem(z + 4 - i % 4, 4) + (core if i < 4 else 1 - core)
        norm = (x_ref[...].astype(F32) * scale * gain_ref[pl.ds(block, 1), :]).astype(BF16)
        norm_s[:, pl.ds(pl.multiple_of(block * w, w), w)] = norm
    both = dot(norm_s[pl.ds(start, half), :], wkv_ref[...])
    queries = dot(norm_s[...], wq_ref[...])

    def finished(vectors, gains, cos, sin):
        mean = jnp.mean(vectors * vectors, -1, keepdims=True)
        vectors = vectors * lax.rsqrt(mean + EPSILON) * gains
        return vectors * cos + pltpu.roll(vectors, HD // 2, 1) * sin

    cos_k = cos_ref[pl.ds(start, half), :]
    sin_k = sin_ref[pl.ds(start, half), :]
    kv_ref[:, :HD] = finished(both[:, :HD], kg_ref[...], cos_k, sin_k).astype(BF16)
    kv_ref[:, HD:] = both[:, HD:].astype(BF16)
    factor = math.log2(math.e) / math.sqrt(HD)
    cos = cos_ref[...]
    sin = sin_ref[...]
    for h in range(low_ref.shape[0]):
        part = slice(h * HD, (h + 1) * HD)
        done = (finished(queries[:, part], qg_ref[:, part], cos, sin) * factor).astype(BF16)
        low_ref[h] = done[:half]
        high_ref[h] = done[half:]


def project(place, blocks, row_gain, w_query, w_kv, q_gain, key_gain, cos, sin):
    tokens, w = blocks[0].shape
    heads = w_query.shape[1] // HD
    part = jax.ShapeDtypeStruct((heads, tokens // 2, HD), BF16)
    return pl.pallas_call(
        qkv_kernel,
        in_specs=[pl.BlockSpec(memory_space=pltpu.SMEM)] + [pl.BlockSpec(memory_space=VMEM)] * 15,
        out_shape=[part, part, jax.ShapeDtypeStruct((tokens // 2, 2 * HD), BF16)],
        scratch_shapes=[VMEM((tokens, 8 * w), BF16)],
        compiler_params=pltpu.CompilerParams(vmem_limit_bytes=20 * MIB),
        name="project_qkv",
    )(
        place,
        *blocks,
        row_gain,
        w_query,
        w_kv,
        q_gain.reshape(1, -1),
        key_gain,
        cos,
        sin,
    )


def attend_kernel(place_ref, low_ref, high_ref, kv_ref, o_ref, value_s):
    core = place_ref[2]
    shards, shard, _ = kv_ref.shape
    heads, half, _ = low_ref.shape
    group = 4
    subs = 2
    span = group * shard
    rows = heads * half // subs
    value_s[:, :, :HD] = kv_ref[:, :, HD:]
    value_s[:, :, HD:] = jnp.ones((shards, shard, HD), BF16)

    for upper, q_ref in enumerate((low_ref, high_ref)):
        own = place_ref[0] if upper == 0 else shards - 1 - place_ref[0]
        queries = q_ref[...].reshape(heads * half, HD)
        pieces = [queries[i * rows : (i + 1) * rows] for i in range(subs)]

        def fold(carry, chunk, masked):
            keys = kv_ref[pl.ds(chunk * group, group), :, :HD].reshape(span, HD)
            values = value_s[pl.ds(chunk * group, group)].reshape(span, 2 * HD)
            every = [dot_t(piece, keys) for piece in pieces]
            result = []
            for (highest, weighted), scores in zip(carry, every):
                if masked:
                    t = iota((rows, span), 1)
                    key_pos = (chunk * group + t // shard) * (2 * shard) + core * shard + t % shard
                    query_pos = own * (2 * half) + upper * half + iota((rows, span), 0) % half
                    allowed = query_pos >= key_pos
                    scores = jnp.where(allowed, scores, NEG)
                fresh = jnp.maximum(highest, jnp.max(scores, 1, keepdims=True))
                weights = jnp.exp2(scores - fresh)
                if masked:
                    weights = jnp.where(allowed, weights, 0.0)
                weighted = weighted * jnp.exp2(highest - fresh) + dot(weights.astype(BF16), values)
                result.append((fresh, weighted))
            return tuple(result)

        start = tuple((jnp.full((rows, 1), NEG, F32), jnp.zeros((rows, 2 * HD), F32)) for _ in range(subs))
        whole = own // group
        state = lax.fori_loop(0, whole, lambda j, carry: fold(carry, j, False), start)
        state = fold(state, whole, True)
        lane = iota((rows, HD), 1)
        for i, (highest, weighted) in enumerate(state):
            part = slice(i * (heads // subs), (i + 1) * (heads // subs))
            o_ref[part, upper * half : (upper + 1) * half, :HD] = weighted[:, :HD].reshape(heads // subs, half, HD)
            stats = jnp.where(lane < HD // 2, highest, weighted[:, HD:])
            o_ref[part, upper * half : (upper + 1) * half, HD:] = stats.reshape(heads // subs, half, HD)


def attend(place, low, high, kv):
    heads, half, _ = low.shape
    return pl.pallas_call(
        attend_kernel,
        in_specs=[pl.BlockSpec(memory_space=pltpu.SMEM)] + [pl.BlockSpec(memory_space=VMEM)] * 3,
        out_shape=jax.ShapeDtypeStruct((heads, 2 * half, 2 * HD), F32),
        scratch_shapes=[VMEM(kv.shape, BF16)],
        compiler_params=pltpu.CompilerParams(vmem_limit_bytes=28 * MIB),
        name="attend",
    )(place, low, high, kv)


def merge_kernel(place_ref, own_ref, other_ref, w_ref, att_ref, o_ref):
    for h in range(own_ref.shape[0]):
        m0 = own_ref[h, :, HD : HD + 1]
        m1 = other_ref[h, :, HD : HD + 1]
        top = jnp.maximum(m0, m1)
        e0 = jnp.exp2(m0 - top)
        e1 = jnp.exp2(m1 - top)
        total = own_ref[h, :, 2 * HD - 1 :] * e0 + other_ref[h, :, 2 * HD - 1 :] * e1
        share = 1.0 / total
        value = own_ref[h, :, :HD] * (e0 * share) + other_ref[h, :, :HD] * (e1 * share)
        att_ref[:, h * HD : (h + 1) * HD] = value.astype(BF16)
    project_blocks(place_ref[1], 1 - place_ref[2], att_ref, w_ref, o_ref)


def project_blocks(z, core, att_ref, w_ref, o_ref):
    w = o_ref.shape[2]
    for i in range(o_ref.shape[0]):
        block = 2 * lax.rem(z + i, 4) + core
        o_ref[i] = dot(att_ref[...], w_ref[:, pl.ds(pl.multiple_of(block * w, w), w)]).astype(BF16)


def own_kernel(place_ref, att_ref, w_ref, o_ref):
    project_blocks(place_ref[1], place_ref[2], att_ref, w_ref, o_ref)


def merge_and_project(place, own, other, w_out):
    heads, tokens, _ = own.shape
    return pl.pallas_call(
        merge_kernel,
        in_specs=[pl.BlockSpec(memory_space=pltpu.SMEM)] + [pl.BlockSpec(memory_space=VMEM)] * 3,
        out_shape=[
            jax.ShapeDtypeStruct((tokens, heads * HD), BF16),
            jax.ShapeDtypeStruct((4, tokens, w_out.shape[1] // 8), BF16),
        ],
        compiler_params=pltpu.CompilerParams(vmem_limit_bytes=16 * MIB),
        name="merge_and_project",
    )(place, own, other, w_out)


def project_own(place, attended, w_out):
    return pl.pallas_call(
        own_kernel,
        in_specs=[pl.BlockSpec(memory_space=pltpu.SMEM)] + [pl.BlockSpec(memory_space=VMEM)] * 2,
        out_shape=jax.ShapeDtypeStruct((4, attended.shape[0], w_out.shape[1] // 8), BF16),
        compiler_params=pltpu.CompilerParams(vmem_limit_bytes=16 * MIB),
        name="project_own",
    )(place, attended, w_out)


def body(
    branch_rows,
    expert_ids,
    targets,
    router,
    w_gate,
    w_up,
    w_down,
    stream,
    attn_gain,
    q_gain,
    k_gain,
    w_query,
    w_key,
    w_value,
    w_out,
):
    ctx = lax.axis_index("ctx")
    head = lax.axis_index("head")
    z = head // 2
    core = head % 2
    place = jnp.stack([ctx, z, core]).astype(jnp.int32)
    experts = router.shape[1]
    tokens, w = stream.shape
    partner = [(i, i ^ 1) for i in range(8)]
    mirror = [(i, 15 - i) for i in range(16)]

    def along(shard, hops):
        return lax.ppermute(shard, "head", [(i, (i + 2 * hops) % 8) for i in range(8)])

    def everywhere(blocks):
        return lax.all_to_all(blocks, ("ctx", "head"), split_axis=0, concat_axis=0, tiled=True)

    half_dim = HD // 2
    frequency = jnp.power(jnp.float32(THETA), -jnp.arange(half_dim, dtype=F32) * 2.0 / HD)
    positions = ctx * tokens + jnp.arange(tokens, dtype=jnp.int32)
    angles = positions.astype(F32)[:, None] * frequency[None, :]
    cosines = jnp.cos(angles)
    sines = jnp.sin(angles)
    cos = jnp.concatenate([cosines, cosines], 1)
    sin = jnp.concatenate([-sines, sines], 1)

    outgoing, rank, gate, spot = dispatch(branch_rows, expert_ids, targets, router)
    shape = (experts, 8, outgoing.shape[1])
    arrived = everywhere(outgoing.reshape(shape)).reshape(outgoing.shape)
    first_column = z * HD
    w_kv = jnp.concatenate([lax.dynamic_slice_in_dim(w, first_column, HD, 1) for w in (w_key, w_value)], 1)
    key_gain = lax.dynamic_slice_in_dim(k_gain, first_column, HD, 0).reshape(1, HD)
    row_gain = attn_gain.reshape(8, w)
    early = (arrived, cos, sin, w_kv, key_gain, row_gain, place)
    arrived, cos, sin, w_kv, key_gain, row_gain, place = lax.optimization_barrier(early)
    produced = run_expert(arrived, w_gate[0], w_up[0], w_down[0])
    returned = everywhere(produced.reshape(shape)).reshape(outgoing.shape)
    parcels = combine(returned, rank, gate, spot)
    landed = everywhere(parcels.reshape(experts, 8, parcels.shape[3])).reshape(experts * 8, parcels.shape[3])
    joined = join(landed, stream)

    mine = [joined] + [along(joined, hops) for hops in (1, 2, 3)]
    blocks = mine + [lax.ppermute(block, "head", partner) for block in mine]
    low, high, kv = project(place, blocks, row_gain, w_query, w_kv, q_gain, key_gain, cos, sin)
    all_kv = lax.all_to_all(
        jnp.broadcast_to(kv[None], (16, *kv.shape)), "ctx", split_axis=0, concat_axis=0, tiled=True
    )
    high = lax.ppermute(high, "ctx", mirror)
    partner_low = lax.ppermute(low, "head", partner)
    partner_high = lax.ppermute(high, "head", partner)
    for_partner = attend(place, partner_low, partner_high, all_kv)
    from_partner = lax.ppermute(for_partner, "head", partner)
    folded = attend(place, low, high, all_kv)
    attended, sent = merge_and_project(place, folded, from_partner, w_out)
    received = lax.ppermute(sent, "head", partner)
    kept = project_own(place, attended, w_out)
    pair = [(kept[i].astype(F32) + received[i].astype(F32)).astype(BF16) for i in range(4)]
    total = pair[0].astype(F32)
    for hops in (1, 2, 3):
        total = total + along(pair[hops], hops).astype(F32)
    half = tokens // 2
    upper = lax.ppermute(total[half:].astype(BF16), "ctx", mirror)
    summed = jnp.concatenate([total[:half], upper.astype(F32)], 0)
    return (joined.astype(F32) + summed).astype(BF16)


def solution(mesh):
    in_specs = (
        P(("ctx", "head"), None),
        P(("ctx", "head"), None),
        P(("ctx", "head")),
        P(),
        P(("ctx", "head"), None, None),
        P(("ctx", "head"), None, None),
        P(("ctx", "head"), None, None),
        P("ctx", "head"),
        P(),
        P("head"),
        P(),
        P(None, "head"),
        P(),
        P(),
        P("head", None),
    )
    out_specs = P("ctx", "head")
    return jax.shard_map(body, mesh=mesh, in_specs=in_specs, out_specs=out_specs, check_vma=False)
```

time: 365 us -> 351 us (0.962)
  the two profiles are of different devices: /device:TPU:24 before, /device:TPU:1 now
where the time goes in v2:
time: 351 us; the launch traced here: 347 us
  waiting for transfers between devices  132 us (38%)
  blocking collectives  104 us (30%)
  Pallas kernels  55.5 us (16%)
  starting transfers between devices  37.1 us (11%)
  local copies, waits for them, and re-layouts  14.7 us (4%)
    all_to_all x2, blocking collectives, everywhere(): lax.all_to_all(blocks, ('ctx', 'head'), split_axis=0, concat_axis=0, tile...  104 us
    all_to_all x1, waiting for transfers between devices, everywhere(): lax.all_to_all(blocks, ('ctx', 'head'), split_axis=0, concat_axis=0, tile...  73.7 us
    ppermute x1, waiting for transfers between devices, body(): high = lax.ppermute(high, 'ctx', mirror)  30.4 us
    pallas_call x1, Pallas kernels, run_expert(): pl.pallas_call(expert_kernel, out_shape=jax.ShapeDtypeStruct(y.shape, BF1...  20 us
    pallas_call x2, Pallas kernels, attend(): pl.pallas_call(attend_kernel, in_specs=[pl.BlockSpec(memory_space=pltpu.S...  19.5 us
    ppermute x6, waiting for transfers between devices, along(): lax.ppermute(shard, 'head', [(i, (i + 2 * hops) % 8) for i in range(8)])  18.7 us
    all_to_all x1, starting transfers between devices, everywhere(): lax.all_to_all(blocks, ('ctx', 'head'), split_axis=0, concat_axis=0, tile...  12.1 us
    unnamed x30, local copies, waits for them, and re-layouts  11.8 us
  transfers between devices with their start and end apart: 18, of which 9 were waited for; matrix products, arithmetic and copies ran while one was open for 1% of the time, Pallas kernels for 3%

profile of v2, /device:TPU:1, one launch (start us, length us, event | category | flops | bytes accessed | tf_op | source)
XLA Modules:
  0.0 346.6 jit_solution(2048658989541582530)
XLA Ops:
  3.4 3.7 %dispatch_rows.1 = (bf16[1024,3072]{1,0:T(8,128)(2,1)S(1)}, f32[128,128]{1,0:T(8,128)S(1)}, f32[128,128]{1,0:T(8,128)S(1)}, f32[128,128]{1,0:T(8,128)S(1)}) custom-call(bf16[128,2048]{1,0:T(8,128)(2,1)S(1)} %copy-done.8, s32[8,128]{1,0:T(8,128)S(1)} %bitcast.36, s32[1,128]{1,0:T(1,128)S(1)} %bitcast.38, bf16[2048,128]{1,0:T(8,128)(2,1)S(1)} %copy-done.9), custom_call_target="tpu_custom_call" | custom-call | tf_op jit(solution)/shard_map/dispatch_rows/pallas_call | solution.py:78
  7.2 2.6 copy-done.3
  9.8 12.1 %all-to-all-start = ((bf16[128,8,3072]{2,1,0:T(8,128)(2,1)}), bf16[128,8,3072]{2,1,0:T(8,128)(2,1)}, u32[]{:S(2)}, u32[]{:S(2)}) async-start(bf16[128,8,3072]{2,1,0:T(8,128)(2,1)} %bitcast.30), calls=%async_computation | async-start | bytes 12582912 | tf_op jit(solution)/shard_map/all_to_all | solution.py:398
  24.8 73.7 %all-to-all-done = bf16[128,8,3072]{2,1,0:T(8,128)(2,1)} async-done(((bf16[128,8,3072]{2,1,0:T(8,128)(2,1)}), bf16[128,8,3072]{2,1,0:T(8,128)(2,1)}, u32[]{:S(2)}, u32[]{:S(2)}) %all-to-all-start) | async-done | bytes 6291488 | tf_op jit(solution)/shard_map/all_to_all | solution.py:398
  98.5 1.9 copy-done.4
  100.4 1.9 copy-done.5
  104.2 20.0 %expert_ffn.1 = bf16[1024,3072]{1,0:T(8,128)(2,1)S(1)} custom-call(bf16[1024,3072]{1,0:T(8,128)(2,1)} %bitcast.3.y_ref, bf16[2048,768]{1,0:T(8,128)(2,1)S(1)} %bitcast.33, bf16[2048,768]{1,0:T(8,128)(2,1)S(1)} %bitcast.34, bf16[768,2048]{1,0:T(8,128)(2,1)S(1)} %bitcast.35), custom_call_target="tpu_custom_call" | custom-call | tf_op jit(solution)/shard_map/expert_ffn/pallas_call | solution.py:120
  124.2 83.2 %all_to_all.20 = bf16[128,8,3072]{2,1,0:T(8,128)(2,1)S(1)} all-to-all(bf16[128,8,3072]{2,1,0:T(8,128)(2,1)S(1)} %bitcast.29), channel_id=1, replica_groups=mesh['ctx'=16,'head'=8] {'ctx','head'}, dimensions={0} | all-to-all | bytes 12582912 | tf_op jit(solution)/shard_map/all_to_all | solution.py:398
  207.4 2.8 combine_rows.1
  210.2 20.8 %all_to_all.21 = bf16[128,8,384]{2,1,0:T(8,128)(2,1)S(1)} all-to-all(bf16[128,8,384]{2,1,0:T(8,128)(2,1)S(1)} %bitcast.31), channel_id=1, replica_groups=mesh['ctx'=16,'head'=8] {'ctx','head'}, dimensions={0} | all-to-all | bytes 1572864 | tf_op jit(solution)/shard_map/all_to_all | solution.py:398
  233.4 1.9 collective-permute-start.3
  235.4 3.0 collective-permute-done.2.refs_3_
  238.4 3.9 %collective-permute-start.6 = (bf16[512,256]{1,0:T(8,128)(2,1)S(1)}, bf16[512,256]{1,0:T(8,128)(2,1)S(1)}, u32[]{:S(2)}, u32[]{:S(2)}) collective-permute-start(bf16[512,256]{1,0:T(8,128)(2,1)S(1)} %collective-permute-done.2.refs_3_), channel_id=1, source_target_pairs={{0,1},{1,0},{2,3},{3,2},{4,5},{5,4},{6,7},{7,6},{8,9},{9,8},{10,11... | collective-permute-start | bytes 786440 | tf_op jit(solution)/shard_map/ppermute | solution.py:425
  244.0 3.8 %collective-permute-done.refs_1_ = bf16[512,256]{1,0:T(8,128)(2,1)S(1)} collective-permute-done((bf16[512,256]{1,0:T(8,128)(2,1)S(1)}, bf16[512,256]{1,0:T(8,128)(2,1)S(1)}, u32[]{:S(2)}, u32[]{:S(2)}) %collective-permute-start) | collective-permute-done | bytes 262176 | tf_op jit(solution)/shard_map/ppermute | solution.py:395
  249.8 4.9 %project_qkv.1 = (bf16[4,256,128]{2,1,0:T(8,128)(2,1)S(1)}, bf16[4,256,128]{2,1,0:T(8,128)(2,1)S(1)}, bf16[256,256]{1,0:T(8,128)(2,1)S(1)}) custom-call(s32[3]{0:T(128)S(1)} %pad_add_fusion.place_ref, bf16[512,256]{1,0:T(8,128)(2,1)S(1)} %join_rows.1.refs_0_, bf16[512,256]{1,0:T(8,128)(2,1)S(1)} %collective-permute-done.refs_1_, ...), custom_call_target="tpu_custom_call" | custom-call | tf_op jit(solution)/shard_map/project_qkv/pallas_call | solution.py:238
  256.2 3.7 %all-to-all-start.3 = ((bf16[16,256,256]{2,1,0:T(8,128)(2,1)}), bf16[16,256,256]{2,1,0:T(8,128)(2,1)S(1)}, u32[]{:S(2)}, u32[]{:S(2)}) async-start(bf16[16,256,256]{2,1,0:T(8,128)(2,1)} %broadcast_in_dim.2), calls=%async_computation.3 | async-start | bytes 4194304 | tf_op jit(solution)/shard_map/all_to_all | solution.py:427
  260.0 4.7 %collective-permute-start.7 = (bf16[4,256,128]{2,1,0:T(8,128)(2,1)S(1)}, bf16[4,256,128]{2,1,0:T(8,128)(2,1)S(1)}, u32[]{:S(2)}, u32[]{:S(2)}) collective-permute-start(bf16[4,256,128]{2,1,0:T(8,128)(2,1)S(1)} %get-tuple-element.33), channel_id=1, source_target_pairs={{0,120},{8,112},{16,104},{24,96},{32,88},{40,80},{48,72},{56,64},{... | collective-permute-start | bytes 786440 | tf_op jit(solution)/shard_map/ppermute | solution.py:430
  265.6 30.4 %collective-permute-done.7.high_ref = bf16[4,256,128]{2,1,0:T(8,128)(2,1)S(1)} collective-permute-done((bf16[4,256,128]{2,1,0:T(8,128)(2,1)S(1)}, bf16[4,256,128]{2,1,0:T(8,128)(2,1)S(1)}, u32[]{:S(2)}, u32[]{:S(2)}) %collective-permute-start.7) | collective-permute-done | bytes 262176 | tf_op jit(solution)/shard_map/ppermute | solution.py:430
  297.9 9.9 %attend.3 = f32[4,512,256]{2,1,0:T(8,128)S(1)} custom-call(s32[3]{0:T(128)S(1)} %pad_add_fusion.place_ref, bf16[4,256,128]{2,1,0:T(8,128)(2,1)S(1)} %collective-permute-done.8.low_ref, bf16[4,256,128]{2,1,0:T(8,128)(2,1)S(1)} %collective-permute-done.9.high_ref, bf16[16,256,256]{2,1,0:T(8,128)(2,1)S(1)} %all-to-all-done.3.kv_ref), custom_call_target="tpu_custom_call" | custom-call | tf_op jit(solution)/shard_map/attend/pallas_call | solution.py:308
  308.3 9.7 %attend.2.own_ref = f32[4,512,256]{2,1,0:T(8,128)S(1)} custom-call(s32[3]{0:T(128)S(1)} %pad_add_fusion.place_ref, bf16[4,256,128]{2,1,0:T(8,128)(2,1)S(1)} %get-tuple-element.32.low_ref, bf16[4,256,128]{2,1,0:T(8,128)(2,1)S(1)} %collective-permute-done.7.high_ref, bf16[16,256,256]{2,1,0:T(8,128)(2,1)S(1)} %all-to-all-done.3.kv_ref), custom_call_target="tpu_custom_call" | custom-call | tf_op jit(solution)/shard_map/attend/pallas_call | solution.py:308
  318.0 2.6 merge_and_project.1
  323.6 2.7 collective-permute-start.14
  326.3 11.9 %collective-permute-done.12 = bf16[512,256]{1,0:T(8,128)(2,1)S(1)} collective-permute-done((bf16[512,256]{1,0:T(8,128)(2,1)S(1)}, bf16[512,256]{1,0:T(8,128)(2,1)S(1)}, u32[]{:S(2)}, u32[]{:S(2)}) %collective-permute-start.12) | collective-permute-done | bytes 262176 | tf_op jit(solution)/shard_map/ppermute | solution.py:395
  339.8 5.8 %collective-permute-done.15 = bf16[256,256]{1,0:T(8,128)(2,1)S(1)} collective-permute-done((bf16[256,256]{1,0:T(8,128)(2,1)S(1)}, bf16[256,256]{1,0:T(8,128)(2,1)S(1)}, u32[]{:S(2)}, u32[]{:S(2)}) %collective-permute-start.15) | collective-permute-done | bytes 131104 | tf_op jit(solution)/shard_map/ppermute | solution.py:444
  (69 shorter events, 24.6 us)
Async XLA Ops:
  0.0 22.0 %copy-start = (f32[512]{0:T(512)S(1)}, f32[512]{0:T(512)}, u32[]{:S(2)}) copy-start(f32[512]{0:T(512)} %param.25) | copy-start | bytes 6148
  9.8 12.1 %copy-start.14 = (f32[2048]{0:T(1024)S(1)}, f32[2048]{0:T(1024)}, u32[]{:S(2)}) copy-start(f32[2048]{0:T(1024)} %param.23) | copy-start | bytes 24580
  9.8 88.7 %all-to-all-start = ((bf16[128,8,3072]{2,1,0:T(8,128)(2,1)}), bf16[128,8,3072]{2,1,0:T(8,128)(2,1)}, u32[]{:S(2)}, u32[]{:S(2)}) async-start(bf16[128,8,3072]{2,1,0:T(8,128)(2,1)} %bitcast.30), calls=%async_computation | async-start | bytes 12582912 | tf_op jit(solution)/shard_map/all_to_all | solution.py:398
  207.4 23.6 %copy-start.10 = (bf16[512,256]{1,0:T(8,128)(2,1)S(1)}, bf16[512,256]{1,0:T(8,128)(2,1)}, u32[]{:S(2)}) copy-start(bf16[512,256]{1,0:T(8,128)(2,1)} %stream_ref.1) | copy-start | bytes 786436
  210.1 39.7 %copy-start.7 = (bf16[2048,512]{1,0:T(8,128)(2,1)S(1)}, bf16[2048,512]{1,0:T(8,128)(2,1)}, u32[]{:S(2)}) copy-start(bf16[2048,512]{1,0:T(8,128)(2,1)} %refs_9_.1) | copy-start | bytes 6291460
  210.2 39.7 %copy-start.12 = (f32[512]{0:T(512)S(1)}, f32[512]{0:T(512)}, u32[]{:S(2)}) copy-start(f32[512]{0:T(512)} %param.24) | copy-start | bytes 6148
  231.8 6.6 %collective-permute-start.2 = (bf16[512,256]{1,0:T(8,128)(2,1)S(1)}, bf16[512,256]{1,0:T(8,128)(2,1)S(1)}, u32[]{:S(2)}, u32[]{:S(2)}) collective-permute-start(bf16[512,256]{1,0:T(8,128)(2,1)S(1)} %join_rows.1.refs_0_), channel_id=1, source_target_pairs={{0,6},{1,7},{2,0},{3,1},{4,2},{5,3},{6,4},{7,5},{8,14},{9,15},{10,... | collective-permute-start | bytes 786440 | tf_op jit(solution)/shard_map/ppermute | solution.py:395
  232.4 9.9 %collective-permute-start.1 = (bf16[512,256]{1,0:T(8,128)(2,1)S(1)}, bf16[512,256]{1,0:T(8,128)(2,1)S(1)}, u32[]{:S(2)}, u32[]{:S(2)}) collective-permute-start(bf16[512,256]{1,0:T(8,128)(2,1)S(1)} %join_rows.1.refs_0_), channel_id=1, source_target_pairs={{0,4},{1,5},{2,6},{3,7},{4,0},{5,1},{6,2},{7,3},{8,12},{9,13},{10,... | collective-permute-start | bytes 786440 | tf_op jit(solution)/shard_map/ppermute | solution.py:395
  233.4 14.3 %collective-permute-start = (bf16[512,256]{1,0:T(8,128)(2,1)S(1)}, bf16[512,256]{1,0:T(8,128)(2,1)S(1)}, u32[]{:S(2)}, u32[]{:S(2)}) collective-permute-start(bf16[512,256]{1,0:T(8,128)(2,1)S(1)} %join_rows.1.refs_0_), channel_id=1, source_target_pairs={{0,2},{1,3},{2,4},{3,5},{4,6},{5,7},{6,0},{7,1},{8,10},{9,11},{10,... | collective-permute-start | bytes 786440 | tf_op jit(solution)/shard_map/ppermute | solution.py:395
  233.4 15.2 %collective-permute-start.3 = (bf16[512,256]{1,0:T(8,128)(2,1)S(1)}, bf16[512,256]{1,0:T(8,128)(2,1)S(1)}, u32[]{:S(2)}, u32[]{:S(2)}) collective-permute-start(bf16[512,256]{1,0:T(8,128)(2,1)S(1)} %join_rows.1.refs_0_), channel_id=1, source_target_pairs={{0,1},{1,0},{2,3},{3,2},{4,5},{5,4},{6,7},{7,6},{8,9},{9,8},{10,11... | collective-permute-start | bytes 786440 | tf_op jit(solution)/shard_map/ppermute | solution.py:425
  238.4 10.2 %collective-permute-start.6 = (bf16[512,256]{1,0:T(8,128)(2,1)S(1)}, bf16[512,256]{1,0:T(8,128)(2,1)S(1)}, u32[]{:S(2)}, u32[]{:S(2)}) collective-permute-start(bf16[512,256]{1,0:T(8,128)(2,1)S(1)} %collective-permute-done.2.refs_3_), channel_id=1, source_target_pairs={{0,1},{1,0},{2,3},{3,2},{4,5},{5,4},{6,7},{7,6},{8,9},{9,8},{10,11... | collective-permute-start | bytes 786440 | tf_op jit(solution)/shard_map/ppermute | solution.py:425
  242.3 6.4 %collective-permute-start.5 = (bf16[512,256]{1,0:T(8,128)(2,1)S(1)}, bf16[512,256]{1,0:T(8,128)(2,1)S(1)}, u32[]{:S(2)}, u32[]{:S(2)}) collective-permute-start(bf16[512,256]{1,0:T(8,128)(2,1)S(1)} %collective-permute-done.1.refs_2_), channel_id=1, source_target_pairs={{0,1},{1,0},{2,3},{3,2},{4,5},{5,4},{6,7},{7,6},{8,9},{9,8},{10,11... | collective-permute-start | bytes 786440 | tf_op jit(solution)/shard_map/ppermute | solution.py:425
  247.7 2.1 collective-permute-start.4
  256.2 41.7 %all-to-all-start.3 = ((bf16[16,256,256]{2,1,0:T(8,128)(2,1)}), bf16[16,256,256]{2,1,0:T(8,128)(2,1)S(1)}, u32[]{:S(2)}, u32[]{:S(2)}) async-start(bf16[16,256,256]{2,1,0:T(8,128)(2,1)} %broadcast_in_dim.2), calls=%async_computation.3 | async-start | bytes 4194304 | tf_op jit(solution)/shard_map/all_to_all | solution.py:427
  260.0 36.0 %collective-permute-start.7 = (bf16[4,256,128]{2,1,0:T(8,128)(2,1)S(1)}, bf16[4,256,128]{2,1,0:T(8,128)(2,1)S(1)}, u32[]{:S(2)}, u32[]{:S(2)}) collective-permute-start(bf16[4,256,128]{2,1,0:T(8,128)(2,1)S(1)} %get-tuple-element.33), channel_id=1, source_target_pairs={{0,120},{8,112},{16,104},{24,96},{32,88},{40,80},{48,72},{56,64},{... | collective-permute-start | bytes 786440 | tf_op jit(solution)/shard_map/ppermute | solution.py:430
  264.6 32.1 %collective-permute-start.8 = (bf16[4,256,128]{2,1,0:T(8,128)(2,1)S(1)}, bf16[4,256,128]{2,1,0:T(8,128)(2,1)S(1)}, u32[]{:S(2)}, u32[]{:S(2)}) collective-permute-start(bf16[4,256,128]{2,1,0:T(8,128)(2,1)S(1)} %get-tuple-element.32.low_ref), channel_id=1, source_target_pairs={{0,1},{1,0},{2,3},{3,2},{4,5},{5,4},{6,7},{7,6},{8,9},{9,8},{10,11... | collective-permute-start | bytes 786440 | tf_op jit(solution)/shard_map/ppermute | solution.py:431
  296.0 1.9 collective-permute-start.9
  307.8 10.1 %collective-permute-start.10 = (f32[4,512,256]{2,1,0:T(8,128)S(1)}, f32[4,512,256]{2,1,0:T(8,128)S(1)}, u32[]{:S(2)}, u32[]{:S(2)}) collective-permute-start(f32[4,512,256]{2,1,0:T(8,128)S(1)} %attend.3), channel_id=1, source_target_pairs={{0,1},{1,0},{2,3},{3,2},{4,5},{5,4},{6,7},{7,6},{8,9},{9,8},{10,11... | collective-permute-start | bytes 6291464 | tf_op jit(solution)/shard_map/ppermute | solution.py:434
  320.6 2.7 collective-permute-start.11
  323.3 23.1 %copy-start.1 = (f32[512]{0:T(512)S(1)}, f32[512]{0:T(512)}, u32[]{:S(2)}) copy-start(f32[512]{0:T(512)} %param.25) | copy-start | bytes 6148
  323.5 14.7 %collective-permute-start.12 = (bf16[512,256]{1,0:T(8,128)(2,1)S(1)}, bf16[512,256]{1,0:T(8,128)(2,1)S(1)}, u32[]{:S(2)}, u32[]{:S(2)}) collective-permute-start(bf16[512,256]{1,0:T(8,128)(2,1)S(1)} %get-tuple-element.37), channel_id=1, source_target_pairs={{0,2},{1,3},{2,4},{3,5},{4,6},{5,7},{6,0},{7,1},{8,10},{9,11},{10,... | collective-permute-start | bytes 786440 | tf_op jit(solution)/shard_map/ppermute | solution.py:395
  323.6 14.6 %collective-permute-start.14 = (bf16[512,256]{1,0:T(8,128)(2,1)S(1)}, bf16[512,256]{1,0:T(8,128)(2,1)S(1)}, u32[]{:S(2)}, u32[]{:S(2)}) collective-permute-start(bf16[512,256]{1,0:T(8,128)(2,1)S(1)} %get-tuple-element.38), channel_id=1, source_target_pairs={{0,6},{1,7},{2,0},{3,1},{4,2},{5,3},{6,4},{7,5},{8,14},{9,15},{10,... | collective-permute-start | bytes 786440 | tf_op jit(solution)/shard_map/ppermute | solution.py:395
  326.3 11.9 %collective-permute-start.13 = (bf16[512,256]{1,0:T(8,128)(2,1)S(1)}, bf16[512,256]{1,0:T(8,128)(2,1)S(1)}, u32[]{:S(2)}, u32[]{:S(2)}) collective-permute-start(bf16[512,256]{1,0:T(8,128)(2,1)S(1)} %get-tuple-element.39), channel_id=1, source_target_pairs={{0,4},{1,5},{2,6},{3,7},{4,0},{5,1},{6,2},{7,3},{8,12},{9,13},{10,... | collective-permute-start | bytes 786440 | tf_op jit(solution)/shard_map/ppermute | solution.py:395
  338.4 7.2 %collective-permute-start.15 = (bf16[256,256]{1,0:T(8,128)(2,1)S(1)}, bf16[256,256]{1,0:T(8,128)(2,1)S(1)}, u32[]{:S(2)}, u32[]{:S(2)}) collective-permute-start(bf16[256,256]{1,0:T(8,128)(2,1)S(1)} %slice.60), channel_id=1, source_target_pairs={{0,120},{8,112},{16,104},{24,96},{32,88},{40,80},{48,72},{56,64},{... | collective-permute-start | bytes 393224 | tf_op jit(solution)/shard_map/ppermute | solution.py:444
  (9 other events, 21.9 us)

commit v3 on v2

--- a/solution.py
+++ b/solution.py
@@ -2,6 +2,7 @@
 
 import jax
 import jax.numpy as jnp
+import numpy as np
 from jax import lax
 from jax.experimental import pallas as pl
 from jax.experimental.pallas import tpu as pltpu
@@ -31,8 +32,23 @@
     return lax.dot_general(a, b, (((1,), (1,)), ((), ())), preferred_element_type=F32)
 
 
-def dispatch_kernel(rows_ref, ids_ref, targets_ref, router_ref, y_ref, rank_ref, gate_ref, spot_ref):
+def start_loads(pairs, sems):
+    loads = [pltpu.make_async_copy(source, target, sems.at[i]) for i, (source, target) in enumerate(pairs)]
+    for load in loads:
+        load.start()
+    return loads
+
+
+def dispatch_kernel(
+    rows_hbm, ids_hbm, targets_hbm, router_hbm, y_ref, rank_ref, gate_ref, spot_ref,
+    rows_ref, ids_ref, targets_ref, router_ref, sems,
+):
+    loads = start_loads(
+        [(targets_hbm, targets_ref), (ids_hbm, ids_ref), (rows_hbm, rows_ref), (router_hbm, router_ref)], sems
+    )
     n, width = rows_ref.shape
+    for load in loads[:3]:
+        load.wait()
     experts = router_ref.shape[1]
     first = iota((n, n), 0)
     second = iota((n, n), 1)
@@ -66,6 +82,7 @@
         y_ref[lines, width:] = (dot(low, rows[:, :half]) + dot(high, rows[:, half:])).astype(BF16)
     rank_ref[...] = rank.T
     member_q = member.T > 0.5
+    loads[3].wait()
     logits = dot(rows, router_ref[...])
     highest = jnp.max(jnp.where(member_q, logits, NEG), 1, keepdims=True)
     raised = jnp.where(member_q, jnp.exp(jnp.minimum(logits - highest, 0.0)), 0.0)
@@ -77,7 +94,15 @@
     table = jax.ShapeDtypeStruct((n, 128), F32)
     return pl.pallas_call(
         dispatch_kernel,
+        in_specs=[pl.BlockSpec(memory_space=pltpu.HBM)] * 4,
         out_shape=[jax.ShapeDtypeStruct((1024, width * 3 // 2), BF16), table, table, table],
+        scratch_shapes=[
+            VMEM((n, width), BF16),
+            VMEM((8, n), jnp.int32),
+            VMEM((1, n), jnp.int32),
+            VMEM(router.shape, BF16),
+            pltpu.SemaphoreType.DMA((4,)),
+        ],
         compiler_params=pltpu.CompilerParams(vmem_limit_bytes=16 * MIB),
         name="dispatch_rows",
     )(rows, ids.T, targets.reshape(1, n), router)
@@ -172,91 +197,128 @@
     )(r, rank, gate, spot)
 
 
-def join_kernel(landed_ref, stream_ref, o_ref):
+def join_kernel(landed_ref, stream_ref, keep_ref, give_ref):
+    core = lax.rem(lax.axis_index("head"), 2)
     tokens, w = stream_ref.shape
+    half = tokens // 2
     tail = landed_ref[:, w:].astype(F32)
     spot = tail[:, 0:1] * 16.0 + tail[:, 1:2]
     count = landed_ref.shape[0]
     hit = jnp.where(spot == iota((count, tokens), 1).astype(F32), 1.0, 0.0).astype(BF16)
     added = lax.dot_general(hit, landed_ref[:, :w], (((0,), (0,)), ((), ())), preferred_element_type=F32)
-    o_ref[...] = (stream_ref[...].astype(F32) + added).astype(BF16)
+    joined = stream_ref[...].astype(F32) + added
+    keep_ref[...] = jnp.where(core == 0, joined[:half], joined[half:]).astype(BF16)
+    give_ref[...] = jnp.where(core == 0, joined[half:], joined[:half]).astype(BF16)
 
 
 def join(landed, stream):
+    part = jax.ShapeDtypeStruct((stream.shape[0] // 2, stream.shape[1]), BF16)
     return pl.pallas_call(
         join_kernel,
-        out_shape=jax.ShapeDtypeStruct(stream.shape, BF16),
+        out_shape=[part, part],
         compiler_params=pltpu.CompilerParams(vmem_limit_bytes=16 * MIB),
         name="join_rows",
     )(landed, stream)
 
 
-def qkv_kernel(place_ref, *refs):
-    x_refs = refs[:8]
-    gain_ref, wq_ref, wkv_ref, qg_ref, kg_ref, cos_ref, sin_ref, low_ref, high_ref, kv_ref, norm_s = refs[8:]
-    z = place_ref[1]
-    core = place_ref[2]
-    tokens, w = x_refs[0].shape
+def turning_tables(tokens, shards):
+    frequency = THETA ** (-np.arange(HD // 2, dtype=np.float64) * 2.0 / HD)
+
+    def table(positions):
+        angles = np.asarray(positions, np.float64)[:, None] * np.concatenate([frequency, frequency])[None, :]
+        return np.stack([np.cos(angles), np.sin(angles)]).astype(np.float32)
+
+    return table(np.arange(tokens)), table(np.arange(shards) * tokens)
+
+
+def turned(vectors, gains, near, far, shard):
+    mean = jnp.mean(vectors * vectors, -1, keepdims=True)
+    vectors = vectors * lax.rsqrt(mean + EPSILON) * gains
+    far_cos = far[0][pl.ds(shard, 1), :]
+    far_sin = far[1][pl.ds(shard, 1), :]
+    cos = near[0] * far_cos - near[1] * far_sin
+    sin = near[1] * far_cos + near[0] * far_sin
+    sign = jnp.where(iota((1, HD), 1) < HD // 2, -1.0, 1.0)
+    return vectors * cos + pltpu.roll(vectors, HD // 2, 1) * (sin * sign)
+
+
+def keys_kernel(x0, x1, x2, x3, gain_ref, kg_ref, wk_hbm, wv_hbm, near_ref, far_ref, kv_ref, norm_ref, wkv_ref, sems):
+    ctx = lax.axis_index("ctx")
+    head = lax.axis_index("head")
+    z = head // 2
+    core = lax.rem(head, 2)
+    x_refs = (x0, x1, x2, x3)
+    columns = pl.ds(pl.multiple_of(z * HD, HD), HD)
+    loads = start_loads(
+        [(wk_hbm.at[:, columns], wkv_ref.at[:, :HD]), (wv_hbm.at[:, columns], wkv_ref.at[:, HD:])], sems
+    )
+    _, half, w = x0.shape
     width = 8 * w
-    square = jnp.zeros((tokens, 1), F32)
+    square = jnp.zeros((half, 1), F32)
     for x_ref in x_refs:
-        x = x_ref[...].astype(F32)
-        square = square + jnp.sum(x * x, 1, keepdims=True)
+        for j in range(2):
+            x = x_ref[j].astype(F32)
+            square = square + jnp.sum(x * x, 1, keepdims=True)
     scale = lax.rsqrt(square * (1.0 / width) + EPSILON)
-    half = tokens // 2
-    start = pl.multiple_of(core * half, half)
     for i, x_ref in enumerate(x_refs):
-        block = 2 * lax.rem(z + 4 - i % 4, 4) + (core if i < 4 else 1 - core)
-        norm = (x_ref[...].astype(F32) * scale * gain_ref[pl.ds(block, 1), :]).astype(BF16)
-        norm_s[:, pl.ds(pl.multiple_of(block * w, w), w)] = norm
-    both = dot(norm_s[pl.ds(start, half), :], wkv_ref[...])
-    queries = dot(norm_s[...], wq_ref[...])
-
-    def finished(vectors, gains, cos, sin):
-        mean = jnp.mean(vectors * vectors, -1, keepdims=True)
-        vectors = vectors * lax.rsqrt(mean + EPSILON) * gains
-        return vectors * cos + pltpu.roll(vectors, HD // 2, 1) * sin
-
-    cos_k = cos_ref[pl.ds(start, half), :]
-    sin_k = sin_ref[pl.ds(start, half), :]
-    kv_ref[:, :HD] = finished(both[:, :HD], kg_ref[...], cos_k, sin_k).astype(BF16)
+        for j in range(2):
+            block = 2 * lax.rem(z + 4 - i, 4) + (core if j == 0 else 1 - core)
+            norm = (x_ref[j].astype(F32) * scale * gain_ref[:, pl.ds(pl.multiple_of(block * w, w), w)]).astype(BF16)
+            norm_ref[:, pl.ds(pl.multiple_of(block * w, w), w)] = norm
+    for load in loads:
+        load.wait()
+    both = dot(norm_ref[...], wkv_ref[...])
+    shard = jnp.where(core == 0, ctx, far_ref.shape[1] - 1 - ctx)
+    near = [jnp.where(core == 0, near_ref[t, :half], near_ref[t, half:]) for t in range(2)]
+    far = [far_ref.at[0], far_ref.at[1]]
+    kv_ref[:, :HD] = turned(both[:, :HD], kg_ref[pl.ds(z, 1), :], near, far, shard).astype(BF16)
     kv_ref[:, HD:] = both[:, HD:].astype(BF16)
+
+
+def project_keys(blocks, row_gain, key_gain, w_key, w_value, near, far):
+    _, half, w = blocks[0].shape
+    return pl.pallas_call(
+        keys_kernel,
+        in_specs=[pl.BlockSpec(memory_space=VMEM)] * 6
+        + [pl.BlockSpec(memory_space=pltpu.HBM)] * 2
+        + [pl.BlockSpec(memory_space=VMEM)] * 2,
+        out_shape=[jax.ShapeDtypeStruct((half, 2 * HD), BF16), jax.ShapeDtypeStruct((half, 8 * w), BF16)],
+        scratch_shapes=[VMEM((w_key.shape[0], 2 * HD), BF16), pltpu.SemaphoreType.DMA((2,))],
+        compiler_params=pltpu.CompilerParams(vmem_limit_bytes=16 * MIB),
+        name="project_keys",
+    )(*blocks, row_gain, key_gain, w_key, w_value, near, far)
+
+
+def queries_kernel(own_ref, other_ref, wq_ref, qg_ref, near_ref, far_ref, low_ref, high_ref):
+    ctx = lax.axis_index("ctx")
+    core = lax.rem(lax.axis_index("head"), 2)
+    half = own_ref.shape[0]
     factor = math.log2(math.e) / math.sqrt(HD)
-    cos = cos_ref[...]
-    sin = sin_ref[...]
-    for h in range(low_ref.shape[0]):
-        part = slice(h * HD, (h + 1) * HD)
-        done = (finished(queries[:, part], qg_ref[:, part], cos, sin) * factor).astype(BF16)
-        low_ref[h] = done[:half]
-        high_ref[h] = done[half:]
-
-
-def project(place, blocks, row_gain, w_query, w_kv, q_gain, key_gain, cos, sin):
-    tokens, w = blocks[0].shape
+    far = [far_ref.at[0], far_ref.at[1]]
+    for upper, o_ref in enumerate((low_ref, high_ref)):
+        norm = jnp.where(core == upper, own_ref[...], other_ref[...])
+        queries = dot(norm, wq_ref[...])
+        shard = ctx if upper == 0 else far_ref.shape[1] - 1 - ctx
+        near = [near_ref[t, upper * half : (upper + 1) * half] for t in range(2)]
+        for h in range(o_ref.shape[0]):
+            part = slice(h * HD, (h + 1) * HD)
+            o_ref[h] = (turned(queries[:, part], qg_ref[:, part], near, far, shard) * factor).astype(BF16)
+
+
+def project_queries(own, other, w_query, q_gain, near, far):
     heads = w_query.shape[1] // HD
-    part = jax.ShapeDtypeStruct((heads, tokens // 2, HD), BF16)
-    return pl.pallas_call(
-        qkv_kernel,
-        in_specs=[pl.BlockSpec(memory_space=pltpu.SMEM)] + [pl.BlockSpec(memory_space=VMEM)] * 15,
-        out_shape=[part, part, jax.ShapeDtypeStruct((tokens // 2, 2 * HD), BF16)],
-        scratch_shapes=[VMEM((tokens, 8 * w), BF16)],
-        compiler_params=pltpu.CompilerParams(vmem_limit_bytes=20 * MIB),
-        name="project_qkv",
-    )(
-        place,
-        *blocks,
-        row_gain,
-        w_query,
-        w_kv,
-        q_gain.reshape(1, -1),
-        key_gain,
-        cos,
-        sin,
-    )
-
-
-def attend_kernel(place_ref, low_ref, high_ref, kv_ref, o_ref, value_s):
-    core = place_ref[2]
+    part = jax.ShapeDtypeStruct((heads, own.shape[0], HD), BF16)
+    return pl.pallas_call(
+        queries_kernel,
+        out_shape=[part, part],
+        compiler_params=pltpu.CompilerParams(vmem_limit_bytes=16 * MIB),
+        name="project_queries",
+    )(own, other, w_query, q_gain.reshape(1, -1), near, far)
+
+
+def attend_kernel(low_ref, high_ref, kv_ref, o_ref, value_s):
+    ctx = lax.axis_index("ctx")
+    core = lax.rem(lax.axis_index("head"), 2)
     shards, shard, _ = kv_ref.shape
     heads, half, _ = low_ref.shape
     group = 4
@@ -267,19 +329,21 @@
     value_s[:, :, HD:] = jnp.ones((shards, shard, HD), BF16)
 
     for upper, q_ref in enumerate((low_ref, high_ref)):
-        own = place_ref[0] if upper == 0 else shards - 1 - place_ref[0]
+        own = ctx if upper == 0 else shards - 1 - ctx
         queries = q_ref[...].reshape(heads * half, HD)
         pieces = [queries[i * rows : (i + 1) * rows] for i in range(subs)]
 
         def fold(carry, chunk, masked):
-            keys = kv_ref[pl.ds(chunk * group, group), :, :HD].reshape(span, HD)
-            values = value_s[pl.ds(chunk * group, group)].reshape(span, 2 * HD)
+            first = jnp.where(core == 0, chunk, shards // group - 1 - chunk) * group
+            keys = kv_ref[pl.ds(first, group), :, :HD].reshape(span, HD)
+            values = value_s[pl.ds(first, group)].reshape(span, 2 * HD)
             every = [dot_t(piece, keys) for piece in pieces]
             result = []
             for (highest, weighted), scores in zip(carry, every):
                 if masked:
                     t = iota((rows, span), 1)
-                    key_pos = (chunk * group + t // shard) * (2 * shard) + core * shard + t % shard
+                    place = first + t // shard
+                    key_pos = jnp.where(core == 0, place, shards - 1 - place) * (2 * shard) + core * shard + t % shard
                     query_pos = own * (2 * half) + upper * half + iota((rows, span), 0) % half
                     allowed = query_pos >= key_pos
                     scores = jnp.where(allowed, scores, NEG)
@@ -303,19 +367,30 @@
             o_ref[part, upper * half : (upper + 1) * half, HD:] = stats.reshape(heads // subs, half, HD)
 
 
-def attend(place, low, high, kv):
+def attend(low, high, kv):
     heads, half, _ = low.shape
     return pl.pallas_call(
         attend_kernel,
-        in_specs=[pl.BlockSpec(memory_space=pltpu.SMEM)] + [pl.BlockSpec(memory_space=VMEM)] * 3,
         out_shape=jax.ShapeDtypeStruct((heads, 2 * half, 2 * HD), F32),
         scratch_shapes=[VMEM(kv.shape, BF16)],
         compiler_params=pltpu.CompilerParams(vmem_limit_bytes=28 * MIB),
         name="attend",
-    )(place, low, high, kv)
-
-
-def merge_kernel(place_ref, own_ref, other_ref, w_ref, att_ref, o_ref):
+    )(low, high, kv)
+
+
+def project_blocks(attended, core, w_ref, o_ref):
+    z = lax.axis_index("head") // 2
+    w = o_ref.shape[3]
+    for i in range(o_ref.shape[0]):
+        for j in range(2):
+            block = 2 * lax.rem(z + i, 4) + (core if j == 0 else 1 - core)
+            o_ref[i, j] = dot(attended, w_ref[:, pl.ds(pl.multiple_of(block * w, w), w)]).astype(BF16)
+
+
+def merge_kernel(own_ref, other_ref, w_ref, keep_ref, o_ref):
+    core = lax.rem(lax.axis_index("head"), 2)
+    half = keep_ref.shape[0]
+    given = []
     for h in range(own_ref.shape[0]):
         m0 = own_ref[h, :, HD : HD + 1]
         m1 = other_ref[h, :, HD : HD + 1]
@@ -325,43 +400,35 @@
         total = own_ref[h, :, 2 * HD - 1 :] * e0 + other_ref[h, :, 2 * HD - 1 :] * e1
         share = 1.0 / total
         value = own_ref[h, :, :HD] * (e0 * share) + other_ref[h, :, :HD] * (e1 * share)
-        att_ref[:, h * HD : (h + 1) * HD] = value.astype(BF16)
-    project_blocks(place_ref[1], 1 - place_ref[2], att_ref, w_ref, o_ref)
-
-
-def project_blocks(z, core, att_ref, w_ref, o_ref):
-    w = o_ref.shape[2]
-    for i in range(o_ref.shape[0]):
-        block = 2 * lax.rem(z + i, 4) + core
-        o_ref[i] = dot(att_ref[...], w_ref[:, pl.ds(pl.multiple_of(block * w, w), w)]).astype(BF16)
-
-
-def own_kernel(place_ref, att_ref, w_ref, o_ref):
-    project_blocks(place_ref[1], place_ref[2], att_ref, w_ref, o_ref)
-
-
-def merge_and_project(place, own, other, w_out):
+        keep_ref[:, h * HD : (h + 1) * HD] = jnp.where(core == 0, value[:half], value[half:]).astype(BF16)
+        given.append(jnp.where(core == 0, value[half:], value[:half]).astype(BF16))
+    project_blocks(jnp.concatenate(given, 1), 1 - core, w_ref, o_ref)
+
+
+def own_kernel(attended_ref, w_ref, o_ref):
+    project_blocks(attended_ref[...], lax.rem(lax.axis_index("head"), 2), w_ref, o_ref)
+
+
+def merge_and_project(own, other, w_out):
     heads, tokens, _ = own.shape
     return pl.pallas_call(
         merge_kernel,
-        in_specs=[pl.BlockSpec(memory_space=pltpu.SMEM)] + [pl.BlockSpec(memory_space=VMEM)] * 3,
         out_shape=[
-            jax.ShapeDtypeStruct((tokens, heads * HD), BF16),
-            jax.ShapeDtypeStruct((4, tokens, w_out.shape[1] // 8), BF16),
+            jax.ShapeDtypeStruct((tokens // 2, heads * HD), BF16),
+            jax.ShapeDtypeStruct((4, 2, tokens // 2, w_out.shape[1] // 8), BF16),
         ],
         compiler_params=pltpu.CompilerParams(vmem_limit_bytes=16 * MIB),
         name="merge_and_project",
-    )(place, own, other, w_out)
-
-
-def project_own(place, attended, w_out):
+    )(own, other, w_out)
+
+
+def project_own(attended, w_out):
     return pl.pallas_call(
         own_kernel,
-        in_specs=[pl.BlockSpec(memory_space=pltpu.SMEM)] + [pl.BlockSpec(memory_space=VMEM)] * 2,
-        out_shape=jax.ShapeDtypeStruct((4, attended.shape[0], w_out.shape[1] // 8), BF16),
+        out_shape=jax.ShapeDtypeStruct((4, 2, attended.shape[0], w_out.shape[1] // 8), BF16),
         compiler_params=pltpu.CompilerParams(vmem_limit_bytes=16 * MIB),
         name="project_own",
-    )(place, attended, w_out)
+    )(attended, w_out)
 
 
 def body(
@@ -381,69 +448,55 @@
     w_value,
     w_out,
 ):
-    ctx = lax.axis_index("ctx")
-    head = lax.axis_index("head")
-    z = head // 2
-    core = head % 2
-    place = jnp.stack([ctx, z, core]).astype(jnp.int32)
+    core = lax.axis_index("head") % 2
     experts = router.shape[1]
     tokens, w = stream.shape
     partner = [(i, i ^ 1) for i in range(8)]
-    mirror = [(i, 15 - i) for i in range(16)]
+
+    def to_partner(shard):
+        return lax.ppermute(shard, "head", partner)
 
     def along(shard, hops):
-        return lax.ppermute(shard, "head", [(i, (i + 2 * hops) % 8) for i in range(8)])
+        pairs = []
+        for c in range(16):
+            for h in range(8):
+                there = c if h % 2 == 0 else 15 - c
+                pairs.append((c * 8 + h, there * 8 + (h + 2 * hops) % 8))
+        return lax.ppermute(shard, ("ctx", "head"), pairs)
 
     def everywhere(blocks):
         return lax.all_to_all(blocks, ("ctx", "head"), split_axis=0, concat_axis=0, tiled=True)
-
-    half_dim = HD // 2
-    frequency = jnp.power(jnp.float32(THETA), -jnp.arange(half_dim, dtype=F32) * 2.0 / HD)
-    positions = ctx * tokens + jnp.arange(tokens, dtype=jnp.int32)
-    angles = positions.astype(F32)[:, None] * frequency[None, :]
-    cosines = jnp.cos(angles)
-    sines = jnp.sin(angles)
-    cos = jnp.concatenate([cosines, cosines], 1)
-    sin = jnp.concatenate([-sines, sines], 1)
 
     outgoing, rank, gate, spot = dispatch(branch_rows, expert_ids, targets, router)
     shape = (experts, 8, outgoing.shape[1])
     arrived = everywhere(outgoing.reshape(shape)).reshape(outgoing.shape)
-    first_column = z * HD
-    w_kv = jnp.concatenate([lax.dynamic_slice_in_dim(w, first_column, HD, 1) for w in (w_key, w_value)], 1)
-    key_gain = lax.dynamic_slice_in_dim(k_gain, first_column, HD, 0).reshape(1, HD)
-    row_gain = attn_gain.reshape(8, w)
-    early = (arrived, cos, sin, w_kv, key_gain, row_gain, place)
-    arrived, cos, sin, w_kv, key_gain, row_gain, place = lax.optimization_barrier(early)
     produced = run_expert(arrived, w_gate[0], w_up[0], w_down[0])
     returned = everywhere(produced.reshape(shape)).reshape(outgoing.shape)
     parcels = combine(returned, rank, gate, spot)
     landed = everywhere(parcels.reshape(experts, 8, parcels.shape[3])).reshape(experts * 8, parcels.shape[3])
-    joined = join(landed, stream)
-
-    mine = [joined] + [along(joined, hops) for hops in (1, 2, 3)]
-    blocks = mine + [lax.ppermute(block, "head", partner) for block in mine]
-    low, high, kv = project(place, blocks, row_gain, w_query, w_kv, q_gain, key_gain, cos, sin)
+    keep, give = join(landed, stream)
+
+    mine = jnp.stack([keep, to_partner(give)])
+    blocks = [along(mine, hops) for hops in range(4)]
+    near, far = turning_tables(tokens, 16)
+    kv, norm = project_keys(blocks, attn_gain.reshape(1, -1), k_gain.reshape(KVH, HD), w_key, w_value, near, far)
     all_kv = lax.all_to_all(
         jnp.broadcast_to(kv[None], (16, *kv.shape)), "ctx", split_axis=0, concat_axis=0, tiled=True
     )
-    high = lax.ppermute(high, "ctx", mirror)
-    partner_low = lax.ppermute(low, "head", partner)
-    partner_high = lax.ppermute(high, "head", partner)
-    for_partner = attend(place, partner_low, partner_high, all_kv)
-    from_partner = lax.ppermute(for_partner, "head", partner)
-    folded = attend(place, low, high, all_kv)
-    attended, sent = merge_and_project(place, folded, from_partner, w_out)
-    received = lax.ppermute(sent, "head", partner)
-    kept = project_own(place, attended, w_out)
-    pair = [(kept[i].astype(F32) + received[i].astype(F32)).astype(BF16) for i in range(4)]
-    total = pair[0].astype(F32)
-    for hops in (1, 2, 3):
-        total = total + along(pair[hops], hops).astype(F32)
-    half = tokens // 2
-    upper = lax.ppermute(total[half:].astype(BF16), "ctx", mirror)
-    summed = jnp.concatenate([total[:half], upper.astype(F32)], 0)
-    return (joined.astype(F32) + summed).astype(BF16)
+    low, high = project_queries(norm, to_partner(norm), w_query, q_gain, near, far)
+    for_partner = attend(to_partner(low), to_partner(high), all_kv)
+    from_partner = to_partner(for_partner)
+    folded = attend(low, high, all_kv)
+    attended, sent = merge_and_project(folded, from_partner, w_out)
+    received = to_partner(sent)
+    kept = project_own(attended, w_out)
+    total = mine.astype(F32)
+    for hops in range(4):
+        pair = (kept[hops].astype(F32) + received[hops].astype(F32)).astype(BF16)
+        total = total + along(pair, hops).astype(F32)
+    total = total.astype(BF16)
+    other = to_partner(total[1])
+    return jnp.where(core == 0, jnp.concatenate([total[0], other], 0), jnp.concatenate([other, total[0]], 0))
 
 
 def solution(mesh):

time: 351 us -> 323 us (0.920)
  waiting for transfers between devices: 132 us -> 40.2 us
  blocking collectives: 104 us -> 187 us
  Pallas kernels: 55.5 us -> 48.8 us
  local copies, waits for them, and re-layouts: 14.7 us -> 8.89 us
  starting transfers between devices: 37.1 us -> 32.9 us
    all_to_all x2 -> x3, blocking collectives: 104 us -> 187 us  [everywhere(): lax.all_to_all(blocks, ('ctx', 'head'), split_axis=0, concat_axis=0, tile...]
    all_to_all x1 -> x0, waiting for transfers between devices: 73.7 us -> none  [everywhere(): lax.all_to_all(blocks, ('ctx', 'head'), split_axis=0, concat_axis=0, tile...]
    ppermute x16 -> x15, waiting for transfers between devices: 58.5 us -> 23.4 us  [the longest x8 15.3 us: along(): return lax.ppermute(shard, ('ctx', 'head'), pairs)]
    all_to_all x1, waiting for transfers between devices: 0.01 us -> 16.8 us  [body(): lax.all_to_all(jnp.broadcast_to(kv[None], (16, *kv.shape)), 'ctx', split_...]
    all_to_all x1 -> x0, starting transfers between devices: 12.1 us -> none  [everywhere(): lax.all_to_all(blocks, ('ctx', 'head'), split_axis=0, concat_axis=0, tile...]
    ppermute x16 -> x15, starting transfers between devices: 21.3 us -> 29.1 us  [the longest x8 26.4 us: along(): return lax.ppermute(shard, ('ctx', 'head'), pairs)]
    unnamed x30 -> x38, local copies, waits for them, and re-layouts: 11.8 us -> 7.3 us
    pallas_call x7 -> x8, Pallas kernels: 32.7 us -> 29.2 us  [the longest x2 18.6 us: attend(): pl.pallas_call(attend_kernel, out_shape=jax.ShapeDtypeStruct((heads, 2 *...]
  transfers between devices with their start and end apart: 18 -> 16, of which waited for: 9 -> 13; matrix products, arithmetic and copies ran while one was open for 1% -> 0% of each run, Pallas kernels for 3% -> 4%
where the time goes in v3:
time: 323 us; the launch traced here: 320 us
  blocking collectives  187 us (58%)
  Pallas kernels  48.8 us (15%)
  waiting for transfers between devices  40.2 us (12%)
  starting transfers between devices  32.9 us (10%)
  local copies, waits for them, and re-layouts  8.89 us (3%)
    all_to_all x3, blocking collectives, everywhere(): lax.all_to_all(blocks, ('ctx', 'head'), split_axis=0, concat_axis=0, tile...  187 us
    ppermute x8, starting transfers between devices, along(): return lax.ppermute(shard, ('ctx', 'head'), pairs)  26.4 us
    pallas_call x2, Pallas kernels, attend(): pl.pallas_call(attend_kernel, out_shape=jax.ShapeDtypeStruct((heads, 2 *...  18.6 us
    pallas_call x1, Pallas kernels, run_expert(): pl.pallas_call(expert_kernel, out_shape=jax.ShapeDtypeStruct(y.shape, BF1...  16.9 us
    all_to_all x1, waiting for transfers between devices, body(): lax.all_to_all(jnp.broadcast_to(kv[None], (16, *kv.shape)), 'ctx', split_...  16.8 us
    ppermute x8, waiting for transfers between devices, along(): return lax.ppermute(shard, ('ctx', 'head'), pairs)  15.3 us
    ppermute x7, waiting for transfers between devices, to_partner(): return lax.ppermute(shard, 'head', partner)  8.1 us
    unnamed x38, local copies, waits for them, and re-layouts  7.3 us
  transfers between devices with their start and end apart: 16, of which 13 were waited for; matrix products, arithmetic and copies ran while one was open for 0% of the time, Pallas kernels for 4%

profile of v3, /device:TPU:1, one launch (start us, length us, event | category | flops | bytes accessed | tf_op | source)
XLA Modules:
  0.0 319.6 jit_solution(5840191206907836868)
XLA Ops:
  3.4 4.0 %dispatch_rows.1 = (bf16[1024,3072]{1,0:T(8,128)(2,1)S(1)}, f32[128,128]{1,0:T(8,128)S(1)}, f32[128,128]{1,0:T(8,128)S(1)}, f32[128,128]{1,0:T(8,128)S(1)}) custom-call(bf16[128,2048]{1,0:T(8,128)(2,1)S(1)} %copy-done.10, s32[8,128]{1,0:T(8,128)S(1)} %bitcast.40, s32[1,128]{1,0:T(1,128)S(1)} %bitcast.43, bf16[2048,128]{1,0:T(8,128)(2,1)S(1)} %copy-done.11), custom_call_target="tpu_custom_call" | custom-call | tf_op jit(solution)/shard_map/dispatch_rows/pallas_call | solution.py:95
  7.4 86.5 %all_to_all.20 = bf16[128,8,3072]{2,1,0:T(8,128)(2,1)S(1)} all-to-all(bf16[128,8,3072]{2,1,0:T(8,128)(2,1)S(1)} %bitcast.31), channel_id=1, replica_groups=mesh['ctx'=16,'head'=8] {'ctx','head'}, dimensions={0} | all-to-all | bytes 12582912 | tf_op jit(solution)/shard_map/all_to_all | solution.py:468
  93.9 16.9 %expert_ffn.1 = bf16[1024,3072]{1,0:T(8,128)(2,1)S(1)} custom-call(bf16[1024,3072]{1,0:T(8,128)(2,1)S(1)} %bitcast.29, bf16[2048,768]{1,0:T(8,128)(2,1)S(1)} %bitcast.34, bf16[2048,768]{1,0:T(8,128)(2,1)S(1)} %bitcast.35, bf16[768,2048]{1,0:T(8,128)(2,1)S(1)} %bitcast.36), custom_call_target="tpu_custom_call" | custom-call | tf_op jit(solution)/shard_map/expert_ffn/pallas_call | solution.py:145
  110.8 79.7 %all_to_all.21 = bf16[128,8,3072]{2,1,0:T(8,128)(2,1)S(1)} all-to-all(bf16[128,8,3072]{2,1,0:T(8,128)(2,1)S(1)} %bitcast.30), channel_id=1, replica_groups=mesh['ctx'=16,'head'=8] {'ctx','head'}, dimensions={0} | all-to-all | bytes 12582912 | tf_op jit(solution)/shard_map/all_to_all | solution.py:468
  190.5 2.7 combine_rows.1
  193.3 20.8 %all_to_all.22 = bf16[128,8,384]{2,1,0:T(8,128)(2,1)S(1)} all-to-all(bf16[128,8,384]{2,1,0:T(8,128)(2,1)S(1)} %bitcast.32), channel_id=1, replica_groups=mesh['ctx'=16,'head'=8] {'ctx','head'}, dimensions={0} | all-to-all | bytes 1572864 | tf_op jit(solution)/shard_map/all_to_all | solution.py:468
  217.2 2.8 collective-permute-start.1
  220.1 3.6 %collective-permute-start.2 = (bf16[2,256,256]{2,1,0:T(8,128)(2,1)S(1)}, bf16[2,256,256]{2,1,0:T(8,128)(2,1)S(1)}, u32[]{:S(2)}, u32[]{:S(2)}) collective-permute-start(bf16[2,256,256]{2,1,0:T(8,128)(2,1)S(1)} %pad_maximum_fusion), channel_id=1, source_target_pairs={{0,2},{1,123},{2,4},{3,125},{4,6},{5,127},{6,0},{7,121},{8,10},{9,... | collective-permute-start | bytes 786440 | tf_op jit(solution)/shard_map/ppermute | solution.py:465
  223.6 2.6 collective-permute-start.3
  226.3 3.6 %collective-permute-start.4 = (bf16[2,256,256]{2,1,0:T(8,128)(2,1)S(1)}, bf16[2,256,256]{2,1,0:T(8,128)(2,1)S(1)}, u32[]{:S(2)}, u32[]{:S(2)}) collective-permute-start(bf16[2,256,256]{2,1,0:T(8,128)(2,1)S(1)} %pad_maximum_fusion), channel_id=1, source_target_pairs={{0,6},{1,127},{2,0},{3,121},{4,2},{5,123},{6,4},{7,125},{8,14},{9,... | collective-permute-start | bytes 786440 | tf_op jit(solution)/shard_map/ppermute | solution.py:465
  230.8 3.8 %collective-permute-done.3.x2 = bf16[2,256,256]{2,1,0:T(8,128)(2,1)S(1)} collective-permute-done((bf16[2,256,256]{2,1,0:T(8,128)(2,1)S(1)}, bf16[2,256,256]{2,1,0:T(8,128)(2,1)S(1)}, u32[]{:S(2)}, u32[]{:S(2)}) %collective-permute-start.3) | collective-permute-done | bytes 262176 | tf_op jit(solution)/shard_map/ppermute | solution.py:465
  234.6 3.8 %collective-permute-done.4.x3 = bf16[2,256,256]{2,1,0:T(8,128)(2,1)S(1)} collective-permute-done((bf16[2,256,256]{2,1,0:T(8,128)(2,1)S(1)}, bf16[2,256,256]{2,1,0:T(8,128)(2,1)S(1)}, u32[]{:S(2)}, u32[]{:S(2)}) %collective-permute-start.4) | collective-permute-done | bytes 262176 | tf_op jit(solution)/shard_map/ppermute | solution.py:465
  242.5 3.8 %all-to-all-start.3 = ((bf16[16,256,256]{2,1,0:T(8,128)(2,1)}), bf16[16,256,256]{2,1,0:T(8,128)(2,1)S(1)}, u32[]{:S(2)}, u32[]{:S(2)}) async-start(bf16[16,256,256]{2,1,0:T(8,128)(2,1)} %broadcast_in_dim.2), calls=%async_computation.3 | async-start | bytes 4194304 | tf_op jit(solution)/shard_map/all_to_all | solution.py:483
  246.5 2.9 collective-permute-done.5.other_ref
  255.7 16.8 %all-to-all-done.3.kv_ref = bf16[16,256,256]{2,1,0:T(8,128)(2,1)S(1)} async-done(((bf16[16,256,256]{2,1,0:T(8,128)(2,1)}), bf16[16,256,256]{2,1,0:T(8,128)(2,1)S(1)}, u32[]{:S(2)}, u32[]{:S(2)}) %all-to-all-start.3) | async-done | bytes 2097184 | tf_op jit(solution)/shard_map/all_to_all | solution.py:483
  272.5 9.4 %attend.3 = f32[4,512,256]{2,1,0:T(8,128)S(1)} custom-call(bf16[4,256,128]{2,1,0:T(8,128)(2,1)S(1)} %collective-permute-done.6.low_ref, bf16[4,256,128]{2,1,0:T(8,128)(2,1)S(1)} %collective-permute-done.7.high_ref, bf16[16,256,256]{2,1,0:T(8,128)(2,1)S(1)} %all-to-all-done.3.kv_ref), custom_call_target="tpu_custom_call" | custom-call | tf_op jit(solution)/shard_map/attend/pallas_call | solution.py:372
  282.0 9.2 %attend.2.own_ref = f32[4,512,256]{2,1,0:T(8,128)S(1)} custom-call(bf16[4,256,128]{2,1,0:T(8,128)(2,1)S(1)} %get-tuple-element.24.low_ref, bf16[4,256,128]{2,1,0:T(8,128)(2,1)S(1)} %get-tuple-element.25.high_ref, bf16[16,256,256]{2,1,0:T(8,128)(2,1)S(1)} %all-to-all-done.3.kv_ref), custom_call_target="tpu_custom_call" | custom-call | tf_op jit(solution)/shard_map/attend/pallas_call | solution.py:372
  291.2 2.1 merge_and_project.1
  296.4 2.4 collective-permute-start.10
  298.8 4.4 %collective-permute-start.11 = (bf16[2,256,256]{2,1,0:T(8,128)(2,1)S(1)}, bf16[2,256,256]{2,1,0:T(8,128)(2,1)S(1)}, u32[]{:S(2)}, u32[]{:S(2)}) collective-permute-start(bf16[2,256,256]{2,1,0:T(8,128)(2,1)S(1)} %get-tuple-element.32), channel_id=1, source_target_pairs={{0,2},{1,123},{2,4},{3,125},{4,6},{5,127},{6,0},{7,121},{8,10},{9,... | collective-permute-start | bytes 786440 | tf_op jit(solution)/shard_map/ppermute | solution.py:465
  303.2 2.7 collective-permute-start.12
  305.9 4.3 %collective-permute-start.13 = (bf16[2,256,256]{2,1,0:T(8,128)(2,1)S(1)}, bf16[2,256,256]{2,1,0:T(8,128)(2,1)S(1)}, u32[]{:S(2)}, u32[]{:S(2)}) collective-permute-start(bf16[2,256,256]{2,1,0:T(8,128)(2,1)S(1)} %get-tuple-element.30), channel_id=1, source_target_pairs={{0,6},{1,127},{2,0},{3,121},{4,2},{5,123},{6,4},{7,125},{8,14},{9,... | collective-permute-start | bytes 786440 | tf_op jit(solution)/shard_map/ppermute | solution.py:465
  311.2 2.9 collective-permute-done.12
  314.2 2.8 collective-permute-done.13
  (65 shorter events, 24.7 us)
Async XLA Ops:
  7.4 86.5 %copy-start.1 = (bf16[1,2048,768]{2,1,0:T(8,128)(2,1)S(1)}, bf16[1,2048,768]{2,1,0:T(8,128)(2,1)}, u32[]{:S(2)}) copy-start(bf16[1,2048,768]{2,1,0:T(8,128)(2,1)} %param.21) | copy-start | bytes 9437188
  7.4 86.5 %copy-start.2 = (bf16[1,2048,768]{2,1,0:T(8,128)(2,1)S(1)}, bf16[1,2048,768]{2,1,0:T(8,128)(2,1)}, u32[]{:S(2)}) copy-start(bf16[1,2048,768]{2,1,0:T(8,128)(2,1)} %param.22) | copy-start | bytes 9437188
  7.4 86.5 %copy-start.3 = (bf16[1,768,2048]{2,1,0:T(8,128)(2,1)S(1)}, bf16[1,768,2048]{2,1,0:T(8,128)(2,1)}, u32[]{:S(2)}) copy-start(bf16[1,768,2048]{2,1,0:T(8,128)(2,1)} %param.23) | copy-start | bytes 9437188
  190.5 47.8 %copy-start.6 = (bf16[2048,512]{1,0:T(8,128)(2,1)S(1)}, bf16[2048,512]{1,0:T(8,128)(2,1)}, u32[]{:S(2)}) copy-start(bf16[2048,512]{1,0:T(8,128)(2,1)} %wv_hbm.1) | copy-start | bytes 6291460
  193.2 45.2 %copy-start.5 = (bf16[2048,512]{1,0:T(8,128)(2,1)S(1)}, bf16[2048,512]{1,0:T(8,128)(2,1)}, u32[]{:S(2)}) copy-start(bf16[2048,512]{1,0:T(8,128)(2,1)} %wk_hbm.1) | copy-start | bytes 6291460
  193.2 45.2 %copy-start.7 = (f32[2,512,128]{2,1,0:T(8,128)S(1)}, f32[2,512,128]{2,1,0:T(8,128)}, u32[]{:S(2)}) copy-start(f32[2,512,128]{2,1,0:T(8,128)} %constant.22.clone.near_ref) | copy-start | bytes 1572868
  193.2 45.2 %copy-start.13 = (f32[2,16,128]{2,1,0:T(8,128)S(1)}, f32[2,16,128]{2,1,0:T(8,128)}, u32[]{:S(2)}) copy-start(f32[2,16,128]{2,1,0:T(8,128)} %constant.23.clone.far_ref) | copy-start | bytes 49156
  193.3 45.2 %copy-start.14 = (f32[2048]{0:T(1024)S(1)}, f32[2048]{0:T(1024)}, u32[]{:S(2)}) copy-start(f32[2048]{0:T(1024)} %param.25) | copy-start | bytes 24580
  214.9 2.3 collective-permute-start
  217.2 12.7 %collective-permute-start.1 = (bf16[2,256,256]{2,1,0:T(8,128)(2,1)S(1)}, bf16[2,256,256]{2,1,0:T(8,128)(2,1)S(1)}, u32[]{:S(2)}, u32[]{:S(2)}) collective-permute-start(bf16[2,256,256]{2,1,0:T(8,128)(2,1)S(1)} %pad_maximum_fusion), channel_id=1, source_target_pairs={{0,0},{1,121},{2,2},{3,123},{4,4},{5,125},{6,6},{7,127},{8,8},{9,1... | collective-permute-start | bytes 786440 | tf_op jit(solution)/shard_map/ppermute | solution.py:465
  220.1 10.8 %collective-permute-start.2 = (bf16[2,256,256]{2,1,0:T(8,128)(2,1)S(1)}, bf16[2,256,256]{2,1,0:T(8,128)(2,1)S(1)}, u32[]{:S(2)}, u32[]{:S(2)}) collective-permute-start(bf16[2,256,256]{2,1,0:T(8,128)(2,1)S(1)} %pad_maximum_fusion), channel_id=1, source_target_pairs={{0,2},{1,123},{2,4},{3,125},{4,6},{5,127},{6,0},{7,121},{8,10},{9,... | collective-permute-start | bytes 786440 | tf_op jit(solution)/shard_map/ppermute | solution.py:465
  223.6 10.9 %collective-permute-start.3 = (bf16[2,256,256]{2,1,0:T(8,128)(2,1)S(1)}, bf16[2,256,256]{2,1,0:T(8,128)(2,1)S(1)}, u32[]{:S(2)}, u32[]{:S(2)}) collective-permute-start(bf16[2,256,256]{2,1,0:T(8,128)(2,1)S(1)} %pad_maximum_fusion), channel_id=1, source_target_pairs={{0,4},{1,125},{2,6},{3,127},{4,0},{5,121},{6,2},{7,123},{8,12},{9,... | collective-permute-start | bytes 786440 | tf_op jit(solution)/shard_map/ppermute | solution.py:465
  226.3 12.1 %collective-permute-start.4 = (bf16[2,256,256]{2,1,0:T(8,128)(2,1)S(1)}, bf16[2,256,256]{2,1,0:T(8,128)(2,1)S(1)}, u32[]{:S(2)}, u32[]{:S(2)}) collective-permute-start(bf16[2,256,256]{2,1,0:T(8,128)(2,1)S(1)} %pad_maximum_fusion), channel_id=1, source_target_pairs={{0,6},{1,127},{2,0},{3,121},{4,2},{5,123},{6,4},{7,125},{8,14},{9,... | collective-permute-start | bytes 786440 | tf_op jit(solution)/shard_map/ppermute | solution.py:465
  242.5 30.0 %all-to-all-start.3 = ((bf16[16,256,256]{2,1,0:T(8,128)(2,1)}), bf16[16,256,256]{2,1,0:T(8,128)(2,1)S(1)}, u32[]{:S(2)}, u32[]{:S(2)}) async-start(bf16[16,256,256]{2,1,0:T(8,128)(2,1)} %broadcast_in_dim.2), calls=%async_computation.3 | async-start | bytes 4194304 | tf_op jit(solution)/shard_map/all_to_all | solution.py:483
  246.4 3.0 collective-permute-start.5
  253.7 1.6 collective-permute-start.6
  253.9 1.8 collective-permute-start.7
  281.9 9.3 %collective-permute-start.8 = (f32[4,512,256]{2,1,0:T(8,128)S(1)}, f32[4,512,256]{2,1,0:T(8,128)S(1)}, u32[]{:S(2)}, u32[]{:S(2)}) collective-permute-start(f32[4,512,256]{2,1,0:T(8,128)S(1)} %attend.3), channel_id=1, source_target_pairs={{0,1},{1,0},{2,3},{3,2},{4,5},{5,4},{6,7},{7,6},{8,9},{9,8},{10,11... | collective-permute-start | bytes 6291464 | tf_op jit(solution)/shard_map/ppermute | solution.py:457
  293.3 2.9 collective-permute-start.9
  296.4 13.7 %collective-permute-start.10 = (bf16[2,256,256]{2,1,0:T(8,128)(2,1)S(1)}, bf16[2,256,256]{2,1,0:T(8,128)(2,1)S(1)}, u32[]{:S(2)}, u32[]{:S(2)}) collective-permute-start(bf16[2,256,256]{2,1,0:T(8,128)(2,1)S(1)} %get-tuple-element.29), channel_id=1, source_target_pairs={{0,0},{1,121},{2,2},{3,123},{4,4},{5,125},{6,6},{7,127},{8,8},{9,1... | collective-permute-start | bytes 786440 | tf_op jit(solution)/shard_map/ppermute | solution.py:465
  298.8 12.4 %collective-permute-start.11 = (bf16[2,256,256]{2,1,0:T(8,128)(2,1)S(1)}, bf16[2,256,256]{2,1,0:T(8,128)(2,1)S(1)}, u32[]{:S(2)}, u32[]{:S(2)}) collective-permute-start(bf16[2,256,256]{2,1,0:T(8,128)(2,1)S(1)} %get-tuple-element.32), channel_id=1, source_target_pairs={{0,2},{1,123},{2,4},{3,125},{4,6},{5,127},{6,0},{7,121},{8,10},{9,... | collective-permute-start | bytes 786440 | tf_op jit(solution)/shard_map/ppermute | solution.py:465
  303.2 10.9 %collective-permute-start.12 = (bf16[2,256,256]{2,1,0:T(8,128)(2,1)S(1)}, bf16[2,256,256]{2,1,0:T(8,128)(2,1)S(1)}, u32[]{:S(2)}, u32[]{:S(2)}) collective-permute-start(bf16[2,256,256]{2,1,0:T(8,128)(2,1)S(1)} %get-tuple-element.31), channel_id=1, source_target_pairs={{0,4},{1,125},{2,6},{3,127},{4,0},{5,121},{6,2},{7,123},{8,12},{9,... | collective-permute-start | bytes 786440 | tf_op jit(solution)/shard_map/ppermute | solution.py:465
  305.9 11.1 %collective-permute-start.13 = (bf16[2,256,256]{2,1,0:T(8,128)(2,1)S(1)}, bf16[2,256,256]{2,1,0:T(8,128)(2,1)S(1)}, u32[]{:S(2)}, u32[]{:S(2)}) collective-permute-start(bf16[2,256,256]{2,1,0:T(8,128)(2,1)S(1)} %get-tuple-element.30), channel_id=1, source_target_pairs={{0,6},{1,127},{2,0},{3,121},{4,2},{5,123},{6,4},{7,125},{8,14},{9,... | collective-permute-start | bytes 786440 | tf_op jit(solution)/shard_map/ppermute | solution.py:465
  317.2 1.4 collective-permute-start.14
  (11 other events, 92.1 us)

commit v4 on v3

--- a/solution.py
+++ b/solution.py
@@ -40,8 +40,8 @@
 
 
 def dispatch_kernel(
-    rows_hbm, ids_hbm, targets_hbm, router_hbm, y_ref, rank_ref, gate_ref, spot_ref,
-    rows_ref, ids_ref, targets_ref, router_ref, sems,
+    rows_hbm, ids_hbm, targets_hbm, router_hbm, y_hbm, rank_ref, gate_ref, spot_ref,
+    y_ref, rows_ref, ids_ref, targets_ref, router_ref, sems,
 ):
     loads = start_loads(
         [(targets_hbm, targets_ref), (ids_hbm, ids_ref), (rows_hbm, rows_ref), (router_hbm, router_ref)], sems
@@ -70,6 +70,7 @@
     half = width // 2
     blk = 32
     packed = rank.astype(BF16)
+    stores = []
     for i in range(experts // blk):
         spread = jnp.where(iota((blk * 8, experts), 0) // 8 + i * blk == iota((blk * 8, experts), 1), 1.0, 0.0)
         rank_e = dot(spread.astype(BF16), packed)
@@ -80,6 +81,8 @@
         lines = slice(i * blk * 8, (i + 1) * blk * 8)
         y_ref[lines, :width] = dot(main, rows).astype(BF16)
         y_ref[lines, width:] = (dot(low, rows[:, :half]) + dot(high, rows[:, half:])).astype(BF16)
+        stores.append(pltpu.make_async_copy(y_ref.at[lines], y_hbm.at[lines], sems.at[4 + i]))
+        stores[-1].start()
     rank_ref[...] = rank.T
     member_q = member.T > 0.5
     loads[3].wait()
@@ -87,6 +90,8 @@
     highest = jnp.max(jnp.where(member_q, logits, NEG), 1, keepdims=True)
     raised = jnp.where(member_q, jnp.exp(jnp.minimum(logits - highest, 0.0)), 0.0)
     gate_ref[...] = raised / jnp.sum(raised, 1, keepdims=True)
+    for store in stores:
+        store.wait()
 
 
 def dispatch(rows, ids, targets, router):
@@ -95,15 +100,17 @@
     return pl.pallas_call(
         dispatch_kernel,
         in_specs=[pl.BlockSpec(memory_space=pltpu.HBM)] * 4,
+        out_specs=[pl.BlockSpec(memory_space=pltpu.HBM)] + [pl.BlockSpec(memory_space=VMEM)] * 3,
         out_shape=[jax.ShapeDtypeStruct((1024, width * 3 // 2), BF16), table, table, table],
         scratch_shapes=[
+            VMEM((1024, width * 3 // 2), BF16),
             VMEM((n, width), BF16),
             VMEM((8, n), jnp.int32),
             VMEM((1, n), jnp.int32),
             VMEM(router.shape, BF16),
-            pltpu.SemaphoreType.DMA((4,)),
+            pltpu.SemaphoreType.DMA((8,)),
         ],
-        compiler_params=pltpu.CompilerParams(vmem_limit_bytes=16 * MIB),
+        compiler_params=pltpu.CompilerParams(vmem_limit_bytes=57 * MIB),
         name="dispatch_rows",
     )(rows, ids.T, targets.reshape(1, n), router)
 
@@ -242,7 +249,7 @@
     return vectors * cos + pltpu.roll(vectors, HD // 2, 1) * (sin * sign)
 
 
-def keys_kernel(x0, x1, x2, x3, gain_ref, kg_ref, wk_hbm, wv_hbm, near_ref, far_ref, kv_ref, norm_ref, wkv_ref, sems):
+def keys_kernel(x0, x1, x2, x3, gain_ref, kg_ref, wk_hbm, wv_hbm, near_ref, far_ref, kv_hbm, norm_hbm, kv_ref, norm_ref, wkv_ref, sems):
     ctx = lax.axis_index("ctx")
     head = lax.axis_index("head")
     z = head // 2
@@ -265,6 +272,8 @@
             block = 2 * lax.rem(z + 4 - i, 4) + (core if j == 0 else 1 - core)
             norm = (x_ref[j].astype(F32) * scale * gain_ref[:, pl.ds(pl.multiple_of(block * w, w), w)]).astype(BF16)
             norm_ref[:, pl.ds(pl.multiple_of(block * w, w), w)] = norm
+    stores = [pltpu.make_async_copy(norm_ref, norm_hbm, sems.at[2])]
+    stores[0].start()
     for load in loads:
         load.wait()
     both = dot(norm_ref[...], wkv_ref[...])
@@ -273,6 +282,11 @@
     far = [far_ref.at[0], far_ref.at[1]]
     kv_ref[:, :HD] = turned(both[:, :HD], kg_ref[pl.ds(z, 1), :], near, far, shard).astype(BF16)
     kv_ref[:, HD:] = both[:, HD:].astype(BF16)
+    for i in range(kv_hbm.shape[0]):
+        stores.append(pltpu.make_async_copy(kv_ref, kv_hbm.at[i], sems.at[3 + i]))
+        stores[-1].start()
+    for store in stores:
+        store.wait()
 
 
 def project_keys(blocks, row_gain, key_gain, w_key, w_value, near, far):
@@ -282,8 +296,17 @@
         in_specs=[pl.BlockSpec(memory_space=VMEM)] * 6
         + [pl.BlockSpec(memory_space=pltpu.HBM)] * 2
         + [pl.BlockSpec(memory_space=VMEM)] * 2,
-        out_shape=[jax.ShapeDtypeStruct((half, 2 * HD), BF16), jax.ShapeDtypeStruct((half, 8 * w), BF16)],
-        scratch_shapes=[VMEM((w_key.shape[0], 2 * HD), BF16), pltpu.SemaphoreType.DMA((2,))],
+        out_specs=[pl.BlockSpec(memory_space=pltpu.HBM)] * 2,
+        out_shape=[
+            jax.ShapeDtypeStruct((far.shape[1], half, 2 * HD), BF16),
+            jax.ShapeDtypeStruct((half, 8 * w), BF16),
+        ],
+        scratch_shapes=[
+            VMEM((half, 2 * HD), BF16),
+            VMEM((half, 8 * w), BF16),
+            VMEM((w_key.shape[0], 2 * HD), BF16),
+            pltpu.SemaphoreType.DMA((3 + far.shape[1],)),
+        ],
         compiler_params=pltpu.CompilerParams(vmem_limit_bytes=16 * MIB),
         name="project_keys",
     )(*blocks, row_gain, key_gain, w_key, w_value, near, far)
@@ -337,25 +360,24 @@
             first = jnp.where(core == 0, chunk, shards // group - 1 - chunk) * group
             keys = kv_ref[pl.ds(first, group), :, :HD].reshape(span, HD)
             values = value_s[pl.ds(first, group)].reshape(span, 2 * HD)
+            if masked:
+                t = iota((1, span), 1)
+                place = first + t // shard
+                key_pos = jnp.where(core == 0, place, shards - 1 - place) * (2 * shard) + core * shard + t % shard
+                query_pos = own * (2 * half) + upper * half + iota((half, span), 0)
+                bias = jnp.where(query_pos >= key_pos, 0.0, NEG)
             every = [dot_t(piece, keys) for piece in pieces]
             result = []
             for (highest, weighted), scores in zip(carry, every):
                 if masked:
-                    t = iota((rows, span), 1)
-                    place = first + t // shard
-                    key_pos = jnp.where(core == 0, place, shards - 1 - place) * (2 * shard) + core * shard + t % shard
-                    query_pos = own * (2 * half) + upper * half + iota((rows, span), 0) % half
-                    allowed = query_pos >= key_pos
-                    scores = jnp.where(allowed, scores, NEG)
+                    scores = (scores.reshape(rows // half, half, span) + bias[None]).reshape(rows, span)
                 fresh = jnp.maximum(highest, jnp.max(scores, 1, keepdims=True))
                 weights = jnp.exp2(scores - fresh)
-                if masked:
-                    weights = jnp.where(allowed, weights, 0.0)
                 weighted = weighted * jnp.exp2(highest - fresh) + dot(weights.astype(BF16), values)
                 result.append((fresh, weighted))
             return tuple(result)
 
-        start = tuple((jnp.full((rows, 1), NEG, F32), jnp.zeros((rows, 2 * HD), F32)) for _ in range(subs))
+        start = tuple((jnp.full((rows, 1), 0.5 * NEG, F32), jnp.zeros((rows, 2 * HD), F32)) for _ in range(subs))
         whole = own // group
         state = lax.fori_loop(0, whole, lambda j, carry: fold(carry, j, False), start)
         state = fold(state, whole, True)
@@ -480,9 +502,7 @@
     blocks = [along(mine, hops) for hops in range(4)]
     near, far = turning_tables(tokens, 16)
     kv, norm = project_keys(blocks, attn_gain.reshape(1, -1), k_gain.reshape(KVH, HD), w_key, w_value, near, far)
-    all_kv = lax.all_to_all(
-        jnp.broadcast_to(kv[None], (16, *kv.shape)), "ctx", split_axis=0, concat_axis=0, tiled=True
-    )
+    all_kv = lax.all_to_all(kv, "ctx", split_axis=0, concat_axis=0, tiled=True)
     low, high = project_queries(norm, to_partner(norm), w_query, q_gain, near, far)
     for_partner = attend(to_partner(low), to_partner(high), all_kv)
     from_partner = to_partner(for_partner)

time: 323 us -> 326 us (level)
  Pallas kernels: 48.8 us -> 54.9 us
  local copies, waits for them, and re-layouts: 8.89 us -> 5.28 us
    pallas_call x1, Pallas kernels: 1.51 us -> 5.01 us  [project_keys(): pl.pallas_call(keys_kernel, in_specs=[pl.BlockSpec(memory_space=VMEM)] *...]
where the time goes in v4:
time: 326 us; the launch traced here: 322 us
  blocking collectives  187 us (57%)
  Pallas kernels  54.9 us (17%)
  waiting for transfers between devices  40.1 us (12%)
  starting transfers between devices  32.9 us (10%)
  local copies, waits for them, and re-layouts  5.28 us (2%)
    all_to_all x3, blocking collectives, everywhere(): lax.all_to_all(blocks, ('ctx', 'head'), split_axis=0, concat_axis=0, tile...  187 us
    ppermute x8, starting transfers between devices, along(): return lax.ppermute(shard, ('ctx', 'head'), pairs)  26.4 us
    pallas_call x2, Pallas kernels, attend(): pl.pallas_call(attend_kernel, out_shape=jax.ShapeDtypeStruct((heads, 2 *...  18.4 us
    pallas_call x1, Pallas kernels, run_expert(): pl.pallas_call(expert_kernel, out_shape=jax.ShapeDtypeStruct(y.shape, BF1...  17.1 us
    all_to_all x1, waiting for transfers between devices, body(): all_kv = lax.all_to_all(kv, 'ctx', split_axis=0, concat_axis=0, tiled=True)  16.7 us
    ppermute x8, waiting for transfers between devices, along(): return lax.ppermute(shard, ('ctx', 'head'), pairs)  15.3 us
    ppermute x7, waiting for transfers between devices, to_partner(): return lax.ppermute(shard, 'head', partner)  8.1 us
  transfers between devices with their start and end apart: 16, of which 13 were waited for; matrix products, arithmetic and copies ran while one was open for 0% of the time, Pallas kernels for 4%

profile of v4, /device:TPU:1, one launch (start us, length us, event | category | flops | bytes accessed | tf_op | source)
XLA Modules:
  0.0 322.2 jit_solution(10539047886291161839)
XLA Ops:
  0.0 6.4 %dispatch_rows.1 = (bf16[1024,3072]{1,0:T(8,128)(2,1)}, f32[128,128]{1,0:T(8,128)}, f32[128,128]{1,0:T(8,128)}, f32[128,128]{1,0:T(8,128)}) custom-call(bf16[128,2048]{1,0:T(8,128)(2,1)} %rows_hbm.1, s32[8,128]{1,0:T(8,128)} %bitcast.44, s32[1,128]{1,0:T(1,128)} %bitcast.45, bf16[2048,128]{1,0:T(8,128)(2,1)} %router_hbm.1), custom_call_target="tpu_custom_call" | custom-call | tf_op jit(solution)/shard_map/dispatch_rows/pallas_call | solution.py:100
  6.4 86.7 %all_to_all.20 = bf16[128,8,3072]{2,1,0:T(8,128)(2,1)S(1)} all-to-all(bf16[128,8,3072]{2,1,0:T(8,128)(2,1)} %bitcast.41), channel_id=1, replica_groups=mesh['ctx'=16,'head'=8] {'ctx','head'}, dimensions={0} | all-to-all | bytes 12582912 | tf_op jit(solution)/shard_map/all_to_all | solution.py:490
  93.1 17.1 %expert_ffn.1 = bf16[1024,3072]{1,0:T(8,128)(2,1)S(1)} custom-call(bf16[1024,3072]{1,0:T(8,128)(2,1)S(1)} %bitcast.29, bf16[2048,768]{1,0:T(8,128)(2,1)S(1)} %bitcast.33, bf16[2048,768]{1,0:T(8,128)(2,1)S(1)} %bitcast.34, bf16[768,2048]{1,0:T(8,128)(2,1)S(1)} %bitcast.35), custom_call_target="tpu_custom_call" | custom-call | tf_op jit(solution)/shard_map/expert_ffn/pallas_call | solution.py:152
  110.3 79.7 %all_to_all.21 = bf16[128,8,3072]{2,1,0:T(8,128)(2,1)S(1)} all-to-all(bf16[128,8,3072]{2,1,0:T(8,128)(2,1)S(1)} %bitcast.30), channel_id=1, replica_groups=mesh['ctx'=16,'head'=8] {'ctx','head'}, dimensions={0} | all-to-all | bytes 12582912 | tf_op jit(solution)/shard_map/all_to_all | solution.py:490
  190.0 2.7 combine_rows.1
  192.7 20.8 %all_to_all.22 = bf16[128,8,384]{2,1,0:T(8,128)(2,1)S(1)} all-to-all(bf16[128,8,384]{2,1,0:T(8,128)(2,1)S(1)} %bitcast.31), channel_id=1, replica_groups=mesh['ctx'=16,'head'=8] {'ctx','head'}, dimensions={0} | all-to-all | bytes 1572864 | tf_op jit(solution)/shard_map/all_to_all | solution.py:490
  216.7 2.8 collective-permute-start.1
  219.5 3.6 %collective-permute-start.2 = (bf16[2,256,256]{2,1,0:T(8,128)(2,1)S(1)}, bf16[2,256,256]{2,1,0:T(8,128)(2,1)S(1)}, u32[]{:S(2)}, u32[]{:S(2)}) collective-permute-start(bf16[2,256,256]{2,1,0:T(8,128)(2,1)S(1)} %pad_maximum_fusion), channel_id=1, source_target_pairs={{0,2},{1,123},{2,4},{3,125},{4,6},{5,127},{6,0},{7,121},{8,10},{9,... | collective-permute-start | bytes 786440 | tf_op jit(solution)/shard_map/ppermute | solution.py:487
  223.1 2.6 collective-permute-start.3
  225.8 3.6 %collective-permute-start.4 = (bf16[2,256,256]{2,1,0:T(8,128)(2,1)S(1)}, bf16[2,256,256]{2,1,0:T(8,128)(2,1)S(1)}, u32[]{:S(2)}, u32[]{:S(2)}) collective-permute-start(bf16[2,256,256]{2,1,0:T(8,128)(2,1)S(1)} %pad_maximum_fusion), channel_id=1, source_target_pairs={{0,6},{1,127},{2,0},{3,121},{4,2},{5,123},{6,4},{7,125},{8,14},{9,... | collective-permute-start | bytes 786440 | tf_op jit(solution)/shard_map/ppermute | solution.py:487
  230.3 3.8 %collective-permute-done.3.x2 = bf16[2,256,256]{2,1,0:T(8,128)(2,1)S(1)} collective-permute-done((bf16[2,256,256]{2,1,0:T(8,128)(2,1)S(1)}, bf16[2,256,256]{2,1,0:T(8,128)(2,1)S(1)}, u32[]{:S(2)}, u32[]{:S(2)}) %collective-permute-start.3) | collective-permute-done | bytes 262176 | tf_op jit(solution)/shard_map/ppermute | solution.py:487
  234.1 3.8 %collective-permute-done.4.x3 = bf16[2,256,256]{2,1,0:T(8,128)(2,1)S(1)} collective-permute-done((bf16[2,256,256]{2,1,0:T(8,128)(2,1)S(1)}, bf16[2,256,256]{2,1,0:T(8,128)(2,1)S(1)}, u32[]{:S(2)}, u32[]{:S(2)}) %collective-permute-start.4) | collective-permute-done | bytes 262176 | tf_op jit(solution)/shard_map/ppermute | solution.py:487
  237.9 5.0 %project_keys.1 = (bf16[16,256,256]{2,1,0:T(8,128)(2,1)S(1)}, bf16[256,2048]{1,0:T(8,128)(2,1)S(1)}) custom-call(bf16[2,256,256]{2,1,0:T(8,128)(2,1)S(1)} %collective-permute-done.1.x0, bf16[2,256,256]{2,1,0:T(8,128)(2,1)S(1)} %collective-permute-done.2.x1, bf16[2,256,256]{2,1,0:T(8,128)(2,1)S(1)} %collective-permute-done.3.x2, ...), custom_call_target="tpu_custom_call" | custom-call | tf_op jit(solution)/shard_map/project_keys/pallas_call | solution.py:294
  245.3 3.8 %all-to-all-start.3 = ((bf16[16,256,256]{2,1,0:T(8,128)(2,1)}), bf16[16,256,256]{2,1,0:T(8,128)(2,1)S(1)}, u32[]{:S(2)}, u32[]{:S(2)}) async-start(bf16[16,256,256]{2,1,0:T(8,128)(2,1)} %copy-done.5), calls=%async_computation.3 | async-start | bytes 4194304 | tf_op jit(solution)/shard_map/all_to_all | solution.py:505
  249.2 2.9 collective-permute-done.5.other_ref
  258.6 16.7 %all-to-all-done.3.kv_ref = bf16[16,256,256]{2,1,0:T(8,128)(2,1)S(1)} async-done(((bf16[16,256,256]{2,1,0:T(8,128)(2,1)}), bf16[16,256,256]{2,1,0:T(8,128)(2,1)S(1)}, u32[]{:S(2)}, u32[]{:S(2)}) %all-to-all-start.3) | async-done | bytes 2097184 | tf_op jit(solution)/shard_map/all_to_all | solution.py:505
  275.2 9.2 %attend.3 = f32[4,512,256]{2,1,0:T(8,128)S(1)} custom-call(bf16[4,256,128]{2,1,0:T(8,128)(2,1)S(1)} %collective-permute-done.6.low_ref, bf16[4,256,128]{2,1,0:T(8,128)(2,1)S(1)} %collective-permute-done.7.high_ref, bf16[16,256,256]{2,1,0:T(8,128)(2,1)S(1)} %all-to-all-done.3.kv_ref), custom_call_target="tpu_custom_call" | custom-call | tf_op jit(solution)/shard_map/attend/pallas_call | solution.py:394
  284.5 9.2 %attend.2.own_ref = f32[4,512,256]{2,1,0:T(8,128)S(1)} custom-call(bf16[4,256,128]{2,1,0:T(8,128)(2,1)S(1)} %get-tuple-element.24.low_ref, bf16[4,256,128]{2,1,0:T(8,128)(2,1)S(1)} %get-tuple-element.25.high_ref, bf16[16,256,256]{2,1,0:T(8,128)(2,1)S(1)} %all-to-all-done.3.kv_ref), custom_call_target="tpu_custom_call" | custom-call | tf_op jit(solution)/shard_map/attend/pallas_call | solution.py:394
  299.1 2.4 collective-permute-start.10
  301.5 4.4 %collective-permute-start.11 = (bf16[2,256,256]{2,1,0:T(8,128)(2,1)S(1)}, bf16[2,256,256]{2,1,0:T(8,128)(2,1)S(1)}, u32[]{:S(2)}, u32[]{:S(2)}) collective-permute-start(bf16[2,256,256]{2,1,0:T(8,128)(2,1)S(1)} %get-tuple-element.32), channel_id=1, source_target_pairs={{0,2},{1,123},{2,4},{3,125},{4,6},{5,127},{6,0},{7,121},{8,10},{9,... | collective-permute-start | bytes 786440 | tf_op jit(solution)/shard_map/ppermute | solution.py:487
  305.9 2.7 collective-permute-start.12
  308.5 4.2 %collective-permute-start.13 = (bf16[2,256,256]{2,1,0:T(8,128)(2,1)S(1)}, bf16[2,256,256]{2,1,0:T(8,128)(2,1)S(1)}, u32[]{:S(2)}, u32[]{:S(2)}) collective-permute-start(bf16[2,256,256]{2,1,0:T(8,128)(2,1)S(1)} %get-tuple-element.30), channel_id=1, source_target_pairs={{0,6},{1,127},{2,0},{3,121},{4,2},{5,123},{6,4},{7,125},{8,14},{9,... | collective-permute-start | bytes 786440 | tf_op jit(solution)/shard_map/ppermute | solution.py:487
  313.9 2.9 collective-permute-done.12
  316.8 2.8 collective-permute-done.13
  (64 shorter events, 21.8 us)
Async XLA Ops:
  6.4 86.7 %copy-start.1 = (bf16[1,2048,768]{2,1,0:T(8,128)(2,1)S(1)}, bf16[1,2048,768]{2,1,0:T(8,128)(2,1)}, u32[]{:S(2)}) copy-start(bf16[1,2048,768]{2,1,0:T(8,128)(2,1)} %param.21) | copy-start | bytes 9437188
  6.4 86.7 %copy-start.2 = (bf16[1,2048,768]{2,1,0:T(8,128)(2,1)S(1)}, bf16[1,2048,768]{2,1,0:T(8,128)(2,1)}, u32[]{:S(2)}) copy-start(bf16[1,2048,768]{2,1,0:T(8,128)(2,1)} %param.22) | copy-start | bytes 9437188
  6.4 86.7 %copy-start.3 = (bf16[1,768,2048]{2,1,0:T(8,128)(2,1)S(1)}, bf16[1,768,2048]{2,1,0:T(8,128)(2,1)}, u32[]{:S(2)}) copy-start(bf16[1,768,2048]{2,1,0:T(8,128)(2,1)} %param.23) | copy-start | bytes 9437188
  110.2 79.7 %copy-start.12 = (f32[128,128]{1,0:T(8,128)S(1)}, f32[128,128]{1,0:T(8,128)}, u32[]{:S(2)}) copy-start(f32[128,128]{1,0:T(8,128)} %get-tuple-element.18.rank_ref) | copy-start | bytes 196612
  110.3 79.7 %copy-start.13 = (f32[128,128]{1,0:T(8,128)S(1)}, f32[128,128]{1,0:T(8,128)}, u32[]{:S(2)}) copy-start(f32[128,128]{1,0:T(8,128)} %get-tuple-element.19.gate_ref) | copy-start | bytes 196612
  110.3 79.7 %copy-start.14 = (f32[128,128]{1,0:T(8,128)S(1)}, f32[128,128]{1,0:T(8,128)}, u32[]{:S(2)}) copy-start(f32[128,128]{1,0:T(8,128)} %get-tuple-element.20.spot_ref) | copy-start | bytes 196612
  190.0 47.9 %copy-start.7 = (bf16[2048,512]{1,0:T(8,128)(2,1)S(1)}, bf16[2048,512]{1,0:T(8,128)(2,1)}, u32[]{:S(2)}) copy-start(bf16[2048,512]{1,0:T(8,128)(2,1)} %wv_hbm.1) | copy-start | bytes 6291460
  192.7 45.2 %copy-start.6 = (bf16[2048,512]{1,0:T(8,128)(2,1)S(1)}, bf16[2048,512]{1,0:T(8,128)(2,1)}, u32[]{:S(2)}) copy-start(bf16[2048,512]{1,0:T(8,128)(2,1)} %wk_hbm.1) | copy-start | bytes 6291460
  214.4 2.3 collective-permute-start
  216.7 12.7 %collective-permute-start.1 = (bf16[2,256,256]{2,1,0:T(8,128)(2,1)S(1)}, bf16[2,256,256]{2,1,0:T(8,128)(2,1)S(1)}, u32[]{:S(2)}, u32[]{:S(2)}) collective-permute-start(bf16[2,256,256]{2,1,0:T(8,128)(2,1)S(1)} %pad_maximum_fusion), channel_id=1, source_target_pairs={{0,0},{1,121},{2,2},{3,123},{4,4},{5,125},{6,6},{7,127},{8,8},{9,1... | collective-permute-start | bytes 786440 | tf_op jit(solution)/shard_map/ppermute | solution.py:487
  219.5 10.8 %collective-permute-start.2 = (bf16[2,256,256]{2,1,0:T(8,128)(2,1)S(1)}, bf16[2,256,256]{2,1,0:T(8,128)(2,1)S(1)}, u32[]{:S(2)}, u32[]{:S(2)}) collective-permute-start(bf16[2,256,256]{2,1,0:T(8,128)(2,1)S(1)} %pad_maximum_fusion), channel_id=1, source_target_pairs={{0,2},{1,123},{2,4},{3,125},{4,6},{5,127},{6,0},{7,121},{8,10},{9,... | collective-permute-start | bytes 786440 | tf_op jit(solution)/shard_map/ppermute | solution.py:487
  223.1 10.9 %collective-permute-start.3 = (bf16[2,256,256]{2,1,0:T(8,128)(2,1)S(1)}, bf16[2,256,256]{2,1,0:T(8,128)(2,1)S(1)}, u32[]{:S(2)}, u32[]{:S(2)}) collective-permute-start(bf16[2,256,256]{2,1,0:T(8,128)(2,1)S(1)} %pad_maximum_fusion), channel_id=1, source_target_pairs={{0,4},{1,125},{2,6},{3,127},{4,0},{5,121},{6,2},{7,123},{8,12},{9,... | collective-permute-start | bytes 786440 | tf_op jit(solution)/shard_map/ppermute | solution.py:487
  225.8 12.1 %collective-permute-start.4 = (bf16[2,256,256]{2,1,0:T(8,128)(2,1)S(1)}, bf16[2,256,256]{2,1,0:T(8,128)(2,1)S(1)}, u32[]{:S(2)}, u32[]{:S(2)}) collective-permute-start(bf16[2,256,256]{2,1,0:T(8,128)(2,1)S(1)} %pad_maximum_fusion), channel_id=1, source_target_pairs={{0,6},{1,127},{2,0},{3,121},{4,2},{5,123},{6,4},{7,125},{8,14},{9,... | collective-permute-start | bytes 786440 | tf_op jit(solution)/shard_map/ppermute | solution.py:487
  245.3 30.0 %all-to-all-start.3 = ((bf16[16,256,256]{2,1,0:T(8,128)(2,1)}), bf16[16,256,256]{2,1,0:T(8,128)(2,1)S(1)}, u32[]{:S(2)}, u32[]{:S(2)}) async-start(bf16[16,256,256]{2,1,0:T(8,128)(2,1)} %copy-done.5), calls=%async_computation.3 | async-start | bytes 4194304 | tf_op jit(solution)/shard_map/all_to_all | solution.py:505
  249.1 3.0 collective-permute-start.5
  256.6 1.6 collective-permute-start.6
  256.8 1.8 collective-permute-start.7
  284.5 9.3 %collective-permute-start.8 = (f32[4,512,256]{2,1,0:T(8,128)S(1)}, f32[4,512,256]{2,1,0:T(8,128)S(1)}, u32[]{:S(2)}, u32[]{:S(2)}) collective-permute-start(f32[4,512,256]{2,1,0:T(8,128)S(1)} %attend.3), channel_id=1, source_target_pairs={{0,1},{1,0},{2,3},{3,2},{4,5},{5,4},{6,7},{7,6},{8,9},{9,8},{10,11... | collective-permute-start | bytes 6291464 | tf_op jit(solution)/shard_map/ppermute | solution.py:479
  295.9 2.9 collective-permute-start.9
  299.1 13.7 %collective-permute-start.10 = (bf16[2,256,256]{2,1,0:T(8,128)(2,1)S(1)}, bf16[2,256,256]{2,1,0:T(8,128)(2,1)S(1)}, u32[]{:S(2)}, u32[]{:S(2)}) collective-permute-start(bf16[2,256,256]{2,1,0:T(8,128)(2,1)S(1)} %get-tuple-element.29), channel_id=1, source_target_pairs={{0,0},{1,121},{2,2},{3,123},{4,4},{5,125},{6,6},{7,127},{8,8},{9,1... | collective-permute-start | bytes 786440 | tf_op jit(solution)/shard_map/ppermute | solution.py:487
  301.5 12.4 %collective-permute-start.11 = (bf16[2,256,256]{2,1,0:T(8,128)(2,1)S(1)}, bf16[2,256,256]{2,1,0:T(8,128)(2,1)S(1)}, u32[]{:S(2)}, u32[]{:S(2)}) collective-permute-start(bf16[2,256,256]{2,1,0:T(8,128)(2,1)S(1)} %get-tuple-element.32), channel_id=1, source_target_pairs={{0,2},{1,123},{2,4},{3,125},{4,6},{5,127},{6,0},{7,121},{8,10},{9,... | collective-permute-start | bytes 786440 | tf_op jit(solution)/shard_map/ppermute | solution.py:487
  305.9 10.9 %collective-permute-start.12 = (bf16[2,256,256]{2,1,0:T(8,128)(2,1)S(1)}, bf16[2,256,256]{2,1,0:T(8,128)(2,1)S(1)}, u32[]{:S(2)}, u32[]{:S(2)}) collective-permute-start(bf16[2,256,256]{2,1,0:T(8,128)(2,1)S(1)} %get-tuple-element.31), channel_id=1, source_target_pairs={{0,4},{1,125},{2,6},{3,127},{4,0},{5,121},{6,2},{7,123},{8,12},{9,... | collective-permute-start | bytes 786440 | tf_op jit(solution)/shard_map/ppermute | solution.py:487
  308.5 11.0 %collective-permute-start.13 = (bf16[2,256,256]{2,1,0:T(8,128)(2,1)S(1)}, bf16[2,256,256]{2,1,0:T(8,128)(2,1)S(1)}, u32[]{:S(2)}, u32[]{:S(2)}) collective-permute-start(bf16[2,256,256]{2,1,0:T(8,128)(2,1)S(1)} %get-tuple-element.30), channel_id=1, source_target_pairs={{0,6},{1,127},{2,0},{3,121},{4,2},{5,123},{6,4},{7,125},{8,14},{9,... | collective-permute-start | bytes 786440 | tf_op jit(solution)/shard_map/ppermute | solution.py:487
  319.8 1.4 collective-permute-start.14
  (11 other events, 225.6 us)

commit v5 on v4

--- a/solution.py
+++ b/solution.py
@@ -249,7 +249,7 @@
     return vectors * cos + pltpu.roll(vectors, HD // 2, 1) * (sin * sign)
 
 
-def keys_kernel(x0, x1, x2, x3, gain_ref, kg_ref, wk_hbm, wv_hbm, near_ref, far_ref, kv_hbm, norm_hbm, kv_ref, norm_ref, wkv_ref, sems):
+def keys_kernel(x0, x1, x2, x3, gain_ref, kg_ref, wk_hbm, wv_hbm, near_ref, far_ref, kv_ref, norm_ref, wkv_ref, sems):
     ctx = lax.axis_index("ctx")
     head = lax.axis_index("head")
     z = head // 2
@@ -268,12 +268,11 @@
             square = square + jnp.sum(x * x, 1, keepdims=True)
     scale = lax.rsqrt(square * (1.0 / width) + EPSILON)
     for i, x_ref in enumerate(x_refs):
+        source = lax.rem(jnp.where(core == 0, z + 4 - i, z + i), 4)
         for j in range(2):
-            block = 2 * lax.rem(z + 4 - i, 4) + (core if j == 0 else 1 - core)
+            block = 2 * source + (core if j == 0 else 1 - core)
             norm = (x_ref[j].astype(F32) * scale * gain_ref[:, pl.ds(pl.multiple_of(block * w, w), w)]).astype(BF16)
             norm_ref[:, pl.ds(pl.multiple_of(block * w, w), w)] = norm
-    stores = [pltpu.make_async_copy(norm_ref, norm_hbm, sems.at[2])]
-    stores[0].start()
     for load in loads:
         load.wait()
     both = dot(norm_ref[...], wkv_ref[...])
@@ -282,11 +281,6 @@
     far = [far_ref.at[0], far_ref.at[1]]
     kv_ref[:, :HD] = turned(both[:, :HD], kg_ref[pl.ds(z, 1), :], near, far, shard).astype(BF16)
     kv_ref[:, HD:] = both[:, HD:].astype(BF16)
-    for i in range(kv_hbm.shape[0]):
-        stores.append(pltpu.make_async_copy(kv_ref, kv_hbm.at[i], sems.at[3 + i]))
-        stores[-1].start()
-    for store in stores:
-        store.wait()
 
 
 def project_keys(blocks, row_gain, key_gain, w_key, w_value, near, far):
@@ -296,17 +290,8 @@
         in_specs=[pl.BlockSpec(memory_space=VMEM)] * 6
         + [pl.BlockSpec(memory_space=pltpu.HBM)] * 2
         + [pl.BlockSpec(memory_space=VMEM)] * 2,
-        out_specs=[pl.BlockSpec(memory_space=pltpu.HBM)] * 2,
-        out_shape=[
-            jax.ShapeDtypeStruct((far.shape[1], half, 2 * HD), BF16),
-            jax.ShapeDtypeStruct((half, 8 * w), BF16),
-        ],
-        scratch_shapes=[
-            VMEM((half, 2 * HD), BF16),
-            VMEM((half, 8 * w), BF16),
-            VMEM((w_key.shape[0], 2 * HD), BF16),
-            pltpu.SemaphoreType.DMA((3 + far.shape[1],)),
-        ],
+        out_shape=[jax.ShapeDtypeStruct((half, 2 * HD), BF16), jax.ShapeDtypeStruct((half, 8 * w), BF16)],
+        scratch_shapes=[VMEM((w_key.shape[0], 2 * HD), BF16), pltpu.SemaphoreType.DMA((2,))],
         compiler_params=pltpu.CompilerParams(vmem_limit_bytes=16 * MIB),
         name="project_keys",
     )(*blocks, row_gain, key_gain, w_key, w_value, near, far)
@@ -404,8 +389,9 @@
     z = lax.axis_index("head") // 2
     w = o_ref.shape[3]
     for i in range(o_ref.shape[0]):
+        target = lax.rem(jnp.where(core == 0, z + i, z + 4 - i), 4)
         for j in range(2):
-            block = 2 * lax.rem(z + i, 4) + (core if j == 0 else 1 - core)
+            block = 2 * target + (core if j == 0 else 1 - core)
             o_ref[i, j] = dot(attended, w_ref[:, pl.ds(pl.multiple_of(block * w, w), w)]).astype(BF16)
 
 
@@ -482,8 +468,8 @@
         pairs = []
         for c in range(16):
             for h in range(8):
-                there = c if h % 2 == 0 else 15 - c
-                pairs.append((c * 8 + h, there * 8 + (h + 2 * hops) % 8))
+                there = c * 8 + (h + 2 * hops) % 8 if h % 2 == 0 else (15 - c) * 8 + (h - 2 * hops) % 8
+                pairs.append((c * 8 + h, there))
         return lax.ppermute(shard, ("ctx", "head"), pairs)
 
     def everywhere(blocks):
@@ -502,7 +488,9 @@
     blocks = [along(mine, hops) for hops in range(4)]
     near, far = turning_tables(tokens, 16)
     kv, norm = project_keys(blocks, attn_gain.reshape(1, -1), k_gain.reshape(KVH, HD), w_key, w_value, near, far)
-    all_kv = lax.all_to_all(kv, "ctx", split_axis=0, concat_axis=0, tiled=True)
+    all_kv = lax.all_to_all(
+        jnp.broadcast_to(kv[None], (16, *kv.shape)), "ctx", split_axis=0, concat_axis=0, tiled=True
+    )
     low, high = project_queries(norm, to_partner(norm), w_query, q_gain, near, far)
     for_partner = attend(to_partner(low), to_partner(high), all_kv)
     from_partner = to_partner(for_partner)

time: 326 us -> 327 us (level)
  waiting for transfers between devices: 40.1 us -> 48.3 us
  Pallas kernels: 54.9 us -> 51.3 us
  starting transfers between devices: 32.9 us -> 29.6 us
    ppermute x8, waiting for transfers between devices: 15.3 us -> 21.3 us  [along(): return lax.ppermute(shard, ('ctx', 'head'), pairs)]
    pallas_call x1, Pallas kernels: 5.01 us -> 1.52 us  [project_keys(): pl.pallas_call(keys_kernel, in_specs=[pl.BlockSpec(memory_space=VMEM)] *...]
    ppermute x8, starting transfers between devices: 26.4 us -> 23 us  [along(): return lax.ppermute(shard, ('ctx', 'head'), pairs)]
where the time goes in v5:
time: 327 us; the launch traced here: 324 us
  blocking collectives  187 us (57%)
  Pallas kernels  51.3 us (16%)
  waiting for transfers between devices  48.3 us (15%)
  starting transfers between devices  29.6 us (9%)
  local copies, waits for them, and re-layouts  5.46 us (2%)
    all_to_all x3, blocking collectives, everywhere(): lax.all_to_all(blocks, ('ctx', 'head'), split_axis=0, concat_axis=0, tile...  187 us
    ppermute x8, starting transfers between devices, along(): return lax.ppermute(shard, ('ctx', 'head'), pairs)  23 us
    ppermute x8, waiting for transfers between devices, along(): return lax.ppermute(shard, ('ctx', 'head'), pairs)  21.3 us
    all_to_all x1, waiting for transfers between devices, body(): lax.all_to_all(jnp.broadcast_to(kv[None], (16, *kv.shape)), 'ctx', split_...  19 us
    pallas_call x2, Pallas kernels, attend(): pl.pallas_call(attend_kernel, out_shape=jax.ShapeDtypeStruct((heads, 2 *...  18.4 us
    pallas_call x1, Pallas kernels, run_expert(): pl.pallas_call(expert_kernel, out_shape=jax.ShapeDtypeStruct(y.shape, BF1...  17.1 us
    ppermute x7, waiting for transfers between devices, to_partner(): return lax.ppermute(shard, 'head', partner)  8.1 us
  transfers between devices with their start and end apart: 16, of which 13 were waited for; matrix products, arithmetic and copies ran while one was open for 0% of the time, Pallas kernels for 4%

profile of v5, /device:TPU:1, one launch (start us, length us, event | category | flops | bytes accessed | tf_op | source)
XLA Modules:
  0.0 323.7 jit_solution(16689105016772317475)
XLA Ops:
  0.0 6.4 %dispatch_rows.1 = (bf16[1024,3072]{1,0:T(8,128)(2,1)}, f32[128,128]{1,0:T(8,128)}, f32[128,128]{1,0:T(8,128)}, f32[128,128]{1,0:T(8,128)}) custom-call(bf16[128,2048]{1,0:T(8,128)(2,1)} %rows_hbm.1, s32[8,128]{1,0:T(8,128)} %bitcast.44, s32[1,128]{1,0:T(1,128)} %bitcast.45, bf16[2048,128]{1,0:T(8,128)(2,1)} %router_hbm.1), custom_call_target="tpu_custom_call" | custom-call | tf_op jit(solution)/shard_map/dispatch_rows/pallas_call | solution.py:100
  6.5 86.7 %all_to_all.20 = bf16[128,8,3072]{2,1,0:T(8,128)(2,1)S(1)} all-to-all(bf16[128,8,3072]{2,1,0:T(8,128)(2,1)} %bitcast.41), channel_id=1, replica_groups=mesh['ctx'=16,'head'=8] {'ctx','head'}, dimensions={0} | all-to-all | bytes 12582912 | tf_op jit(solution)/shard_map/all_to_all | solution.py:476
  93.2 17.1 %expert_ffn.1 = bf16[1024,3072]{1,0:T(8,128)(2,1)S(1)} custom-call(bf16[1024,3072]{1,0:T(8,128)(2,1)S(1)} %bitcast.29, bf16[2048,768]{1,0:T(8,128)(2,1)S(1)} %bitcast.33, bf16[2048,768]{1,0:T(8,128)(2,1)S(1)} %bitcast.34, bf16[768,2048]{1,0:T(8,128)(2,1)S(1)} %bitcast.35), custom_call_target="tpu_custom_call" | custom-call | tf_op jit(solution)/shard_map/expert_ffn/pallas_call | solution.py:152
  110.3 79.7 %all_to_all.21 = bf16[128,8,3072]{2,1,0:T(8,128)(2,1)S(1)} all-to-all(bf16[128,8,3072]{2,1,0:T(8,128)(2,1)S(1)} %bitcast.30), channel_id=1, replica_groups=mesh['ctx'=16,'head'=8] {'ctx','head'}, dimensions={0} | all-to-all | bytes 12582912 | tf_op jit(solution)/shard_map/all_to_all | solution.py:476
  190.0 2.7 combine_rows.1
  192.8 20.8 %all_to_all.22 = bf16[128,8,384]{2,1,0:T(8,128)(2,1)S(1)} all-to-all(bf16[128,8,384]{2,1,0:T(8,128)(2,1)S(1)} %bitcast.31), channel_id=1, replica_groups=mesh['ctx'=16,'head'=8] {'ctx','head'}, dimensions={0} | all-to-all | bytes 1572864 | tf_op jit(solution)/shard_map/all_to_all | solution.py:476
  216.7 2.8 collective-permute-start.1
  219.5 3.5 %collective-permute-start.2 = (bf16[2,256,256]{2,1,0:T(8,128)(2,1)S(1)}, bf16[2,256,256]{2,1,0:T(8,128)(2,1)S(1)}, u32[]{:S(2)}, u32[]{:S(2)}) collective-permute-start(bf16[2,256,256]{2,1,0:T(8,128)(2,1)S(1)} %pad_maximum_fusion), channel_id=1, source_target_pairs={{0,2},{1,127},{2,4},{3,121},{4,6},{5,123},{6,0},{7,125},{8,10},{9,... | collective-permute-start | bytes 786440 | tf_op jit(solution)/shard_map/ppermute | solution.py:473
  223.0 2.4 collective-permute-start.3
  225.4 2.8 collective-permute-start.4
  229.7 4.3 %collective-permute-done.3.x2 = bf16[2,256,256]{2,1,0:T(8,128)(2,1)S(1)} collective-permute-done((bf16[2,256,256]{2,1,0:T(8,128)(2,1)S(1)}, bf16[2,256,256]{2,1,0:T(8,128)(2,1)S(1)}, u32[]{:S(2)}, u32[]{:S(2)}) %collective-permute-start.3) | collective-permute-done | bytes 262176 | tf_op jit(solution)/shard_map/ppermute | solution.py:473
  234.0 3.9 %collective-permute-done.4.x3 = bf16[2,256,256]{2,1,0:T(8,128)(2,1)S(1)} collective-permute-done((bf16[2,256,256]{2,1,0:T(8,128)(2,1)S(1)}, bf16[2,256,256]{2,1,0:T(8,128)(2,1)S(1)}, u32[]{:S(2)}, u32[]{:S(2)}) %collective-permute-start.4) | collective-permute-done | bytes 262176 | tf_op jit(solution)/shard_map/ppermute | solution.py:473
  240.4 1.6 broadcast_in_dim.2
  241.9 3.8 %all-to-all-start.3 = ((bf16[16,256,256]{2,1,0:T(8,128)(2,1)}), bf16[16,256,256]{2,1,0:T(8,128)(2,1)S(1)}, u32[]{:S(2)}, u32[]{:S(2)}) async-start(bf16[16,256,256]{2,1,0:T(8,128)(2,1)} %broadcast_in_dim.2), calls=%async_computation.3 | async-start | bytes 4194304 | tf_op jit(solution)/shard_map/all_to_all | solution.py:491
  245.9 2.9 collective-permute-done.5.other_ref
  248.7 1.6 copy-done.4
  255.1 19.0 %all-to-all-done.3.kv_ref = bf16[16,256,256]{2,1,0:T(8,128)(2,1)S(1)} async-done(((bf16[16,256,256]{2,1,0:T(8,128)(2,1)}), bf16[16,256,256]{2,1,0:T(8,128)(2,1)S(1)}, u32[]{:S(2)}, u32[]{:S(2)}) %all-to-all-start.3) | async-done | bytes 2097184 | tf_op jit(solution)/shard_map/all_to_all | solution.py:491
  274.1 9.2 %attend.3 = f32[4,512,256]{2,1,0:T(8,128)S(1)} custom-call(bf16[4,256,128]{2,1,0:T(8,128)(2,1)S(1)} %collective-permute-done.6.low_ref, bf16[4,256,128]{2,1,0:T(8,128)(2,1)S(1)} %collective-permute-done.7.high_ref, bf16[16,256,256]{2,1,0:T(8,128)(2,1)S(1)} %all-to-all-done.3.kv_ref), custom_call_target="tpu_custom_call" | custom-call | tf_op jit(solution)/shard_map/attend/pallas_call | solution.py:379
  283.4 9.2 %attend.2.own_ref = f32[4,512,256]{2,1,0:T(8,128)S(1)} custom-call(bf16[4,256,128]{2,1,0:T(8,128)(2,1)S(1)} %get-tuple-element.24.low_ref, bf16[4,256,128]{2,1,0:T(8,128)(2,1)S(1)} %get-tuple-element.25.high_ref, bf16[16,256,256]{2,1,0:T(8,128)(2,1)S(1)} %all-to-all-done.3.kv_ref), custom_call_target="tpu_custom_call" | custom-call | tf_op jit(solution)/shard_map/attend/pallas_call | solution.py:379
  292.7 2.1 merge_and_project.1
  297.9 1.9 collective-permute-start.10
  299.8 7.5 %collective-permute-start.11 = (bf16[2,256,256]{2,1,0:T(8,128)(2,1)S(1)}, bf16[2,256,256]{2,1,0:T(8,128)(2,1)S(1)}, u32[]{:S(2)}, u32[]{:S(2)}) collective-permute-start(bf16[2,256,256]{2,1,0:T(8,128)(2,1)S(1)} %get-tuple-element.32), channel_id=1, source_target_pairs={{0,2},{1,127},{2,4},{3,121},{4,6},{5,123},{6,0},{7,125},{8,10},{9,... | collective-permute-start | bytes 786440 | tf_op jit(solution)/shard_map/ppermute | solution.py:473
  307.3 2.1 collective-permute-start.13
  310.6 9.6 %collective-permute-done.12 = bf16[2,256,256]{2,1,0:T(8,128)(2,1)S(1)} collective-permute-done((bf16[2,256,256]{2,1,0:T(8,128)(2,1)S(1)}, bf16[2,256,256]{2,1,0:T(8,128)(2,1)S(1)}, u32[]{:S(2)}, u32[]{:S(2)}) %collective-permute-start.12) | collective-permute-done | bytes 262176 | tf_op jit(solution)/shard_map/ppermute | solution.py:473
  (63 shorter events, 19.7 us)
Async XLA Ops:
  6.4 86.7 %copy-start.1 = (bf16[1,2048,768]{2,1,0:T(8,128)(2,1)S(1)}, bf16[1,2048,768]{2,1,0:T(8,128)(2,1)}, u32[]{:S(2)}) copy-start(bf16[1,2048,768]{2,1,0:T(8,128)(2,1)} %param.21) | copy-start | bytes 9437188
  6.4 86.7 %copy-start.2 = (bf16[1,2048,768]{2,1,0:T(8,128)(2,1)S(1)}, bf16[1,2048,768]{2,1,0:T(8,128)(2,1)}, u32[]{:S(2)}) copy-start(bf16[1,2048,768]{2,1,0:T(8,128)(2,1)} %param.22) | copy-start | bytes 9437188
  6.4 86.7 %copy-start.3 = (bf16[1,768,2048]{2,1,0:T(8,128)(2,1)S(1)}, bf16[1,768,2048]{2,1,0:T(8,128)(2,1)}, u32[]{:S(2)}) copy-start(bf16[1,768,2048]{2,1,0:T(8,128)(2,1)} %param.23) | copy-start | bytes 9437188
  110.3 79.7 %copy-start.11 = (f32[128,128]{1,0:T(8,128)S(1)}, f32[128,128]{1,0:T(8,128)}, u32[]{:S(2)}) copy-start(f32[128,128]{1,0:T(8,128)} %get-tuple-element.18.rank_ref) | copy-start | bytes 196612
  110.3 79.7 %copy-start.12 = (f32[128,128]{1,0:T(8,128)S(1)}, f32[128,128]{1,0:T(8,128)}, u32[]{:S(2)}) copy-start(f32[128,128]{1,0:T(8,128)} %get-tuple-element.19.gate_ref) | copy-start | bytes 196612
  110.3 79.7 %copy-start.13 = (f32[128,128]{1,0:T(8,128)S(1)}, f32[128,128]{1,0:T(8,128)}, u32[]{:S(2)}) copy-start(f32[128,128]{1,0:T(8,128)} %get-tuple-element.20.spot_ref) | copy-start | bytes 196612
  190.0 47.8 %copy-start.6 = (bf16[2048,512]{1,0:T(8,128)(2,1)S(1)}, bf16[2048,512]{1,0:T(8,128)(2,1)}, u32[]{:S(2)}) copy-start(bf16[2048,512]{1,0:T(8,128)(2,1)} %wv_hbm.1) | copy-start | bytes 6291460
  192.7 45.1 %copy-start.5 = (bf16[2048,512]{1,0:T(8,128)(2,1)S(1)}, bf16[2048,512]{1,0:T(8,128)(2,1)}, u32[]{:S(2)}) copy-start(bf16[2048,512]{1,0:T(8,128)(2,1)} %wk_hbm.1) | copy-start | bytes 6291460
  214.4 2.3 collective-permute-start
  216.7 11.5 %collective-permute-start.1 = (bf16[2,256,256]{2,1,0:T(8,128)(2,1)S(1)}, bf16[2,256,256]{2,1,0:T(8,128)(2,1)S(1)}, u32[]{:S(2)}, u32[]{:S(2)}) collective-permute-start(bf16[2,256,256]{2,1,0:T(8,128)(2,1)S(1)} %pad_maximum_fusion), channel_id=1, source_target_pairs={{0,0},{1,121},{2,2},{3,123},{4,4},{5,125},{6,6},{7,127},{8,8},{9,1... | collective-permute-start | bytes 786440 | tf_op jit(solution)/shard_map/ppermute | solution.py:473
  219.5 10.2 %collective-permute-start.2 = (bf16[2,256,256]{2,1,0:T(8,128)(2,1)S(1)}, bf16[2,256,256]{2,1,0:T(8,128)(2,1)S(1)}, u32[]{:S(2)}, u32[]{:S(2)}) collective-permute-start(bf16[2,256,256]{2,1,0:T(8,128)(2,1)S(1)} %pad_maximum_fusion), channel_id=1, source_target_pairs={{0,2},{1,127},{2,4},{3,121},{4,6},{5,123},{6,0},{7,125},{8,10},{9,... | collective-permute-start | bytes 786440 | tf_op jit(solution)/shard_map/ppermute | solution.py:473
  223.0 10.9 %collective-permute-start.3 = (bf16[2,256,256]{2,1,0:T(8,128)(2,1)S(1)}, bf16[2,256,256]{2,1,0:T(8,128)(2,1)S(1)}, u32[]{:S(2)}, u32[]{:S(2)}) collective-permute-start(bf16[2,256,256]{2,1,0:T(8,128)(2,1)S(1)} %pad_maximum_fusion), channel_id=1, source_target_pairs={{0,4},{1,125},{2,6},{3,127},{4,0},{5,121},{6,2},{7,123},{8,12},{9,... | collective-permute-start | bytes 786440 | tf_op jit(solution)/shard_map/ppermute | solution.py:473
  225.4 12.4 %collective-permute-start.4 = (bf16[2,256,256]{2,1,0:T(8,128)(2,1)S(1)}, bf16[2,256,256]{2,1,0:T(8,128)(2,1)S(1)}, u32[]{:S(2)}, u32[]{:S(2)}) collective-permute-start(bf16[2,256,256]{2,1,0:T(8,128)(2,1)S(1)} %pad_maximum_fusion), channel_id=1, source_target_pairs={{0,6},{1,123},{2,0},{3,125},{4,2},{5,127},{6,4},{7,121},{8,14},{9,... | collective-permute-start | bytes 786440 | tf_op jit(solution)/shard_map/ppermute | solution.py:473
  241.9 32.1 %all-to-all-start.3 = ((bf16[16,256,256]{2,1,0:T(8,128)(2,1)}), bf16[16,256,256]{2,1,0:T(8,128)(2,1)S(1)}, u32[]{:S(2)}, u32[]{:S(2)}) async-start(bf16[16,256,256]{2,1,0:T(8,128)(2,1)} %broadcast_in_dim.2), calls=%async_computation.3 | async-start | bytes 4194304 | tf_op jit(solution)/shard_map/all_to_all | solution.py:491
  245.8 3.0 collective-permute-start.5
  253.1 1.6 collective-permute-start.6
  253.3 1.8 collective-permute-start.7
  283.3 9.3 %collective-permute-start.8 = (f32[4,512,256]{2,1,0:T(8,128)S(1)}, f32[4,512,256]{2,1,0:T(8,128)S(1)}, u32[]{:S(2)}, u32[]{:S(2)}) collective-permute-start(f32[4,512,256]{2,1,0:T(8,128)S(1)} %attend.3), channel_id=1, source_target_pairs={{0,1},{1,0},{2,3},{3,2},{4,5},{5,4},{6,7},{7,6},{8,9},{9,8},{10,11... | collective-permute-start | bytes 6291464 | tf_op jit(solution)/shard_map/ppermute | solution.py:465
  294.7 2.9 collective-permute-start.9
  297.9 11.5 %collective-permute-start.10 = (bf16[2,256,256]{2,1,0:T(8,128)(2,1)S(1)}, bf16[2,256,256]{2,1,0:T(8,128)(2,1)S(1)}, u32[]{:S(2)}, u32[]{:S(2)}) collective-permute-start(bf16[2,256,256]{2,1,0:T(8,128)(2,1)S(1)} %get-tuple-element.29), channel_id=1, source_target_pairs={{0,0},{1,121},{2,2},{3,123},{4,4},{5,125},{6,6},{7,127},{8,8},{9,1... | collective-permute-start | bytes 786440 | tf_op jit(solution)/shard_map/ppermute | solution.py:473
  299.8 10.8 %collective-permute-start.11 = (bf16[2,256,256]{2,1,0:T(8,128)(2,1)S(1)}, bf16[2,256,256]{2,1,0:T(8,128)(2,1)S(1)}, u32[]{:S(2)}, u32[]{:S(2)}) collective-permute-start(bf16[2,256,256]{2,1,0:T(8,128)(2,1)S(1)} %get-tuple-element.32), channel_id=1, source_target_pairs={{0,2},{1,127},{2,4},{3,121},{4,6},{5,123},{6,0},{7,125},{8,10},{9,... | collective-permute-start | bytes 786440 | tf_op jit(solution)/shard_map/ppermute | solution.py:473
  307.3 12.9 %collective-permute-start.12 = (bf16[2,256,256]{2,1,0:T(8,128)(2,1)S(1)}, bf16[2,256,256]{2,1,0:T(8,128)(2,1)S(1)}, u32[]{:S(2)}, u32[]{:S(2)}) collective-permute-start(bf16[2,256,256]{2,1,0:T(8,128)(2,1)S(1)} %get-tuple-element.31), channel_id=1, source_target_pairs={{0,4},{1,125},{2,6},{3,127},{4,0},{5,121},{6,2},{7,123},{8,12},{9,... | collective-permute-start | bytes 786440 | tf_op jit(solution)/shard_map/ppermute | solution.py:473
  307.3 13.8 %collective-permute-start.13 = (bf16[2,256,256]{2,1,0:T(8,128)(2,1)S(1)}, bf16[2,256,256]{2,1,0:T(8,128)(2,1)S(1)}, u32[]{:S(2)}, u32[]{:S(2)}) collective-permute-start(bf16[2,256,256]{2,1,0:T(8,128)(2,1)S(1)} %get-tuple-element.30), channel_id=1, source_target_pairs={{0,6},{1,123},{2,0},{3,125},{4,2},{5,127},{6,4},{7,121},{8,14},{9,... | collective-permute-start | bytes 786440 | tf_op jit(solution)/shard_map/ppermute | solution.py:473
  321.3 1.4 collective-permute-start.14
  (10 other events, 224.0 us)

commit v6 on v5

--- a/solution.py
+++ b/solution.py
@@ -18,6 +18,7 @@
 VMEM = pltpu.VMEM
 NEG = -1e30
 MIB = 1024 * 1024
+GROUP = 4
 
 
 def iota(shape, dim):
@@ -228,6 +229,10 @@
     )(landed, stream)
 
 
+def mirrored(shard):
+    return shard + 16 - GROUP - 2 * GROUP * (shard // GROUP)
+
+
 def turning_tables(tokens, shards):
     frequency = THETA ** (-np.arange(HD // 2, dtype=np.float64) * 2.0 / HD)
 
@@ -268,7 +273,7 @@
             square = square + jnp.sum(x * x, 1, keepdims=True)
     scale = lax.rsqrt(square * (1.0 / width) + EPSILON)
     for i, x_ref in enumerate(x_refs):
-        source = lax.rem(jnp.where(core == 0, z + 4 - i, z + i), 4)
+        source = lax.rem(z + 4 - i, 4)
         for j in range(2):
             block = 2 * source + (core if j == 0 else 1 - core)
             norm = (x_ref[j].astype(F32) * scale * gain_ref[:, pl.ds(pl.multiple_of(block * w, w), w)]).astype(BF16)
@@ -276,7 +281,7 @@
     for load in loads:
         load.wait()
     both = dot(norm_ref[...], wkv_ref[...])
-    shard = jnp.where(core == 0, ctx, far_ref.shape[1] - 1 - ctx)
+    shard = jnp.where(core == 0, ctx, mirrored(ctx))
     near = [jnp.where(core == 0, near_ref[t, :half], near_ref[t, half:]) for t in range(2)]
     far = [far_ref.at[0], far_ref.at[1]]
     kv_ref[:, :HD] = turned(both[:, :HD], kg_ref[pl.ds(z, 1), :], near, far, shard).astype(BF16)
@@ -306,7 +311,7 @@
     for upper, o_ref in enumerate((low_ref, high_ref)):
         norm = jnp.where(core == upper, own_ref[...], other_ref[...])
         queries = dot(norm, wq_ref[...])
-        shard = ctx if upper == 0 else far_ref.shape[1] - 1 - ctx
+        shard = ctx if upper == 0 else mirrored(ctx)
         near = [near_ref[t, upper * half : (upper + 1) * half] for t in range(2)]
         for h in range(o_ref.shape[0]):
             part = slice(h * HD, (h + 1) * HD)
@@ -329,7 +334,7 @@
     core = lax.rem(lax.axis_index("head"), 2)
     shards, shard, _ = kv_ref.shape
     heads, half, _ = low_ref.shape
-    group = 4
+    group = GROUP
     subs = 2
     span = group * shard
     rows = heads * half // subs
@@ -337,7 +342,7 @@
     value_s[:, :, HD:] = jnp.ones((shards, shard, HD), BF16)
 
     for upper, q_ref in enumerate((low_ref, high_ref)):
-        own = ctx if upper == 0 else shards - 1 - ctx
+        own = ctx if upper == 0 else mirrored(ctx)
         queries = q_ref[...].reshape(heads * half, HD)
         pieces = [queries[i * rows : (i + 1) * rows] for i in range(subs)]
 
@@ -347,8 +352,7 @@
             values = value_s[pl.ds(first, group)].reshape(span, 2 * HD)
             if masked:
                 t = iota((1, span), 1)
-                place = first + t // shard
-                key_pos = jnp.where(core == 0, place, shards - 1 - place) * (2 * shard) + core * shard + t % shard
+                key_pos = (chunk * group + t // shard) * (2 * shard) + core * shard + t % shard
                 query_pos = own * (2 * half) + upper * half + iota((half, span), 0)
                 bias = jnp.where(query_pos >= key_pos, 0.0, NEG)
             every = [dot_t(piece, keys) for piece in pieces]
@@ -389,7 +393,7 @@
     z = lax.axis_index("head") // 2
     w = o_ref.shape[3]
     for i in range(o_ref.shape[0]):
-        target = lax.rem(jnp.where(core == 0, z + i, z + 4 - i), 4)
+        target = lax.rem(z + i, 4)
         for j in range(2):
             block = 2 * target + (core if j == 0 else 1 - core)
             o_ref[i, j] = dot(attended, w_ref[:, pl.ds(pl.multiple_of(block * w, w), w)]).astype(BF16)
@@ -468,8 +472,8 @@
         pairs = []
         for c in range(16):
             for h in range(8):
-                there = c * 8 + (h + 2 * hops) % 8 if h % 2 == 0 else (15 - c) * 8 + (h - 2 * hops) % 8
-                pairs.append((c * 8 + h, there))
+                there = c if h % 2 == 0 else mirrored(c)
+                pairs.append((c * 8 + h, there * 8 + (h + 2 * hops) % 8))
         return lax.ppermute(shard, ("ctx", "head"), pairs)
 
     def everywhere(blocks):

time: 327 us -> 324 us (level)
    ppermute x8, waiting for transfers between devices: 21.3 us -> 16.3 us  [along(): return lax.ppermute(shard, ('ctx', 'head'), pairs)]
  transfers between devices with their start and end apart: 16 -> 16, of which waited for: 13 -> 14; matrix products, arithmetic and copies ran while one was open for 0% -> 0% of each run, Pallas kernels for 4% -> 4%
where the time goes in v6:
time: 324 us; the launch traced here: 321 us
  blocking collectives  187 us (58%)
  Pallas kernels  51.3 us (16%)
  waiting for transfers between devices  45.1 us (14%)
  starting transfers between devices  29.8 us (9%)
  local copies, waits for them, and re-layouts  5.46 us (2%)
    all_to_all x3, blocking collectives, everywhere(): lax.all_to_all(blocks, ('ctx', 'head'), split_axis=0, concat_axis=0, tile...  187 us
    all_to_all x1, waiting for transfers between devices, body(): lax.all_to_all(jnp.broadcast_to(kv[None], (16, *kv.shape)), 'ctx', split_...  21 us
    ppermute x8, starting transfers between devices, along(): return lax.ppermute(shard, ('ctx', 'head'), pairs)  20 us
    pallas_call x2, Pallas kernels, attend(): pl.pallas_call(attend_kernel, out_shape=jax.ShapeDtypeStruct((heads, 2 *...  18.6 us
    pallas_call x1, Pallas kernels, run_expert(): pl.pallas_call(expert_kernel, out_shape=jax.ShapeDtypeStruct(y.shape, BF1...  16.9 us
    ppermute x8, waiting for transfers between devices, along(): return lax.ppermute(shard, ('ctx', 'head'), pairs)  16.3 us
    ppermute x7, waiting for transfers between devices, to_partner(): return lax.ppermute(shard, 'head', partner)  7.75 us
  transfers between devices with their start and end apart: 16, of which 14 were waited for; matrix products, arithmetic and copies ran while one was open for 0% of the time, Pallas kernels for 4%

profile of v6, /device:TPU:1, one launch (start us, length us, event | category | flops | bytes accessed | tf_op | source)
XLA Modules:
  0.0 320.6 jit_solution(9564552964482433316)
XLA Ops:
  0.0 6.4 %dispatch_rows.1 = (bf16[1024,3072]{1,0:T(8,128)(2,1)}, f32[128,128]{1,0:T(8,128)}, f32[128,128]{1,0:T(8,128)}, f32[128,128]{1,0:T(8,128)}) custom-call(bf16[128,2048]{1,0:T(8,128)(2,1)} %rows_hbm.1, s32[8,128]{1,0:T(8,128)} %bitcast.44, s32[1,128]{1,0:T(1,128)} %bitcast.45, bf16[2048,128]{1,0:T(8,128)(2,1)} %router_hbm.1), custom_call_target="tpu_custom_call" | custom-call | tf_op jit(solution)/shard_map/dispatch_rows/pallas_call | solution.py:101
  6.5 86.7 %all_to_all.20 = bf16[128,8,3072]{2,1,0:T(8,128)(2,1)S(1)} all-to-all(bf16[128,8,3072]{2,1,0:T(8,128)(2,1)} %bitcast.41), channel_id=1, replica_groups=mesh['ctx'=16,'head'=8] {'ctx','head'}, dimensions={0} | all-to-all | bytes 12582912 | tf_op jit(solution)/shard_map/all_to_all | solution.py:480
  93.2 16.9 %expert_ffn.1 = bf16[1024,3072]{1,0:T(8,128)(2,1)S(1)} custom-call(bf16[1024,3072]{1,0:T(8,128)(2,1)S(1)} %bitcast.29, bf16[2048,768]{1,0:T(8,128)(2,1)S(1)} %bitcast.33, bf16[2048,768]{1,0:T(8,128)(2,1)S(1)} %bitcast.34, bf16[768,2048]{1,0:T(8,128)(2,1)S(1)} %bitcast.35), custom_call_target="tpu_custom_call" | custom-call | tf_op jit(solution)/shard_map/expert_ffn/pallas_call | solution.py:153
  110.1 79.7 %all_to_all.21 = bf16[128,8,3072]{2,1,0:T(8,128)(2,1)S(1)} all-to-all(bf16[128,8,3072]{2,1,0:T(8,128)(2,1)S(1)} %bitcast.30), channel_id=1, replica_groups=mesh['ctx'=16,'head'=8] {'ctx','head'}, dimensions={0} | all-to-all | bytes 12582912 | tf_op jit(solution)/shard_map/all_to_all | solution.py:480
  189.8 2.7 combine_rows.1
  192.6 20.8 %all_to_all.22 = bf16[128,8,384]{2,1,0:T(8,128)(2,1)S(1)} all-to-all(bf16[128,8,384]{2,1,0:T(8,128)(2,1)S(1)} %bitcast.31), channel_id=1, replica_groups=mesh['ctx'=16,'head'=8] {'ctx','head'}, dimensions={0} | all-to-all | bytes 1572864 | tf_op jit(solution)/shard_map/all_to_all | solution.py:480
  216.5 2.7 collective-permute-start.1
  222.4 2.5 collective-permute-start.4
  225.1 3.3 %collective-permute-done.2.x1 = bf16[2,256,256]{2,1,0:T(8,128)(2,1)S(1)} collective-permute-done((bf16[2,256,256]{2,1,0:T(8,128)(2,1)S(1)}, bf16[2,256,256]{2,1,0:T(8,128)(2,1)S(1)}, u32[]{:S(2)}, u32[]{:S(2)}) %collective-permute-start.2) | collective-permute-done | bytes 262176 | tf_op jit(solution)/shard_map/ppermute | solution.py:477
  228.4 2.3 collective-permute-done.3.x2
  230.7 2.9 collective-permute-done.4.x3
  237.7 3.8 %all-to-all-start.3 = ((bf16[16,256,256]{2,1,0:T(8,128)(2,1)}), bf16[16,256,256]{2,1,0:T(8,128)(2,1)S(1)}, u32[]{:S(2)}, u32[]{:S(2)}) async-start(bf16[16,256,256]{2,1,0:T(8,128)(2,1)} %broadcast_in_dim.2), calls=%async_computation.3 | async-start | bytes 4194304 | tf_op jit(solution)/shard_map/all_to_all | solution.py:495
  242.6 2.5 collective-permute-done.5.other_ref
  251.4 21.0 %all-to-all-done.3.kv_ref = bf16[16,256,256]{2,1,0:T(8,128)(2,1)S(1)} async-done(((bf16[16,256,256]{2,1,0:T(8,128)(2,1)}), bf16[16,256,256]{2,1,0:T(8,128)(2,1)S(1)}, u32[]{:S(2)}, u32[]{:S(2)}) %all-to-all-start.3) | async-done | bytes 2097184 | tf_op jit(solution)/shard_map/all_to_all | solution.py:495
  272.5 9.4 %attend.3 = f32[4,512,256]{2,1,0:T(8,128)S(1)} custom-call(bf16[4,256,128]{2,1,0:T(8,128)(2,1)S(1)} %collective-permute-done.6.low_ref, bf16[4,256,128]{2,1,0:T(8,128)(2,1)S(1)} %collective-permute-done.7.high_ref, bf16[16,256,256]{2,1,0:T(8,128)(2,1)S(1)} %all-to-all-done.3.kv_ref), custom_call_target="tpu_custom_call" | custom-call | tf_op jit(solution)/shard_map/attend/pallas_call | solution.py:383
  281.9 1.8 collective-permute-start.8
  283.8 9.2 %attend.2.own_ref = f32[4,512,256]{2,1,0:T(8,128)S(1)} custom-call(bf16[4,256,128]{2,1,0:T(8,128)(2,1)S(1)} %get-tuple-element.24.low_ref, bf16[4,256,128]{2,1,0:T(8,128)(2,1)S(1)} %get-tuple-element.25.high_ref, bf16[16,256,256]{2,1,0:T(8,128)(2,1)S(1)} %all-to-all-done.3.kv_ref), custom_call_target="tpu_custom_call" | custom-call | tf_op jit(solution)/shard_map/attend/pallas_call | solution.py:383
  293.0 2.1 merge_and_project.1
  295.9 1.9 collective-permute-done.9
  298.1 3.3 %collective-permute-start.10 = (bf16[2,256,256]{2,1,0:T(8,128)(2,1)S(1)}, bf16[2,256,256]{2,1,0:T(8,128)(2,1)S(1)}, u32[]{:S(2)}, u32[]{:S(2)}) collective-permute-start(bf16[2,256,256]{2,1,0:T(8,128)(2,1)S(1)} %get-tuple-element.29), channel_id=1, source_target_pairs={{0,0},{1,97},{2,2},{3,99},{4,4},{5,101},{6,6},{7,103},{8,8},{9,105... | collective-permute-start | bytes 786440 | tf_op jit(solution)/shard_map/ppermute | solution.py:477
  301.4 3.6 %collective-permute-start.11 = (bf16[2,256,256]{2,1,0:T(8,128)(2,1)S(1)}, bf16[2,256,256]{2,1,0:T(8,128)(2,1)S(1)}, u32[]{:S(2)}, u32[]{:S(2)}) collective-permute-start(bf16[2,256,256]{2,1,0:T(8,128)(2,1)S(1)} %get-tuple-element.32), channel_id=1, source_target_pairs={{0,2},{1,99},{2,4},{3,101},{4,6},{5,103},{6,0},{7,97},{8,10},{9,10... | collective-permute-start | bytes 786440 | tf_op jit(solution)/shard_map/ppermute | solution.py:477
  305.0 4.2 %collective-permute-start.12 = (bf16[2,256,256]{2,1,0:T(8,128)(2,1)S(1)}, bf16[2,256,256]{2,1,0:T(8,128)(2,1)S(1)}, u32[]{:S(2)}, u32[]{:S(2)}) collective-permute-start(bf16[2,256,256]{2,1,0:T(8,128)(2,1)S(1)} %get-tuple-element.31), channel_id=1, source_target_pairs={{0,4},{1,101},{2,6},{3,103},{4,0},{5,97},{6,2},{7,99},{8,12},{9,10... | collective-permute-start | bytes 786440 | tf_op jit(solution)/shard_map/ppermute | solution.py:477
  309.7 4.1 %collective-permute-done.11 = bf16[2,256,256]{2,1,0:T(8,128)(2,1)S(1)} collective-permute-done((bf16[2,256,256]{2,1,0:T(8,128)(2,1)S(1)}, bf16[2,256,256]{2,1,0:T(8,128)(2,1)S(1)}, u32[]{:S(2)}, u32[]{:S(2)}) %collective-permute-start.11) | collective-permute-done | bytes 262176 | tf_op jit(solution)/shard_map/ppermute | solution.py:477
  313.8 2.4 collective-permute-done.12
  (63 shorter events, 23.7 us)
Async XLA Ops:
  6.4 86.7 %copy-start.1 = (bf16[1,2048,768]{2,1,0:T(8,128)(2,1)S(1)}, bf16[1,2048,768]{2,1,0:T(8,128)(2,1)}, u32[]{:S(2)}) copy-start(bf16[1,2048,768]{2,1,0:T(8,128)(2,1)} %param.21) | copy-start | bytes 9437188
  6.4 86.7 %copy-start.2 = (bf16[1,2048,768]{2,1,0:T(8,128)(2,1)S(1)}, bf16[1,2048,768]{2,1,0:T(8,128)(2,1)}, u32[]{:S(2)}) copy-start(bf16[1,2048,768]{2,1,0:T(8,128)(2,1)} %param.22) | copy-start | bytes 9437188
  6.4 86.7 %copy-start.3 = (bf16[1,768,2048]{2,1,0:T(8,128)(2,1)S(1)}, bf16[1,768,2048]{2,1,0:T(8,128)(2,1)}, u32[]{:S(2)}) copy-start(bf16[1,768,2048]{2,1,0:T(8,128)(2,1)} %param.23) | copy-start | bytes 9437188
  110.1 79.7 %copy-start.11 = (f32[128,128]{1,0:T(8,128)S(1)}, f32[128,128]{1,0:T(8,128)}, u32[]{:S(2)}) copy-start(f32[128,128]{1,0:T(8,128)} %get-tuple-element.18.rank_ref) | copy-start | bytes 196612
  110.1 79.7 %copy-start.12 = (f32[128,128]{1,0:T(8,128)S(1)}, f32[128,128]{1,0:T(8,128)}, u32[]{:S(2)}) copy-start(f32[128,128]{1,0:T(8,128)} %get-tuple-element.19.gate_ref) | copy-start | bytes 196612
  110.1 79.7 %copy-start.13 = (f32[128,128]{1,0:T(8,128)S(1)}, f32[128,128]{1,0:T(8,128)}, u32[]{:S(2)}) copy-start(f32[128,128]{1,0:T(8,128)} %get-tuple-element.20.spot_ref) | copy-start | bytes 196612
  189.8 43.8 %copy-start.6 = (bf16[2048,512]{1,0:T(8,128)(2,1)S(1)}, bf16[2048,512]{1,0:T(8,128)(2,1)}, u32[]{:S(2)}) copy-start(bf16[2048,512]{1,0:T(8,128)(2,1)} %wv_hbm.1) | copy-start | bytes 6291460
  192.5 41.1 %copy-start.5 = (bf16[2048,512]{1,0:T(8,128)(2,1)S(1)}, bf16[2048,512]{1,0:T(8,128)(2,1)}, u32[]{:S(2)}) copy-start(bf16[2048,512]{1,0:T(8,128)(2,1)} %wk_hbm.1) | copy-start | bytes 6291460
  214.2 2.3 collective-permute-start
  216.5 8.6 %collective-permute-start.1 = (bf16[2,256,256]{2,1,0:T(8,128)(2,1)S(1)}, bf16[2,256,256]{2,1,0:T(8,128)(2,1)S(1)}, u32[]{:S(2)}, u32[]{:S(2)}) collective-permute-start(bf16[2,256,256]{2,1,0:T(8,128)(2,1)S(1)} %pad_maximum_fusion), channel_id=1, source_target_pairs={{0,0},{1,97},{2,2},{3,99},{4,4},{5,101},{6,6},{7,103},{8,8},{9,105... | collective-permute-start | bytes 786440 | tf_op jit(solution)/shard_map/ppermute | solution.py:477
  219.2 9.2 %collective-permute-start.2 = (bf16[2,256,256]{2,1,0:T(8,128)(2,1)S(1)}, bf16[2,256,256]{2,1,0:T(8,128)(2,1)S(1)}, u32[]{:S(2)}, u32[]{:S(2)}) collective-permute-start(bf16[2,256,256]{2,1,0:T(8,128)(2,1)S(1)} %pad_maximum_fusion), channel_id=1, source_target_pairs={{0,2},{1,99},{2,4},{3,101},{4,6},{5,103},{6,0},{7,97},{8,10},{9,10... | collective-permute-start | bytes 786440 | tf_op jit(solution)/shard_map/ppermute | solution.py:477
  220.8 9.9 %collective-permute-start.3 = (bf16[2,256,256]{2,1,0:T(8,128)(2,1)S(1)}, bf16[2,256,256]{2,1,0:T(8,128)(2,1)S(1)}, u32[]{:S(2)}, u32[]{:S(2)}) collective-permute-start(bf16[2,256,256]{2,1,0:T(8,128)(2,1)S(1)} %pad_maximum_fusion), channel_id=1, source_target_pairs={{0,4},{1,101},{2,6},{3,103},{4,0},{5,97},{6,2},{7,99},{8,12},{9,10... | collective-permute-start | bytes 786440 | tf_op jit(solution)/shard_map/ppermute | solution.py:477
  222.4 11.2 %collective-permute-start.4 = (bf16[2,256,256]{2,1,0:T(8,128)(2,1)S(1)}, bf16[2,256,256]{2,1,0:T(8,128)(2,1)S(1)}, u32[]{:S(2)}, u32[]{:S(2)}) collective-permute-start(bf16[2,256,256]{2,1,0:T(8,128)(2,1)S(1)} %pad_maximum_fusion), channel_id=1, source_target_pairs={{0,6},{1,103},{2,0},{3,97},{4,2},{5,99},{6,4},{7,101},{8,14},{9,11... | collective-permute-start | bytes 786440 | tf_op jit(solution)/shard_map/ppermute | solution.py:477
  237.7 34.7 %all-to-all-start.3 = ((bf16[16,256,256]{2,1,0:T(8,128)(2,1)}), bf16[16,256,256]{2,1,0:T(8,128)(2,1)S(1)}, u32[]{:S(2)}, u32[]{:S(2)}) async-start(bf16[16,256,256]{2,1,0:T(8,128)(2,1)} %broadcast_in_dim.2), calls=%async_computation.3 | async-start | bytes 4194304 | tf_op jit(solution)/shard_map/all_to_all | solution.py:495
  241.6 3.5 %collective-permute-start.5 = (bf16[256,2048]{1,0:T(8,128)(2,1)}, bf16[256,2048]{1,0:T(8,128)(2,1)S(1)}, u32[]{:S(2)}, u32[]{:S(2)}) collective-permute-start(bf16[256,2048]{1,0:T(8,128)(2,1)} %copy-done.8), channel_id=1, source_target_pairs={{0,1},{1,0},{2,3},{3,2},{4,5},{5,4},{6,7},{7,6},{8,9},{9,8},{10,11... | collective-permute-start | bytes 3145736 | tf_op jit(solution)/shard_map/ppermute | solution.py:469
  249.4 1.6 collective-permute-start.6
  249.9 1.5 collective-permute-start.7
  281.9 11.0 %collective-permute-start.8 = (f32[4,512,256]{2,1,0:T(8,128)S(1)}, f32[4,512,256]{2,1,0:T(8,128)S(1)}, u32[]{:S(2)}, u32[]{:S(2)}) collective-permute-start(f32[4,512,256]{2,1,0:T(8,128)S(1)} %attend.3), channel_id=1, source_target_pairs={{0,1},{1,0},{2,3},{3,2},{4,5},{5,4},{6,7},{7,6},{8,9},{9,8},{10,11... | collective-permute-start | bytes 6291464 | tf_op jit(solution)/shard_map/ppermute | solution.py:469
  295.1 2.7 collective-permute-start.9
  298.1 11.6 %collective-permute-start.10 = (bf16[2,256,256]{2,1,0:T(8,128)(2,1)S(1)}, bf16[2,256,256]{2,1,0:T(8,128)(2,1)S(1)}, u32[]{:S(2)}, u32[]{:S(2)}) collective-permute-start(bf16[2,256,256]{2,1,0:T(8,128)(2,1)S(1)} %get-tuple-element.29), channel_id=1, source_target_pairs={{0,0},{1,97},{2,2},{3,99},{4,4},{5,101},{6,6},{7,103},{8,8},{9,105... | collective-permute-start | bytes 786440 | tf_op jit(solution)/shard_map/ppermute | solution.py:477
  301.4 12.5 %collective-permute-start.11 = (bf16[2,256,256]{2,1,0:T(8,128)(2,1)S(1)}, bf16[2,256,256]{2,1,0:T(8,128)(2,1)S(1)}, u32[]{:S(2)}, u32[]{:S(2)}) collective-permute-start(bf16[2,256,256]{2,1,0:T(8,128)(2,1)S(1)} %get-tuple-element.32), channel_id=1, source_target_pairs={{0,2},{1,99},{2,4},{3,101},{4,6},{5,103},{6,0},{7,97},{8,10},{9,10... | collective-permute-start | bytes 786440 | tf_op jit(solution)/shard_map/ppermute | solution.py:477
  305.0 11.3 %collective-permute-start.12 = (bf16[2,256,256]{2,1,0:T(8,128)(2,1)S(1)}, bf16[2,256,256]{2,1,0:T(8,128)(2,1)S(1)}, u32[]{:S(2)}, u32[]{:S(2)}) collective-permute-start(bf16[2,256,256]{2,1,0:T(8,128)(2,1)S(1)} %get-tuple-element.31), channel_id=1, source_target_pairs={{0,4},{1,101},{2,6},{3,103},{4,0},{5,97},{6,2},{7,99},{8,12},{9,10... | collective-permute-start | bytes 786440 | tf_op jit(solution)/shard_map/ppermute | solution.py:477
  309.2 8.2 %collective-permute-start.13 = (bf16[2,256,256]{2,1,0:T(8,128)(2,1)S(1)}, bf16[2,256,256]{2,1,0:T(8,128)(2,1)S(1)}, u32[]{:S(2)}, u32[]{:S(2)}) collective-permute-start(bf16[2,256,256]{2,1,0:T(8,128)(2,1)S(1)} %get-tuple-element.30), channel_id=1, source_target_pairs={{0,6},{1,103},{2,0},{3,97},{4,2},{5,99},{6,4},{7,101},{8,14},{9,11... | collective-permute-start | bytes 786440 | tf_op jit(solution)/shard_map/ppermute | solution.py:477
  317.6 2.1 collective-permute-start.14
  (10 other events, 210.2 us)

commit v7 on v3

--- a/solution.py
+++ b/solution.py
@@ -40,8 +40,8 @@
 
 
 def dispatch_kernel(
-    rows_hbm, ids_hbm, targets_hbm, router_hbm, y_ref, rank_ref, gate_ref, spot_ref,
-    rows_ref, ids_ref, targets_ref, router_ref, sems,
+    rows_hbm, ids_hbm, targets_hbm, router_hbm, y_hbm, rank_ref, gate_ref, spot_ref,
+    y_ref, rows_ref, ids_ref, targets_ref, router_ref, sems,
 ):
     loads = start_loads(
         [(targets_hbm, targets_ref), (ids_hbm, ids_ref), (rows_hbm, rows_ref), (router_hbm, router_ref)], sems
@@ -70,6 +70,7 @@
     half = width // 2
     blk = 32
     packed = rank.astype(BF16)
+    stores = []
     for i in range(experts // blk):
         spread = jnp.where(iota((blk * 8, experts), 0) // 8 + i * blk == iota((blk * 8, experts), 1), 1.0, 0.0)
         rank_e = dot(spread.astype(BF16), packed)
@@ -80,6 +81,8 @@
         lines = slice(i * blk * 8, (i + 1) * blk * 8)
         y_ref[lines, :width] = dot(main, rows).astype(BF16)
         y_ref[lines, width:] = (dot(low, rows[:, :half]) + dot(high, rows[:, half:])).astype(BF16)
+        stores.append(pltpu.make_async_copy(y_ref.at[lines], y_hbm.at[lines], sems.at[4 + i]))
+        stores[-1].start()
     rank_ref[...] = rank.T
     member_q = member.T > 0.5
     loads[3].wait()
@@ -87,6 +90,8 @@
     highest = jnp.max(jnp.where(member_q, logits, NEG), 1, keepdims=True)
     raised = jnp.where(member_q, jnp.exp(jnp.minimum(logits - highest, 0.0)), 0.0)
     gate_ref[...] = raised / jnp.sum(raised, 1, keepdims=True)
+    for store in stores:
+        store.wait()
 
 
 def dispatch(rows, ids, targets, router):
@@ -95,15 +100,17 @@
     return pl.pallas_call(
         dispatch_kernel,
         in_specs=[pl.BlockSpec(memory_space=pltpu.HBM)] * 4,
+        out_specs=[pl.BlockSpec(memory_space=pltpu.HBM)] + [pl.BlockSpec(memory_space=VMEM)] * 3,
         out_shape=[jax.ShapeDtypeStruct((1024, width * 3 // 2), BF16), table, table, table],
         scratch_shapes=[
+            VMEM((1024, width * 3 // 2), BF16),
             VMEM((n, width), BF16),
             VMEM((8, n), jnp.int32),
             VMEM((1, n), jnp.int32),
             VMEM(router.shape, BF16),
-            pltpu.SemaphoreType.DMA((4,)),
+            pltpu.SemaphoreType.DMA((8,)),
         ],
-        compiler_params=pltpu.CompilerParams(vmem_limit_bytes=16 * MIB),
+        compiler_params=pltpu.CompilerParams(vmem_limit_bytes=57 * MIB),
         name="dispatch_rows",
     )(rows, ids.T, targets.reshape(1, n), router)
 

time: 323 us -> 322 us (level)
  local copies, waits for them, and re-layouts: 8.89 us -> 5.46 us
    unnamed x38 -> x36, local copies, waits for them, and re-layouts: 7.3 us -> 3.89 us
where the time goes in v7:
time: 322 us; the launch traced here: 319 us
  blocking collectives  187 us (58%)
  Pallas kernels  51.2 us (16%)
  waiting for transfers between devices  40.2 us (12%)
  starting transfers between devices  33 us (10%)
  local copies, waits for them, and re-layouts  5.46 us (2%)
    all_to_all x3, blocking collectives, everywhere(): lax.all_to_all(blocks, ('ctx', 'head'), split_axis=0, concat_axis=0, tile...  187 us
    ppermute x8, starting transfers between devices, along(): return lax.ppermute(shard, ('ctx', 'head'), pairs)  26.4 us
    pallas_call x2, Pallas kernels, attend(): pl.pallas_call(attend_kernel, out_shape=jax.ShapeDtypeStruct((heads, 2 *...  18.6 us
    pallas_call x1, Pallas kernels, run_expert(): pl.pallas_call(expert_kernel, out_shape=jax.ShapeDtypeStruct(y.shape, BF1...  16.9 us
    all_to_all x1, waiting for transfers between devices, body(): lax.all_to_all(jnp.broadcast_to(kv[None], (16, *kv.shape)), 'ctx', split_...  16.8 us
    ppermute x8, waiting for transfers between devices, along(): return lax.ppermute(shard, ('ctx', 'head'), pairs)  15.3 us
    ppermute x7, waiting for transfers between devices, to_partner(): return lax.ppermute(shard, 'head', partner)  8.1 us
  transfers between devices with their start and end apart: 16, of which 13 were waited for; matrix products, arithmetic and copies ran while one was open for 0% of the time, Pallas kernels for 4%

profile of v7, /device:TPU:1, one launch (start us, length us, event | category | flops | bytes accessed | tf_op | source)
XLA Modules:
  0.0 318.8 jit_solution(6734646502408459079)
XLA Ops:
  0.0 6.4 %dispatch_rows.1 = (bf16[1024,3072]{1,0:T(8,128)(2,1)}, f32[128,128]{1,0:T(8,128)}, f32[128,128]{1,0:T(8,128)}, f32[128,128]{1,0:T(8,128)}) custom-call(bf16[128,2048]{1,0:T(8,128)(2,1)} %rows_hbm.1, s32[8,128]{1,0:T(8,128)} %bitcast.44, s32[1,128]{1,0:T(1,128)} %bitcast.45, bf16[2048,128]{1,0:T(8,128)(2,1)} %router_hbm.1), custom_call_target="tpu_custom_call" | custom-call | tf_op jit(solution)/shard_map/dispatch_rows/pallas_call | solution.py:100
  6.5 86.7 %all_to_all.20 = bf16[128,8,3072]{2,1,0:T(8,128)(2,1)S(1)} all-to-all(bf16[128,8,3072]{2,1,0:T(8,128)(2,1)} %bitcast.41), channel_id=1, replica_groups=mesh['ctx'=16,'head'=8] {'ctx','head'}, dimensions={0} | all-to-all | bytes 12582912 | tf_op jit(solution)/shard_map/all_to_all | solution.py:475
  93.2 16.9 %expert_ffn.1 = bf16[1024,3072]{1,0:T(8,128)(2,1)S(1)} custom-call(bf16[1024,3072]{1,0:T(8,128)(2,1)S(1)} %bitcast.29, bf16[2048,768]{1,0:T(8,128)(2,1)S(1)} %bitcast.33, bf16[2048,768]{1,0:T(8,128)(2,1)S(1)} %bitcast.34, bf16[768,2048]{1,0:T(8,128)(2,1)S(1)} %bitcast.35), custom_call_target="tpu_custom_call" | custom-call | tf_op jit(solution)/shard_map/expert_ffn/pallas_call | solution.py:152
  110.1 79.7 %all_to_all.21 = bf16[128,8,3072]{2,1,0:T(8,128)(2,1)S(1)} all-to-all(bf16[128,8,3072]{2,1,0:T(8,128)(2,1)S(1)} %bitcast.30), channel_id=1, replica_groups=mesh['ctx'=16,'head'=8] {'ctx','head'}, dimensions={0} | all-to-all | bytes 12582912 | tf_op jit(solution)/shard_map/all_to_all | solution.py:475
  189.8 2.7 combine_rows.1
  192.6 20.8 %all_to_all.22 = bf16[128,8,384]{2,1,0:T(8,128)(2,1)S(1)} all-to-all(bf16[128,8,384]{2,1,0:T(8,128)(2,1)S(1)} %bitcast.31), channel_id=1, replica_groups=mesh['ctx'=16,'head'=8] {'ctx','head'}, dimensions={0} | all-to-all | bytes 1572864 | tf_op jit(solution)/shard_map/all_to_all | solution.py:475
  216.5 2.8 collective-permute-start.1
  219.3 3.6 %collective-permute-start.2 = (bf16[2,256,256]{2,1,0:T(8,128)(2,1)S(1)}, bf16[2,256,256]{2,1,0:T(8,128)(2,1)S(1)}, u32[]{:S(2)}, u32[]{:S(2)}) collective-permute-start(bf16[2,256,256]{2,1,0:T(8,128)(2,1)S(1)} %pad_maximum_fusion), channel_id=1, source_target_pairs={{0,2},{1,123},{2,4},{3,125},{4,6},{5,127},{6,0},{7,121},{8,10},{9,... | collective-permute-start | bytes 786440 | tf_op jit(solution)/shard_map/ppermute | solution.py:472
  222.9 2.6 collective-permute-start.3
  225.6 3.6 %collective-permute-start.4 = (bf16[2,256,256]{2,1,0:T(8,128)(2,1)S(1)}, bf16[2,256,256]{2,1,0:T(8,128)(2,1)S(1)}, u32[]{:S(2)}, u32[]{:S(2)}) collective-permute-start(bf16[2,256,256]{2,1,0:T(8,128)(2,1)S(1)} %pad_maximum_fusion), channel_id=1, source_target_pairs={{0,6},{1,127},{2,0},{3,121},{4,2},{5,123},{6,4},{7,125},{8,14},{9,... | collective-permute-start | bytes 786440 | tf_op jit(solution)/shard_map/ppermute | solution.py:472
  230.1 3.8 %collective-permute-done.3.x2 = bf16[2,256,256]{2,1,0:T(8,128)(2,1)S(1)} collective-permute-done((bf16[2,256,256]{2,1,0:T(8,128)(2,1)S(1)}, bf16[2,256,256]{2,1,0:T(8,128)(2,1)S(1)}, u32[]{:S(2)}, u32[]{:S(2)}) %collective-permute-start.3) | collective-permute-done | bytes 262176 | tf_op jit(solution)/shard_map/ppermute | solution.py:472
  233.9 3.8 %collective-permute-done.4.x3 = bf16[2,256,256]{2,1,0:T(8,128)(2,1)S(1)} collective-permute-done((bf16[2,256,256]{2,1,0:T(8,128)(2,1)S(1)}, bf16[2,256,256]{2,1,0:T(8,128)(2,1)S(1)}, u32[]{:S(2)}, u32[]{:S(2)}) %collective-permute-start.4) | collective-permute-done | bytes 262176 | tf_op jit(solution)/shard_map/ppermute | solution.py:472
  241.8 3.8 %all-to-all-start.3 = ((bf16[16,256,256]{2,1,0:T(8,128)(2,1)}), bf16[16,256,256]{2,1,0:T(8,128)(2,1)S(1)}, u32[]{:S(2)}, u32[]{:S(2)}) async-start(bf16[16,256,256]{2,1,0:T(8,128)(2,1)} %broadcast_in_dim.2), calls=%async_computation.3 | async-start | bytes 4194304 | tf_op jit(solution)/shard_map/all_to_all | solution.py:490
  245.7 2.9 collective-permute-done.5.other_ref
  255.0 16.8 %all-to-all-done.3.kv_ref = bf16[16,256,256]{2,1,0:T(8,128)(2,1)S(1)} async-done(((bf16[16,256,256]{2,1,0:T(8,128)(2,1)}), bf16[16,256,256]{2,1,0:T(8,128)(2,1)S(1)}, u32[]{:S(2)}, u32[]{:S(2)}) %all-to-all-start.3) | async-done | bytes 2097184 | tf_op jit(solution)/shard_map/all_to_all | solution.py:490
  271.7 9.4 %attend.3 = f32[4,512,256]{2,1,0:T(8,128)S(1)} custom-call(bf16[4,256,128]{2,1,0:T(8,128)(2,1)S(1)} %collective-permute-done.6.low_ref, bf16[4,256,128]{2,1,0:T(8,128)(2,1)S(1)} %collective-permute-done.7.high_ref, bf16[16,256,256]{2,1,0:T(8,128)(2,1)S(1)} %all-to-all-done.3.kv_ref), custom_call_target="tpu_custom_call" | custom-call | tf_op jit(solution)/shard_map/attend/pallas_call | solution.py:379
  281.3 9.2 %attend.2.own_ref = f32[4,512,256]{2,1,0:T(8,128)S(1)} custom-call(bf16[4,256,128]{2,1,0:T(8,128)(2,1)S(1)} %get-tuple-element.24.low_ref, bf16[4,256,128]{2,1,0:T(8,128)(2,1)S(1)} %get-tuple-element.25.high_ref, bf16[16,256,256]{2,1,0:T(8,128)(2,1)S(1)} %all-to-all-done.3.kv_ref), custom_call_target="tpu_custom_call" | custom-call | tf_op jit(solution)/shard_map/attend/pallas_call | solution.py:379
  290.5 2.1 merge_and_project.1
  295.7 2.4 collective-permute-start.10
  298.1 4.4 %collective-permute-start.11 = (bf16[2,256,256]{2,1,0:T(8,128)(2,1)S(1)}, bf16[2,256,256]{2,1,0:T(8,128)(2,1)S(1)}, u32[]{:S(2)}, u32[]{:S(2)}) collective-permute-start(bf16[2,256,256]{2,1,0:T(8,128)(2,1)S(1)} %get-tuple-element.32), channel_id=1, source_target_pairs={{0,2},{1,123},{2,4},{3,125},{4,6},{5,127},{6,0},{7,121},{8,10},{9,... | collective-permute-start | bytes 786440 | tf_op jit(solution)/shard_map/ppermute | solution.py:472
  302.5 2.7 collective-permute-start.12
  305.2 4.2 %collective-permute-start.13 = (bf16[2,256,256]{2,1,0:T(8,128)(2,1)S(1)}, bf16[2,256,256]{2,1,0:T(8,128)(2,1)S(1)}, u32[]{:S(2)}, u32[]{:S(2)}) collective-permute-start(bf16[2,256,256]{2,1,0:T(8,128)(2,1)S(1)} %get-tuple-element.30), channel_id=1, source_target_pairs={{0,6},{1,127},{2,0},{3,121},{4,2},{5,123},{6,4},{7,125},{8,14},{9,... | collective-permute-start | bytes 786440 | tf_op jit(solution)/shard_map/ppermute | solution.py:472
  310.5 2.9 collective-permute-done.12
  313.4 2.8 collective-permute-done.13
  (63 shorter events, 21.3 us)
Async XLA Ops:
  6.4 86.7 %copy-start.1 = (bf16[1,2048,768]{2,1,0:T(8,128)(2,1)S(1)}, bf16[1,2048,768]{2,1,0:T(8,128)(2,1)}, u32[]{:S(2)}) copy-start(bf16[1,2048,768]{2,1,0:T(8,128)(2,1)} %param.21) | copy-start | bytes 9437188
  6.4 86.7 %copy-start.2 = (bf16[1,2048,768]{2,1,0:T(8,128)(2,1)S(1)}, bf16[1,2048,768]{2,1,0:T(8,128)(2,1)}, u32[]{:S(2)}) copy-start(bf16[1,2048,768]{2,1,0:T(8,128)(2,1)} %param.22) | copy-start | bytes 9437188
  6.4 86.7 %copy-start.3 = (bf16[1,768,2048]{2,1,0:T(8,128)(2,1)S(1)}, bf16[1,768,2048]{2,1,0:T(8,128)(2,1)}, u32[]{:S(2)}) copy-start(bf16[1,768,2048]{2,1,0:T(8,128)(2,1)} %param.23) | copy-start | bytes 9437188
  110.1 79.7 %copy-start.11 = (f32[128,128]{1,0:T(8,128)S(1)}, f32[128,128]{1,0:T(8,128)}, u32[]{:S(2)}) copy-start(f32[128,128]{1,0:T(8,128)} %get-tuple-element.18.rank_ref) | copy-start | bytes 196612
  110.1 79.7 %copy-start.12 = (f32[128,128]{1,0:T(8,128)S(1)}, f32[128,128]{1,0:T(8,128)}, u32[]{:S(2)}) copy-start(f32[128,128]{1,0:T(8,128)} %get-tuple-element.19.gate_ref) | copy-start | bytes 196612
  110.1 79.7 %copy-start.13 = (f32[128,128]{1,0:T(8,128)S(1)}, f32[128,128]{1,0:T(8,128)}, u32[]{:S(2)}) copy-start(f32[128,128]{1,0:T(8,128)} %get-tuple-element.20.spot_ref) | copy-start | bytes 196612
  189.8 47.9 %copy-start.6 = (bf16[2048,512]{1,0:T(8,128)(2,1)S(1)}, bf16[2048,512]{1,0:T(8,128)(2,1)}, u32[]{:S(2)}) copy-start(bf16[2048,512]{1,0:T(8,128)(2,1)} %wv_hbm.1) | copy-start | bytes 6291460
  192.5 45.2 %copy-start.5 = (bf16[2048,512]{1,0:T(8,128)(2,1)S(1)}, bf16[2048,512]{1,0:T(8,128)(2,1)}, u32[]{:S(2)}) copy-start(bf16[2048,512]{1,0:T(8,128)(2,1)} %wk_hbm.1) | copy-start | bytes 6291460
  214.2 2.3 collective-permute-start
  216.5 12.7 %collective-permute-start.1 = (bf16[2,256,256]{2,1,0:T(8,128)(2,1)S(1)}, bf16[2,256,256]{2,1,0:T(8,128)(2,1)S(1)}, u32[]{:S(2)}, u32[]{:S(2)}) collective-permute-start(bf16[2,256,256]{2,1,0:T(8,128)(2,1)S(1)} %pad_maximum_fusion), channel_id=1, source_target_pairs={{0,0},{1,121},{2,2},{3,123},{4,4},{5,125},{6,6},{7,127},{8,8},{9,1... | collective-permute-start | bytes 786440 | tf_op jit(solution)/shard_map/ppermute | solution.py:472
  219.3 10.8 %collective-permute-start.2 = (bf16[2,256,256]{2,1,0:T(8,128)(2,1)S(1)}, bf16[2,256,256]{2,1,0:T(8,128)(2,1)S(1)}, u32[]{:S(2)}, u32[]{:S(2)}) collective-permute-start(bf16[2,256,256]{2,1,0:T(8,128)(2,1)S(1)} %pad_maximum_fusion), channel_id=1, source_target_pairs={{0,2},{1,123},{2,4},{3,125},{4,6},{5,127},{6,0},{7,121},{8,10},{9,... | collective-permute-start | bytes 786440 | tf_op jit(solution)/shard_map/ppermute | solution.py:472
  222.9 10.9 %collective-permute-start.3 = (bf16[2,256,256]{2,1,0:T(8,128)(2,1)S(1)}, bf16[2,256,256]{2,1,0:T(8,128)(2,1)S(1)}, u32[]{:S(2)}, u32[]{:S(2)}) collective-permute-start(bf16[2,256,256]{2,1,0:T(8,128)(2,1)S(1)} %pad_maximum_fusion), channel_id=1, source_target_pairs={{0,4},{1,125},{2,6},{3,127},{4,0},{5,121},{6,2},{7,123},{8,12},{9,... | collective-permute-start | bytes 786440 | tf_op jit(solution)/shard_map/ppermute | solution.py:472
  225.6 12.1 %collective-permute-start.4 = (bf16[2,256,256]{2,1,0:T(8,128)(2,1)S(1)}, bf16[2,256,256]{2,1,0:T(8,128)(2,1)S(1)}, u32[]{:S(2)}, u32[]{:S(2)}) collective-permute-start(bf16[2,256,256]{2,1,0:T(8,128)(2,1)S(1)} %pad_maximum_fusion), channel_id=1, source_target_pairs={{0,6},{1,127},{2,0},{3,121},{4,2},{5,123},{6,4},{7,125},{8,14},{9,... | collective-permute-start | bytes 786440 | tf_op jit(solution)/shard_map/ppermute | solution.py:472
  241.8 30.0 %all-to-all-start.3 = ((bf16[16,256,256]{2,1,0:T(8,128)(2,1)}), bf16[16,256,256]{2,1,0:T(8,128)(2,1)S(1)}, u32[]{:S(2)}, u32[]{:S(2)}) async-start(bf16[16,256,256]{2,1,0:T(8,128)(2,1)} %broadcast_in_dim.2), calls=%async_computation.3 | async-start | bytes 4194304 | tf_op jit(solution)/shard_map/all_to_all | solution.py:490
  245.6 3.0 collective-permute-start.5
  253.0 1.6 collective-permute-start.6
  253.2 1.8 collective-permute-start.7
  281.2 9.3 %collective-permute-start.8 = (f32[4,512,256]{2,1,0:T(8,128)S(1)}, f32[4,512,256]{2,1,0:T(8,128)S(1)}, u32[]{:S(2)}, u32[]{:S(2)}) collective-permute-start(f32[4,512,256]{2,1,0:T(8,128)S(1)} %attend.3), channel_id=1, source_target_pairs={{0,1},{1,0},{2,3},{3,2},{4,5},{5,4},{6,7},{7,6},{8,9},{9,8},{10,11... | collective-permute-start | bytes 6291464 | tf_op jit(solution)/shard_map/ppermute | solution.py:464
  292.6 2.8 collective-permute-start.9
  295.7 13.7 %collective-permute-start.10 = (bf16[2,256,256]{2,1,0:T(8,128)(2,1)S(1)}, bf16[2,256,256]{2,1,0:T(8,128)(2,1)S(1)}, u32[]{:S(2)}, u32[]{:S(2)}) collective-permute-start(bf16[2,256,256]{2,1,0:T(8,128)(2,1)S(1)} %get-tuple-element.29), channel_id=1, source_target_pairs={{0,0},{1,121},{2,2},{3,123},{4,4},{5,125},{6,6},{7,127},{8,8},{9,1... | collective-permute-start | bytes 786440 | tf_op jit(solution)/shard_map/ppermute | solution.py:472
  298.1 12.4 %collective-permute-start.11 = (bf16[2,256,256]{2,1,0:T(8,128)(2,1)S(1)}, bf16[2,256,256]{2,1,0:T(8,128)(2,1)S(1)}, u32[]{:S(2)}, u32[]{:S(2)}) collective-permute-start(bf16[2,256,256]{2,1,0:T(8,128)(2,1)S(1)} %get-tuple-element.32), channel_id=1, source_target_pairs={{0,2},{1,123},{2,4},{3,125},{4,6},{5,127},{6,0},{7,121},{8,10},{9,... | collective-permute-start | bytes 786440 | tf_op jit(solution)/shard_map/ppermute | solution.py:472
  302.5 10.9 %collective-permute-start.12 = (bf16[2,256,256]{2,1,0:T(8,128)(2,1)S(1)}, bf16[2,256,256]{2,1,0:T(8,128)(2,1)S(1)}, u32[]{:S(2)}, u32[]{:S(2)}) collective-permute-start(bf16[2,256,256]{2,1,0:T(8,128)(2,1)S(1)} %get-tuple-element.31), channel_id=1, source_target_pairs={{0,4},{1,125},{2,6},{3,127},{4,0},{5,121},{6,2},{7,123},{8,12},{9,... | collective-permute-start | bytes 786440 | tf_op jit(solution)/shard_map/ppermute | solution.py:472
  305.2 11.0 %collective-permute-start.13 = (bf16[2,256,256]{2,1,0:T(8,128)(2,1)S(1)}, bf16[2,256,256]{2,1,0:T(8,128)(2,1)S(1)}, u32[]{:S(2)}, u32[]{:S(2)}) collective-permute-start(bf16[2,256,256]{2,1,0:T(8,128)(2,1)S(1)} %get-tuple-element.30), channel_id=1, source_target_pairs={{0,6},{1,127},{2,0},{3,121},{4,2},{5,123},{6,4},{7,125},{8,14},{9,... | collective-permute-start | bytes 786440 | tf_op jit(solution)/shard_map/ppermute | solution.py:472
  316.4 1.4 collective-permute-start.14
  (10 other events, 224.1 us)
